TPU v7x, 256 devices: a whole 4x4x8 slice. The times are simulated.
256 devices in a mesh: row: 16 (over z, y_hi), col: 16 (over x, y_lo, core).
Axes of the slice: x: 4, y: 4 (y_hi: 2, y_lo: 2; y = y_hi * 2 + y_lo), z: 8, core: 2. Of those that a mesh axis runs over, the one named last changes fastest.
Arguments:
- amplitudes: float32 [16, 16, 400, 400], P('row', None, 'col'), may hold values from -6 to 6
- integrals: float32 [64, 64, 400, 400], P('row', None, 'col'), may hold values from -0.015625 to 0.015625
- rest: float32 [16, 16, 64, 64], P('col', None, 'row'), may hold values from -6 to 6
- occ_energy: float32 [16], replicated, may hold values from -2 to -0.5
- vir_energy: float32 [64], replicated, may hold values from 0.5 to 3
Outputs:
- new_amps: float32 [16, 16, 64, 64], P('col', None, 'row')
All inputs are finite; a program needn't handle non-finite values.
Results may differ from a plain program's by a relative error of at most 0.000057.
Values sent between devices are 32-bit elements; how exact they have to be, the bound alone decides.
No kernel may reach another device: no remote copies, remote signals or barrier semaphores. Data moves between devices by JAX's collectives and lax.ppermute only.
A program may use at most 128 MiB of HBM per device.

v0:
```python
import jax
import jax.numpy as jnp
from jax import lax
from jax.sharding import PartitionSpec as P


def on_device(amplitudes, integrals, rest, occ_energy, vir_energy):
    row_index = lax.axis_index("row")
    col_index = lax.axis_index("col")
    a_count = integrals.shape[0]
    b_count = integrals.shape[1]
    integral_slab = integrals.reshape(a_count * b_count, -1)
    occupied = amplitudes.shape[1]
    shard_piece = lax.all_gather(amplitudes, "row", axis=0, tiled=True)
    piece_rows = shard_piece.shape[0]
    flattened = shard_piece.reshape(piece_rows * occupied, -1)
    product = lax.dot_general(
        flattened,
        integral_slab,
        (((1,), (1,)), ((), ())),
        precision=lax.Precision.HIGHEST,
        preferred_element_type=jnp.float32,
    )
    partial_value = product.reshape(piece_rows, occupied, a_count, b_count)
    summed = lax.psum_scatter(partial_value, "col", scatter_dimension=0, tiled=True)
    moved = lax.all_to_all(
        lax.all_to_all(summed, "row", split_axis=3, concat_axis=2, tiled=True),
        "col",
        split_axis=1,
        concat_axis=0,
        tiled=True,
    )
    combined = summed + jnp.transpose(moved, (1, 0, 3, 2))
    i_count = combined.shape[0]
    occ_local = lax.dynamic_slice_in_dim(occ_energy, col_index * i_count, i_count, 0)
    vir_local = lax.dynamic_slice_in_dim(vir_energy, row_index * a_count, a_count, 0)
    denominator = (
        vir_local[None, None, :, None]
        + vir_energy[None, None, None, :]
        - occ_local[:, None, None, None]
        - occ_energy[None, :, None, None]
    )
    return (combined + rest) / denominator


def solution(mesh):
    in_specs = (
        P("row", None, "col", None),
        P("row", None, "col", None),
        P("col", None, "row", None),
        P(),
        P(),
    )
    out_specs = P("col", None, "row", None)
    return jax.shard_map(
        on_device, mesh=mesh, in_specs=in_specs, out_specs=out_specs, check_vma=False
    )
```

profile of v0, /device:TPU:1, one launch (start us, length us, event | category | flops | bytes accessed | tf_op | source)
XLA Modules:
  0.0 327.3 jit_solution(11584524614010061250)
XLA Ops:
  6.5 0.0 all-gather.2.cloned.1.call-start
  6.5 0.7 all-gather.2.cloned.1.call-update
  7.3 0.0 copy-start.1
  7.3 0.0 copy-start.2
  7.3 0.0 copy-start
  7.3 0.0 reduce-scatter.2.cloned.1.call-start
  7.3 189.7 %all-gather.2.cloned.1.call-done = f32[16,16,25,400]{3,1,2,0:T(8,128)} async-done(((f32[1,16,25,400]{3,1,2,0:T(8,128)}), f32[16,16,25,400]{3,1,2,0:T(8,128)}) %all-gather.2.cloned.1.call-update) | async-done | bytes 10240016 | tf_op jit(solution)/shard_map/all_gather | solution.py:14
  197.0 26.4 %fusion.3 = f32[16,16,4,64]{3,1,2,0:T(8,128)} fusion(f32[4,64,25,400]{3,1,2,0:T(8,128)} %param.6, f32[16,16,25,400]{3,1,2,0:T(8,128)} %all-gather.2.cloned.1.call-done), kind=kOutput, calls=%fused_computation.3 | convolution fusion | flops 7864320000 | bytes 20742144 | tf_op jit(solution)/shard_map/dot_general | solution.py:17
  223.4 0.0 reduce-scatter.2.cloned.1.call-update
  223.4 58.5 %reduce-scatter.2.cloned.1.call-done = f32[1,16,4,64]{3,1,2,0:T(8,128)} async-done(((f32[16,16,4,64]{3,1,2,0:T(8,128)}), f32[1,16,4,64]{3,1,2,0:T(8,128)}) %reduce-scatter.2.cloned.1.call-update) | async-done | bytes 16400 | tf_op jit(solution)/shard_map/reduce_scatter | solution.py:25
  281.9 0.9 copy.14
  282.8 0.7 reshape.59
  283.5 9.0 %all-to-all-start = ((f32[16,1,256]{2,1,0:T(1,128)}), f32[16,1,256]{2,1,0:T(1,128)S(1)}, u32[]{:S(2)}, u32[]{:S(2)}) async-start(f32[16,1,256]{2,1,0:T(1,128)} %reshape.59), calls=%async_computation.1 | async-start | bytes 32768 | tf_op jit(solution)/shard_map/all_to_all | solution.py:27
  292.6 0.0 copy-done.1
  292.6 0.6 dynamic_slice.7
  293.2 0.0 copy-done.2
  293.2 0.1 dynamic_slice.6
  293.2 8.2 %all-to-all-done = f32[16,1,256]{2,1,0:T(1,128)S(1)} async-done(((f32[16,1,256]{2,1,0:T(1,128)}), f32[16,1,256]{2,1,0:T(1,128)S(1)}, u32[]{:S(2)}, u32[]{:S(2)}) %all-to-all-start) | async-done | bytes 16416 | tf_op jit(solution)/shard_map/all_to_all | solution.py:27
  301.5 0.6 broadcast.48
  302.1 0.7 reduce
  302.8 0.1 reshape.60
  303.0 0.1 copy.16
  303.1 0.1 copy.17
  303.2 0.7 reshape.61
  303.9 8.4 %all-to-all-start.1 = ((f32[16,1,256]{2,1,0:T(1,128)}), f32[16,1,256]{2,1,0:T(1,128)S(1)}, u32[]{:S(2)}, u32[]{:S(2)}) async-start(f32[16,1,256]{2,1,0:T(1,128)} %reshape.61), calls=%async_computation.2 | async-start | bytes 32768 | tf_op jit(solution)/shard_map/all_to_all | solution.py:26
  312.3 0.6 add_subtract_fusion
  312.9 5.2 %all-to-all-done.1 = f32[16,1,256]{2,1,0:T(1,128)S(1)} async-done(((f32[16,1,256]{2,1,0:T(1,128)}), f32[16,1,256]{2,1,0:T(1,128)S(1)}, u32[]{:S(2)}, u32[]{:S(2)}) %all-to-all-start.1) | async-done | bytes 16416 | tf_op jit(solution)/shard_map/all_to_all | solution.py:26
  318.2 0.7 reduce.1
  318.9 0.1 reshape.62
  319.0 0.0 copy-done
  319.0 0.8 fusion.9
  319.8 0.6 copy.20
  (1 shorter events, 0.0 us)
Async XLA Ops:
  6.5 190.5 %all-gather.2.cloned.1.call-start = ((), (), s32[]{:S(2)}) async-start(), calls=%async_computation.3 | async-start | bytes 13926400 | tf_op jit(solution)/shard_map/all_gather | solution.py:14
  7.3 285.3 %copy-start.1 = (f32[16]{0:T(128)S(1)}, f32[16]{0:T(128)}, u32[]{:S(2)}) copy-start(f32[16]{0:T(128)} %param.8) | copy-start | bytes 196
  7.3 285.9 %copy-start.2 = (f32[64]{0:T(128)S(1)}, f32[64]{0:T(128)}, u32[]{:S(2)}) copy-start(f32[64]{0:T(128)} %param.9) | copy-start | bytes 772
  7.3 311.7 %copy-start = (f32[1,16,4,64]{3,2,1,0:T(4,128)S(1)}, f32[1,16,4,64]{3,2,1,0:T(4,128)}, u32[]{:S(2)}) copy-start(f32[1,16,4,64]{3,2,1,0:T(4,128)} %param.7) | copy-start | bytes 49156
  7.3 274.6 %reduce-scatter.2.cloned.1.call-start = ((), (), s32[]{:S(2)}) async-start(), calls=%async_computation.4 | async-start | bytes 557056 | tf_op jit(solution)/shard_map/reduce_scatter | solution.py:25
  283.5 18.0 %all-to-all-start = ((f32[16,1,256]{2,1,0:T(1,128)}), f32[16,1,256]{2,1,0:T(1,128)S(1)}, u32[]{:S(2)}, u32[]{:S(2)}) async-start(f32[16,1,256]{2,1,0:T(1,128)} %reshape.59), calls=%async_computation.1 | async-start | bytes 32768 | tf_op jit(solution)/shard_map/all_to_all | solution.py:27
  303.9 14.3 %all-to-all-start.1 = ((f32[16,1,256]{2,1,0:T(1,128)}), f32[16,1,256]{2,1,0:T(1,128)S(1)}, u32[]{:S(2)}, u32[]{:S(2)}) async-start(f32[16,1,256]{2,1,0:T(1,128)} %reshape.61), calls=%async_computation.2 | async-start | bytes 32768 | tf_op jit(solution)/shard_map/all_to_all | solution.py:26
Sparse Core Ops, SparseCore 0:
  9.9 187.0 all-gather.1
  223.5 58.3 reduce-scatter.1
where the time goes:
time: 328 us; the launch traced here: 327 us
  waiting for transfers between devices  262 us (80%)
  matrix products  26.4 us (8%)
  starting transfers between devices  17.5 us (5%)
  between operations  13.5 us (4%)
  local copies, waits for them, and re-layouts  4.61 us (1%)
    all_gather x1, waiting for transfers between devices, on_device(): shard_piece = lax.all_gather(amplitudes, 'row', axis=0, tiled=True)  190 us
    reduce_scatter x1, waiting for transfers between devices, on_device(): lax.psum_scatter(partial_value, 'col', scatter_dimension=0, tiled=True)  58.5 us
    dot_general x1, matrix products, on_device(): lax.dot_general(flattened, integral_slab, (((1,), (1,)), ((), ())), preci...  26.4 us
    all_to_all x1, starting transfers between devices, on_device(): lax.all_to_all(summed, 'row', split_axis=3, concat_axis=2, tiled=True)  9.03 us
    all_to_all x1, starting transfers between devices, on_device(): lax.all_to_all(lax.all_to_all(summed, 'row', split_axis=3, concat_axis=2,...  8.43 us
    all_to_all x1, waiting for transfers between devices, on_device(): lax.all_to_all(summed, 'row', split_axis=3, concat_axis=2, tiled=True)  8.25 us
  transfers between devices with their start and end apart: 4, of which 4 were waited for; matrix products, arithmetic and copies ran while one was open for 0% of the time, Pallas kernels for 0%

commit v1 on v0

v1 whole, which is shorter than its diff:
```python
import jax
import jax.numpy as jnp
from jax import lax
from jax.experimental import pallas as pl
from jax.experimental.pallas import tpu as pltpu
from jax.sharding import PartitionSpec as P


NR, NC = 16, 16
NZ = 8
ND = 400
LANES = 128
NJ, NAB = 16, 256
TA, TB = 50, 29
F32, BF16 = jnp.float32, jnp.bfloat16


def rows_of_rest(x, n):
    parts = [x(c) for c in range(n)]
    if n < 8:
        parts.append(jnp.zeros(parts[0].shape[:-1] + (LANES - 16 * n,), F32))
    return jnp.concatenate(parts, axis=-1)


def pack_t_kernel(t_ref, a_ref, b_ref):
    for ref, at, c0, n in ((a_ref, 0, 0, 8), (a_ref, 25, 8, 8), (b_ref, 0, 16, 8), (b_ref, 25, 24, 1)):
        for c in range(n):
            for s in range(3):
                ref[at + 3 * c + s] = t_ref[c0 + c, :, LANES * s : LANES * (s + 1)]
        ref[at + 3 * n] = rows_of_rest(lambda c: t_ref[c0 + c, :, 384:400], n)


def pack_t(t):
    return pl.pallas_call(
        pack_t_kernel,
        out_shape=(
            jax.ShapeDtypeStruct((TA, NJ, LANES), F32),
            jax.ShapeDtypeStruct((TB, NJ, LANES), F32),
        ),
        name="pack_t",
    )(t)


def split(x):
    hi = x.astype(BF16)
    return hi, (x - hi.astype(F32)).astype(BF16)


def pack_v_group(v_ref, h_ref, l_ref, at, n):
    for c in range(n):
        for s in range(3):
            t = at + 3 * c + s
            h_ref[t], l_ref[t] = split(v_ref[c, :, LANES * s : LANES * (s + 1)])
    t = at + 3 * n
    h_ref[t], l_ref[t] = split(rows_of_rest(lambda c: v_ref[c, :, 384:400], n))


def pack_va_kernel(v_ref, h_ref, l_ref):
    pack_v_group(v_ref, h_ref, l_ref, 0, 8)


def pack_vb_kernel(v_ref, w_ref, h_ref, l_ref):
    pack_v_group(v_ref, h_ref, l_ref, 0, 8)
    pack_v_group(w_ref, h_ref, l_ref, 25, 1)


def pack_va(v):
    out = jax.ShapeDtypeStruct((TA, NAB, LANES), BF16)
    spec = pl.BlockSpec((25, 64, LANES), lambda g, a: (g, a, 0))
    return pl.pallas_call(
        pack_va_kernel,
        grid=(2, 4),
        in_specs=[pl.BlockSpec((None, 8, 64, ND), lambda g, a: (a, g, 0, 0))],
        out_specs=(spec, spec),
        out_shape=(out, out),
        name="pack_va",
    )(v)


def pack_vb(v):
    out = jax.ShapeDtypeStruct((TB, NAB, LANES), BF16)
    spec = pl.BlockSpec((TB, 64, LANES), lambda a: (0, a, 0))
    return pl.pallas_call(
        pack_vb_kernel,
        grid=(4,),
        in_specs=[
            pl.BlockSpec((None, 8, 64, ND), lambda a: (a, 2, 0, 0)),
            pl.BlockSpec((None, 1, 64, ND), lambda a: (a, 24, 0, 0)),
        ],
        out_specs=(spec, spec),
        out_shape=(out, out),
        name="pack_vb",
    )(v, v)


def product(t_refs, vh_ref, vl_ref, first, n):
    cat = lambda ref: jnp.concatenate([ref[first + t] for t in range(n)], axis=-1)
    hi, lo = split(jnp.concatenate([cat(r) for r in t_refs], axis=0))
    vh, vl = cat(vh_ref), cat(vl_ref)
    dims = (((1,), (1,)), ((), ()))
    both = lax.dot_general(jnp.concatenate([hi, lo], axis=0), vh, dims, preferred_element_type=F32)
    m = hi.shape[0]
    return both[:m] + both[m:] + lax.dot_general(hi, vl, dims, preferred_element_type=F32)


def product_b(refs, vh, vl):
    rows = []
    for ref in refs:
        rows += [ref.at[0], ref.at[1]] if len(ref.shape) == 4 else [ref]
    total = product(rows, vh, vl, 0, 6)
    for first, n in ((6, 6), (12, 6), (18, 6), (24, 5)):
        total += product(rows, vh, vl, first, n)
    return total


STEPS_A = 5


def dot_a_kernel(*refs):
    *t_refs, vh, vl, out = refs
    value = product(t_refs, vh, vl, 0, TA // STEPS_A)

    @pl.when(pl.program_id(0) == 0)
    def _():
        out[...] = value

    @pl.when(pl.program_id(0) > 0)
    def _():
        out[...] += value


def dot_a(blocks, vh, vl):
    n = len(blocks)
    tiles = TA // STEPS_A
    tspec = pl.BlockSpec((tiles, NJ, LANES), lambda s: (s, 0, 0))
    vspec = pl.BlockSpec((tiles, NAB, LANES), lambda s: (s, 0, 0))
    return pl.pallas_call(
        dot_a_kernel,
        grid=(STEPS_A,),
        in_specs=[tspec] * n + [vspec, vspec],
        out_specs=pl.BlockSpec((NJ * n, NAB), lambda s: (0, 0)),
        out_shape=jax.ShapeDtypeStruct((NJ * n, NAB), F32),
        name="dot_a",
    )(*blocks, vh, vl)


def dot_b_kernel(*refs):
    *t_refs, vh, vl, out = refs
    out[...] = product_b(t_refs, vh, vl)


def dot_b(blocks, rows, vh, vl):
    return pl.pallas_call(
        dot_b_kernel, out_shape=jax.ShapeDtypeStruct((rows, NAB), F32), name="dot_b"
    )(*blocks, vh, vl)


def absolute_row(row, dz, dy):
    return (((row >> 1) + dz) & (NZ - 1)) * 2 + ((row & 1) ^ dy)


def last_kernel(where, n1, row_ref, *refs):
    *t_refs, vh, vl, pa1, pa2, pb, out, left, right = refs
    new = product_b(t_refs, vh, vl)
    row = row_ref[0]
    for q, (dz, dy) in enumerate(where):
        here = slice(NJ * q, NJ * (q + 1))
        there = slice(NJ * (q - n1), NJ * (q - n1 + 1))
        block = pa1[here, :] + pb[here, :] if q < n1 else pa2[there, :] + new[there, :]
        at = pl.ds(pl.multiple_of(absolute_row(row, dz, dy) * NJ, NJ), NJ)
        left[at, :] = block[:, :LANES]
        right[at, :] = block[:, LANES:]
    for k in range(NC):
        for ref, lanes in ((left, slice(0, LANES)), (right, slice(LANES, NAB))):
            out[k, :NJ, lanes] = ref[NJ * k : NJ * (k + 1), :]
            out[k, NJ:, lanes] = ref[pl.ds(k, NJ, stride=NJ), :]


def last(row, where, n1, blocks, vh, vl, pa1, pa2, pb):
    return pl.pallas_call(
        lambda *refs: last_kernel(where, n1, *refs),
        in_specs=[pl.BlockSpec(memory_space=pltpu.SMEM)]
        + [pl.BlockSpec(memory_space=pltpu.VMEM)] * (len(blocks) + 5),
        out_specs=pl.BlockSpec(memory_space=pltpu.VMEM),
        out_shape=jax.ShapeDtypeStruct((NC, 2 * NJ, NAB), F32),
        scratch_shapes=[pltpu.VMEM((NAB, LANES), F32)] * 2,
        name="last",
    )(row, *blocks, vh, vl, pa1, pa2, pb)


def permute_lanes(x, source):
    lane = lax.broadcasted_iota(jnp.int32, (NAB, NAB), 1)
    one_hot = (lax.broadcasted_iota(jnp.int32, (NAB, NAB), 0) == source(lane)).astype(BF16)
    p1, r1 = x.astype(BF16), x - x.astype(BF16).astype(F32)
    p2 = r1.astype(BF16)
    p3 = (r1 - p2.astype(F32)).astype(BF16)
    y = jnp.dot(jnp.concatenate([p1, p2, p3], axis=0), one_hot, preferred_element_type=F32)
    m = x.shape[0]
    return y[:m] + y[m : 2 * m] + y[2 * m :]


def fold_kernel(r_ref, d_ref, e_ref):
    total = r_ref[0]
    for k in range(1, NC):
        total += r_ref[k]
    d_ref[...] = total[:NJ]
    mixed = permute_lanes(total[NJ:], lambda n: ((n >> 2) & 3) * 64 + (n >> 4) * 4 + (n & 3))
    zeros = jnp.zeros((8, LANES - 32), F32)
    for r in range(NR):
        lanes = slice(16 * r, 16 * (r + 1))
        e_ref[r] = jnp.concatenate([mixed[:8, lanes], mixed[8:, lanes], zeros], axis=-1)


def fold(r):
    return pl.pallas_call(
        fold_kernel,
        out_shape=(
            jax.ShapeDtypeStruct((NJ, NAB), F32),
            jax.ShapeDtypeStruct((NR, 8, LANES), F32),
        ),
        name="fold",
    )(r)


def finish_kernel(d_ref, m_ref, rest_ref, den_ref, out_ref):
    halves = [
        jnp.concatenate([m_ref[r, :, 16 * h : 16 * (h + 1)] for r in range(NR)], axis=-1)
        for h in range(2)
    ]
    mirror = permute_lanes(
        jnp.concatenate(halves, axis=0), lambda n: ((n >> 2) & 15) * 16 + (n & 3) * 4 + (n >> 6)
    )
    value = (d_ref[...] + mirror + rest_ref[...]) / den_ref[...]
    for a in range(4):
        out_ref[:, a, :] = value[:, 64 * a : 64 * (a + 1)]


def finish(d, m, rest, den):
    return pl.pallas_call(
        finish_kernel, out_shape=jax.ShapeDtypeStruct((NJ, 4, 64), F32), name="finish"
    )(d, m, rest, den)


AXES = ("row", "col")


def moves(dz=0, dy=0):
    pairs = []
    for z in range(NZ):
        for h in range(2):
            for k in range(NC):
                to = ((z + dz) % NZ * 2 + (h ^ dy)) * NC + k
                pairs.append(((z * 2 + h) * NC + k, to))
    return pairs


UP, DOWN, ACROSS = moves(dz=1), moves(dz=-1), moves(dy=1)


def send(x, where):
    return lax.ppermute(x, AXES, where)


def on_device(amplitudes, integrals, rest, occ_energy, vir_energy):
    row = lax.axis_index("row")
    col = lax.axis_index("col")
    a0, b0 = pack_t(jnp.transpose(amplitudes, (0, 2, 1, 3))[0])
    v = jnp.transpose(integrals, (0, 2, 1, 3))
    vah, val = pack_va(v)
    vbh, vbl = pack_vb(v)

    bx = send(b0, ACROSS)
    au, ad, yu, yd = [a0], [a0], [send(a0, ACROSS)], [None]
    bb = jnp.stack([b0, bx])
    bu, bd = [bb], [bb]
    for _ in range(3):
        au.append(send(au[-1], UP))
        ad.append(send(ad[-1], DOWN))
        bu.append(send(bu[-1], UP))
        bd.append(send(bd[-1], DOWN))
        yu.append(send(au[-1], ACROSS))
        yd.append(send(ad[-1], ACROSS))
    a4 = send(au[3], UP)
    a4x = send(yd[3], DOWN)
    b4 = send(bu[3][0], UP)
    b4x = send(bd[3][1], DOWN)

    blocks, where, pairs = [au[0], yu[0]], [(0, 0), (0, 1)], [bb]
    for s in (1, 2, 3):
        blocks += [au[s], yu[s], ad[s], yd[s]]
        where += [(-s, 0), (-s, 1), (s, 0), (s, 1)]
        pairs += [bu[s], bd[s]]
    blocks += [a4, a4x]
    where += [(4, 0), (4, 1)]
    n1 = 10
    pa1 = dot_a(blocks[:n1], vah, val)
    pa2 = dot_a(blocks[n1:], vah, val)
    pb = dot_b(pairs[:5], NJ * n1, vbh, vbl)
    partial = last(row.reshape(1), where, n1, pairs[5:] + [b4, b4x], vbh, vbl, pa1, pa2, pb)

    received = lax.all_to_all(partial, "col", 0, 0, tiled=True)
    direct, messages = fold(received)
    mirror = lax.all_to_all(messages, "row", 0, 0, tiled=True)

    vir_local = lax.dynamic_slice_in_dim(vir_energy, row * 4, 4, 0)
    occ_local = lax.dynamic_slice_in_dim(occ_energy, col, 1, 0)
    den = (
        vir_local[None, :, None] + vir_energy[None, None, :] - occ_local[:, None, None]
        - occ_energy[:, None, None]
    )
    out = finish(direct, mirror, rest.reshape(NJ, NAB), den.reshape(NJ, NAB))
    return out[None]


def solution(mesh):
    in_specs = (
        P("row", None, "col", None),
        P("row", None, "col", None),
        P("col", None, "row", None),
        P(),
        P(),
    )

    return jax.shard_map(
        on_device, mesh=mesh, in_specs=in_specs, out_specs=P("col", None, "row", None), check_vma=False
    )
```

time: 328 us -> 178 us (0.54)
  waiting for transfers between devices: 262 us -> 58 us
  starting transfers between devices: 17.5 us -> 68.6 us
  Pallas kernels: 0 us -> 43.2 us
  matrix products: 26.4 us -> 0 us
  between operations: 13.5 us -> 0.22 us
    all_gather x1 -> x0, waiting for transfers between devices: 190 us -> none  [on_device(): shard_piece = lax.all_gather(amplitudes, 'row', axis=0, tiled=True)]
    reduce_scatter x1 -> x0, waiting for transfers between devices: 58.5 us -> none  [on_device(): lax.psum_scatter(partial_value, 'col', scatter_dimension=0, tiled=True)]
    ppermute x0 -> x24, starting transfers between devices: none -> 46.1 us  [send(): return lax.ppermute(x, AXES, where)]
    pallas_call x0 -> x9, Pallas kernels: none -> 43.2 us  [the longest x2 14 us: dot_a(): pl.pallas_call(dot_a_kernel, grid=(STEPS_A,), in_specs=[tspec] * n + [vsp...]
    ppermute x0 -> x24, waiting for transfers between devices: none -> 41.8 us  [send(): return lax.ppermute(x, AXES, where)]
    dot_general x1 -> x0, matrix products: 26.4 us -> none  [on_device(): lax.dot_general(flattened, integral_slab, (((1,), (1,)), ((), ())), preci...]
    all_to_all x2, starting transfers between devices: 17.5 us -> 22.6 us  [the longest x1 15.2 us: on_device(): received = lax.all_to_all(partial, 'col', 0, 0, tiled=True)]
  transfers between devices with their start and end apart: 4 -> 26, of which waited for: 4 -> 11; matrix products, arithmetic and copies ran while one was open for 0% -> 2% of each run, Pallas kernels for 0% -> 18%
where the time goes in v1:
time: 178 us; the launch traced here: 177 us
  starting transfers between devices  68.6 us (39%)
  waiting for transfers between devices  58 us (33%)
  Pallas kernels  43.2 us (24%)
  local copies, waits for them, and re-layouts  4.59 us (3%)
  other arithmetic  2.29 us (1%)
    ppermute x24, starting transfers between devices, send(): return lax.ppermute(x, AXES, where)  46.1 us
    ppermute x24, waiting for transfers between devices, send(): return lax.ppermute(x, AXES, where)  41.8 us
    all_to_all x1, starting transfers between devices, on_device(): received = lax.all_to_all(partial, 'col', 0, 0, tiled=True)  15.2 us
    pallas_call x2, Pallas kernels, dot_a(): pl.pallas_call(dot_a_kernel, grid=(STEPS_A,), in_specs=[tspec] * n + [vsp...  14 us
    pallas_call x1, Pallas kernels, pack_va(): pl.pallas_call(pack_va_kernel, grid=(2, 4), in_specs=[pl.BlockSpec((None,...  8.8 us
    all_to_all x1, waiting for transfers between devices, on_device(): mirror = lax.all_to_all(messages, 'row', 0, 0, tiled=True)  8.77 us
    all_to_all x1, waiting for transfers between devices, on_device(): received = lax.all_to_all(partial, 'col', 0, 0, tiled=True)  7.42 us
    all_to_all x1, starting transfers between devices, on_device(): mirror = lax.all_to_all(messages, 'row', 0, 0, tiled=True)  7.37 us
  transfers between devices with their start and end apart: 26, of which 11 were waited for; matrix products, arithmetic and copies ran while one was open for 2% of the time, Pallas kernels for 18%

profile of v1, /device:TPU:1, one launch (start us, length us, event | category | flops | bytes accessed | tf_op | source)
XLA Modules:
  0.0 177.0 jit_solution(4727768870533350258)
XLA Ops:
  0.0 2.1 %pack_t.1 = (f32[50,16,128]{2,1,0:T(8,128)}, f32[29,16,128]{2,1,0:T(8,128)}) custom-call(f32[25,16,400]{2,1,0:T(8,128)} %bitcast.16), custom_call_target="tpu_custom_call" | custom-call | tf_op jit(solution)/shard_map/pack_t/pallas_call | solution.py:34
  2.1 3.7 %collective-permute-start = (f32[29,16,128]{2,1,0:T(8,128)}, f32[29,16,128]{2,1,0:T(8,128)S(1)}, u32[]{:S(2)}, u32[]{:S(2)}) collective-permute-start(f32[29,16,128]{2,1,0:T(8,128)} %get-tuple-element.13), channel_id=1, source_target_pairs={{0,16},{1,17},{2,18},{3,19},{4,20},{5,21},{6,22},{7,23},{8,24},{9,... | collective-permute-start | bytes 712712 | tf_op jit(solution)/shard_map/ppermute | solution.py:261
  5.8 4.8 %collective-permute-done = f32[29,16,128]{2,1,0:T(8,128)S(1)} collective-permute-done((f32[29,16,128]{2,1,0:T(8,128)}, f32[29,16,128]{2,1,0:T(8,128)S(1)}, u32[]{:S(2)}, u32[]{:S(2)}) %collective-permute-start) | collective-permute-done | bytes 237600 | tf_op jit(solution)/shard_map/ppermute | solution.py:261
  10.6 1.0 pad_maximum_fusion.refs_0_
  11.6 2.4 %collective-permute-start.1 = (f32[2,29,16,128]{3,2,1,0:T(8,128)S(1)}, f32[2,29,16,128]{3,2,1,0:T(8,128)S(1)}, u32[]{:S(2)}, u32[]{:S(2)}) collective-permute-start(f32[2,29,16,128]{3,2,1,0:T(8,128)S(1)} %pad_maximum_fusion.refs_0_), channel_id=1, source_target_pairs={{0,32},{1,33},{2,34},{3,35},{4,36},{5,37},{6,38},{7,39},{8,40},{9,... | collective-permute-start | bytes 1425416 | tf_op jit(solution)/shard_map/ppermute | solution.py:261
  14.0 4.0 %collective-permute-start.12 = (f32[50,16,128]{2,1,0:T(8,128)}, f32[50,16,128]{2,1,0:T(8,128)S(1)}, u32[]{:S(2)}, u32[]{:S(2)}) collective-permute-start(f32[50,16,128]{2,1,0:T(8,128)} %get-tuple-element.16.refs_0_), channel_id=1, source_target_pairs={{0,224},{1,225},{2,226},{3,227},{4,228},{5,229},{6,230},{7,231},{8... | collective-permute-start | bytes 1228808 | tf_op jit(solution)/shard_map/ppermute | solution.py:261
  18.0 0.0 collective-permute-start.10
  18.0 2.7 %collective-permute-start.4 = (f32[2,29,16,128]{3,2,1,0:T(8,128)S(1)}, f32[2,29,16,128]{3,2,1,0:T(8,128)S(1)}, u32[]{:S(2)}, u32[]{:S(2)}) collective-permute-start(f32[2,29,16,128]{3,2,1,0:T(8,128)S(1)} %pad_maximum_fusion.refs_0_), channel_id=1, source_target_pairs={{0,224},{1,225},{2,226},{3,227},{4,228},{5,229},{6,230},{7,231},{8... | collective-permute-start | bytes 1425416 | tf_op jit(solution)/shard_map/ppermute | solution.py:261
  20.7 2.9 %collective-permute-start.9 = (f32[50,16,128]{2,1,0:T(8,128)}, f32[50,16,128]{2,1,0:T(8,128)S(1)}, u32[]{:S(2)}, u32[]{:S(2)}) collective-permute-start(f32[50,16,128]{2,1,0:T(8,128)} %get-tuple-element.16.refs_0_), channel_id=1, source_target_pairs={{0,16},{1,17},{2,18},{3,19},{4,20},{5,21},{6,22},{7,23},{8,24},{9,... | collective-permute-start | bytes 1228808 | tf_op jit(solution)/shard_map/ppermute | solution.py:261
  23.6 2.0 %collective-permute-done.12.refs_4_ = f32[50,16,128]{2,1,0:T(8,128)S(1)} collective-permute-done((f32[50,16,128]{2,1,0:T(8,128)}, f32[50,16,128]{2,1,0:T(8,128)S(1)}, u32[]{:S(2)}, u32[]{:S(2)}) %collective-permute-start.12) | collective-permute-done | bytes 409632 | tf_op jit(solution)/shard_map/ppermute | solution.py:261
  25.6 3.3 %collective-permute-start.16 = (f32[50,16,128]{2,1,0:T(8,128)S(1)}, f32[50,16,128]{2,1,0:T(8,128)S(1)}, u32[]{:S(2)}, u32[]{:S(2)}) collective-permute-start(f32[50,16,128]{2,1,0:T(8,128)S(1)} %collective-permute-done.12.refs_4_), channel_id=1, source_target_pairs={{0,224},{1,225},{2,226},{3,227},{4,228},{5,229},{6,230},{7,231},{8... | collective-permute-start | bytes 1228808 | tf_op jit(solution)/shard_map/ppermute | solution.py:261
  28.9 0.0 collective-permute-done.1.refs_1_
  28.9 0.0 collective-permute-start.2
  29.0 7.5 %collective-permute-done.10.refs_2_ = f32[50,16,128]{2,1,0:T(8,128)S(1)} collective-permute-done((f32[50,16,128]{2,1,0:T(8,128)}, f32[50,16,128]{2,1,0:T(8,128)S(1)}, u32[]{:S(2)}, u32[]{:S(2)}) %collective-permute-start.10) | collective-permute-done | bytes 409632 | tf_op jit(solution)/shard_map/ppermute | solution.py:261
  36.4 0.0 collective-permute-start.14
  36.4 0.0 collective-permute-done.4.refs_2_
  36.5 2.7 %collective-permute-start.5 = (f32[2,29,16,128]{3,2,1,0:T(8,128)S(1)}, f32[2,29,16,128]{3,2,1,0:T(8,128)S(1)}, u32[]{:S(2)}, u32[]{:S(2)}) collective-permute-start(f32[2,29,16,128]{3,2,1,0:T(8,128)S(1)} %collective-permute-done.4.refs_2_), channel_id=1, source_target_pairs={{0,224},{1,225},{2,226},{3,227},{4,228},{5,229},{6,230},{7,231},{8... | collective-permute-start | bytes 1425416 | tf_op jit(solution)/shard_map/ppermute | solution.py:261
  39.1 0.0 collective-permute-done.9.refs_1_
  39.1 2.9 %collective-permute-start.11 = (f32[50,16,128]{2,1,0:T(8,128)S(1)}, f32[50,16,128]{2,1,0:T(8,128)S(1)}, u32[]{:S(2)}, u32[]{:S(2)}) collective-permute-start(f32[50,16,128]{2,1,0:T(8,128)S(1)} %collective-permute-done.10.refs_2_), channel_id=1, source_target_pairs={{0,16},{1,17},{2,18},{3,19},{4,20},{5,21},{6,22},{7,23},{8,24},{9,... | collective-permute-start | bytes 1228808 | tf_op jit(solution)/shard_map/ppermute | solution.py:261
  42.0 2.4 %collective-permute-done.16.refs_8_ = f32[50,16,128]{2,1,0:T(8,128)S(1)} collective-permute-done((f32[50,16,128]{2,1,0:T(8,128)S(1)}, f32[50,16,128]{2,1,0:T(8,128)S(1)}, u32[]{:S(2)}, u32[]{:S(2)}) %collective-permute-start.16) | collective-permute-done | bytes 409632 | tf_op jit(solution)/shard_map/ppermute | solution.py:261
  44.5 3.4 %collective-permute-start.20 = (f32[50,16,128]{2,1,0:T(8,128)S(1)}, f32[50,16,128]{2,1,0:T(8,128)S(1)}, u32[]{:S(2)}, u32[]{:S(2)}) collective-permute-start(f32[50,16,128]{2,1,0:T(8,128)S(1)} %collective-permute-done.16.refs_8_), channel_id=1, source_target_pairs={{0,224},{1,225},{2,226},{3,227},{4,228},{5,229},{6,230},{7,231},{8... | collective-permute-start | bytes 1228808 | tf_op jit(solution)/shard_map/ppermute | solution.py:261
  47.9 0.1 collective-permute-start.3
  48.0 7.4 %collective-permute-done.14.refs_6_ = f32[50,16,128]{2,1,0:T(8,128)S(1)} collective-permute-done((f32[50,16,128]{2,1,0:T(8,128)S(1)}, f32[50,16,128]{2,1,0:T(8,128)S(1)}, u32[]{:S(2)}, u32[]{:S(2)}) %collective-permute-start.14) | collective-permute-done | bytes 409632 | tf_op jit(solution)/shard_map/ppermute | solution.py:261
  55.4 2.9 %collective-permute-start.13 = (f32[50,16,128]{2,1,0:T(8,128)S(1)}, f32[50,16,128]{2,1,0:T(8,128)S(1)}, u32[]{:S(2)}, u32[]{:S(2)}) collective-permute-start(f32[50,16,128]{2,1,0:T(8,128)S(1)} %collective-permute-done.12.refs_4_), channel_id=1, source_target_pairs={{0,16},{1,17},{2,18},{3,19},{4,20},{5,21},{6,22},{7,23},{8,24},{9,... | collective-permute-start | bytes 1228808 | tf_op jit(solution)/shard_map/ppermute | solution.py:261
  58.3 1.2 collective-permute-start.6
  59.5 0.3 collective-permute-start.18
  59.8 3.7 %collective-permute-done.20.refs_2_ = f32[50,16,128]{2,1,0:T(8,128)S(1)} collective-permute-done((f32[50,16,128]{2,1,0:T(8,128)S(1)}, f32[50,16,128]{2,1,0:T(8,128)S(1)}, u32[]{:S(2)}, u32[]{:S(2)}) %collective-permute-start.20) | collective-permute-done | bytes 409632 | tf_op jit(solution)/shard_map/ppermute | solution.py:261
  63.5 2.9 %collective-permute-start.21 = (f32[50,16,128]{2,1,0:T(8,128)S(1)}, f32[50,16,128]{2,1,0:T(8,128)}, u32[]{:S(2)}, u32[]{:S(2)}) collective-permute-start(f32[50,16,128]{2,1,0:T(8,128)S(1)} %collective-permute-done.20.refs_2_), channel_id=1, source_target_pairs={{0,16},{1,17},{2,18},{3,19},{4,20},{5,21},{6,22},{7,23},{8,24},{9,... | collective-permute-start | bytes 1228808 | tf_op jit(solution)/shard_map/ppermute | solution.py:261
  66.4 0.7 collective-permute-start.15
  67.1 0.1 copy-done.15
  67.1 2.3 %collective-permute-start.17 = (f32[50,16,128]{2,1,0:T(8,128)S(1)}, f32[50,16,128]{2,1,0:T(8,128)S(1)}, u32[]{:S(2)}, u32[]{:S(2)}) collective-permute-start(f32[50,16,128]{2,1,0:T(8,128)S(1)} %collective-permute-done.16.refs_8_), channel_id=1, source_target_pairs={{0,16},{1,17},{2,18},{3,19},{4,20},{5,21},{6,22},{7,23},{8,24},{9,... | collective-permute-start | bytes 1228808 | tf_op jit(solution)/shard_map/ppermute | solution.py:261
  69.5 0.7 slice_bitcast_fusion.1
  70.2 4.3 %collective-permute-done.18.refs_0_ = f32[50,16,128]{2,1,0:T(8,128)} collective-permute-done((f32[50,16,128]{2,1,0:T(8,128)S(1)}, f32[50,16,128]{2,1,0:T(8,128)}, u32[]{:S(2)}, u32[]{:S(2)}) %collective-permute-start.18) | collective-permute-done | bytes 409632 | tf_op jit(solution)/shard_map/ppermute | solution.py:261
  74.5 2.9 %collective-permute-start.19 = (f32[50,16,128]{2,1,0:T(8,128)}, f32[50,16,128]{2,1,0:T(8,128)}, u32[]{:S(2)}, u32[]{:S(2)}) collective-permute-start(f32[50,16,128]{2,1,0:T(8,128)} %collective-permute-done.18.refs_0_), channel_id=1, source_target_pairs={{0,16},{1,17},{2,18},{3,19},{4,20},{5,21},{6,22},{7,23},{8,24},{9,... | collective-permute-start | bytes 1228808 | tf_op jit(solution)/shard_map/ppermute | solution.py:261
  77.4 2.7 %collective-permute-start.23 = (f32[50,16,128]{2,1,0:T(8,128)}, f32[50,16,128]{2,1,0:T(8,128)}, u32[]{:S(2)}, u32[]{:S(2)}) collective-permute-start(f32[50,16,128]{2,1,0:T(8,128)} %collective-permute-done.21.refs_3_), channel_id=1, source_target_pairs={{0,224},{1,225},{2,226},{3,227},{4,228},{5,229},{6,230},{7,231},{8... | collective-permute-start | bytes 1228808 | tf_op jit(solution)/shard_map/ppermute | solution.py:261
  80.1 0.7 slice_bitcast_fusion
  80.8 1.0 collective-permute-done.15.refs_7_
  81.8 8.8 %collective-permute-done.17.refs_9_ = f32[50,16,128]{2,1,0:T(8,128)S(1)} collective-permute-done((f32[50,16,128]{2,1,0:T(8,128)S(1)}, f32[50,16,128]{2,1,0:T(8,128)S(1)}, u32[]{:S(2)}, u32[]{:S(2)}) %collective-permute-start.17) | collective-permute-done | bytes 409632 | tf_op jit(solution)/shard_map/ppermute | solution.py:261
  90.6 2.0 %collective-permute-start.8 = (f32[29,16,128]{2,1,0:T(8,128)}, f32[29,16,128]{2,1,0:T(8,128)}, u32[]{:S(2)}, u32[]{:S(2)}) collective-permute-start(f32[29,16,128]{2,1,0:T(8,128)} %slice_bitcast_fusion), channel_id=1, source_target_pairs={{0,224},{1,225},{2,226},{3,227},{4,228},{5,229},{6,230},{7,231},{8... | collective-permute-start | bytes 712712 | tf_op jit(solution)/shard_map/ppermute | solution.py:261
  92.6 8.8 %pack_va.1 = (bf16[50,256,128]{2,1,0:T(8,128)(2,1)}, bf16[50,256,128]{2,1,0:T(8,128)(2,1)}) custom-call(f32[4,25,64,400]{3,2,1,0:T(8,128)} %bitcast.13), custom_call_target="tpu_custom_call" | custom-call | tf_op jit(solution)/shard_map/pack_va/pallas_call | solution.py:70
  101.4 4.9 %pack_vb.1 = (bf16[29,256,128]{2,1,0:T(8,128)(2,1)}, bf16[29,256,128]{2,1,0:T(8,128)(2,1)}) custom-call(f32[4,25,64,400]{3,2,1,0:T(8,128)} %bitcast.14, f32[4,25,64,400]{3,2,1,0:T(8,128)} %bitcast.15), custom_call_target="tpu_custom_call" | custom-call | tf_op jit(solution)/shard_map/pack_vb/pallas_call | solution.py:83
  106.3 4.8 %dot_b.1.refs_9_ = f32[160,256]{1,0:T(8,128)} custom-call(f32[2,29,16,128]{3,2,1,0:T(8,128)} %copy-done.1, f32[2,29,16,128]{3,2,1,0:T(8,128)} %copy-done.4, f32[2,29,16,128]{3,2,1,0:T(8,128)} %copy-done.5, f32[2,29,16,128]{3,2,1,0:T(8,128)} %copy-done.6, f32[2,29,16,128]{3,2,1,0:T(8,128)} %copy-done.7, bf16[29,256,128]{2,1,0:T(8,128)(2,1)} %get-tuple-element.14.refs_5_, ...), custom_call_target="tpu_custom_call" | custom-call | tf_op jit(solution)/shard_map/dot_b/pallas_call | solution.py:153
  111.2 7.2 %dot_a.2.refs_7_ = f32[160,256]{1,0:T(8,128)} custom-call(f32[50,16,128]{2,1,0:T(8,128)} %get-tuple-element.16.refs_0_, f32[50,16,128]{2,1,0:T(8,128)} %copy-done.11, f32[50,16,128]{2,1,0:T(8,128)} %copy-done.10, f32[50,16,128]{2,1,0:T(8,128)} %copy-done.14, f32[50,16,128]{2,1,0:T(8,128)} %copy-done.9, f32[50,16,128]{2,1,0:T(8,128)} %copy-done.15, ...), custom_call_target="tpu_custom_call" | custom-call | tf_op jit(solution)/shard_map/dot_a/pallas_call | solution.py:137
  118.4 6.8 %dot_a.3.refs_8_ = f32[96,256]{1,0:T(8,128)} custom-call(f32[50,16,128]{2,1,0:T(8,128)} %collective-permute-done.18.refs_0_, f32[50,16,128]{2,1,0:T(8,128)} %collective-permute-done.19.refs_1_, f32[50,16,128]{2,1,0:T(8,128)} %copy-done.8, f32[50,16,128]{2,1,0:T(8,128)} %collective-permute-done.21.refs_3_, f32[50,16,128]{2,1,0:T(8,128)} %collective-permute-done.22.refs_4_, ...), custom_call_target="tpu_custom_call" | custom-call | tf_op jit(solution)/shard_map/dot_a/pallas_call | solution.py:137
  125.3 0.0 copy-start.20
  125.3 0.0 copy-start.19
  125.3 0.0 copy-start.21
  125.3 4.8 %last.1 = f32[16,32,256]{2,1,0:T(8,128)} custom-call(s32[1]{0:T(128)} %bitcast.refs_0_, f32[2,29,16,128]{3,2,1,0:T(8,128)} %copy-done.2, f32[2,29,16,128]{3,2,1,0:T(8,128)} %copy-done.3, f32[29,16,128]{2,1,0:T(8,128)} %collective-permute-done.7.refs_3_, f32[29,16,128]{2,1,0:T(8,128)} %collective-permute-done.8.refs_4_, ...), custom_call_target="tpu_custom_call" | custom-call | tf_op jit(solution)/shard_map/last/pallas_call | solution.py:180
  130.1 15.2 %all-to-all-start = ((f32[16,32,256]{2,1,0:T(8,128)}), f32[16,32,256]{2,1,0:T(8,128)S(1)}, u32[]{:S(2)}, u32[]{:S(2)}) async-start(f32[16,32,256]{2,1,0:T(8,128)} %last.1), calls=%async_computation | async-start | bytes 1048576 | tf_op jit(solution)/shard_map/all_to_all | solution.py:301
  145.3 0.1 dynamic_slice.6
  145.4 0.1 broadcast_reduce_fusion
  145.5 0.1 add.30
  145.6 0.1 add.32
  145.7 0.7 reshape.44.rest_ref
  146.4 0.6 dynamic_slice.7
  147.0 0.6 add_subtract_fusion
  147.6 7.4 %all-to-all-done.r_ref = f32[16,32,256]{2,1,0:T(8,128)S(1)} async-done(((f32[16,32,256]{2,1,0:T(8,128)}), f32[16,32,256]{2,1,0:T(8,128)S(1)}, u32[]{:S(2)}, u32[]{:S(2)}) %all-to-all-start) | async-done | bytes 524320 | tf_op jit(solution)/shard_map/all_to_all | solution.py:301
  155.0 0.8 copy-done
  155.8 1.9 %fold.1 = (f32[16,256]{1,0:T(8,128)}, f32[16,8,128]{2,1,0:T(8,128)}) custom-call(f32[16,32,256]{2,1,0:T(8,128)} %copy-done), custom_call_target="tpu_custom_call" | custom-call | tf_op jit(solution)/shard_map/fold/pallas_call | solution.py:215
  157.8 7.4 %all-to-all-start.1 = ((f32[16,8,128]{2,1,0:T(8,128)}), f32[16,8,128]{2,1,0:T(8,128)S(1)}, u32[]{:S(2)}, u32[]{:S(2)}) async-start(f32[16,8,128]{2,1,0:T(8,128)} %get-tuple-element.20), calls=%async_computation.1 | async-start | bytes 131072 | tf_op jit(solution)/shard_map/all_to_all | solution.py:303
  165.1 0.7 broadcast_subtract_fusion.den_ref
  165.8 8.8 %all-to-all-done.1.m_ref = f32[16,8,128]{2,1,0:T(8,128)S(1)} async-done(((f32[16,8,128]{2,1,0:T(8,128)}), f32[16,8,128]{2,1,0:T(8,128)S(1)}, u32[]{:S(2)}, u32[]{:S(2)}) %all-to-all-start.1) | async-done | bytes 65568 | tf_op jit(solution)/shard_map/all_to_all | solution.py:303
  174.6 0.6 copy-done.18
  175.2 1.8 %finish.1 = f32[16,4,64]{2,1,0:T(4,128)} custom-call(f32[16,256]{1,0:T(8,128)} %get-tuple-element.19.d_ref, f32[16,8,128]{2,1,0:T(8,128)} %copy-done.18, f32[16,256]{1,0:T(8,128)} %reshape.44.rest_ref, f32[16,256]{1,0:T(8,128)} %broadcast_subtract_fusion.den_ref), custom_call_target="tpu_custom_call" | custom-call | tf_op jit(solution)/shard_map/finish/pallas_call | solution.py:239
  (53 shorter events, 0.1 us)
Async XLA Ops:
  2.1 8.5 %collective-permute-start = (f32[29,16,128]{2,1,0:T(8,128)}, f32[29,16,128]{2,1,0:T(8,128)S(1)}, u32[]{:S(2)}, u32[]{:S(2)}) collective-permute-start(f32[29,16,128]{2,1,0:T(8,128)} %get-tuple-element.13), channel_id=1, source_target_pairs={{0,16},{1,17},{2,18},{3,19},{4,20},{5,21},{6,22},{7,23},{8,24},{9,... | collective-permute-start | bytes 712712 | tf_op jit(solution)/shard_map/ppermute | solution.py:261
  11.6 89.8 %copy-start.1 = (f32[2,29,16,128]{3,2,1,0:T(8,128)}, f32[2,29,16,128]{3,2,1,0:T(8,128)S(1)}, u32[]{:S(2)}) copy-start(f32[2,29,16,128]{3,2,1,0:T(8,128)S(1)} %pad_maximum_fusion.refs_0_) | copy-start | bytes 1425412
  11.6 17.3 %collective-permute-start.1 = (f32[2,29,16,128]{3,2,1,0:T(8,128)S(1)}, f32[2,29,16,128]{3,2,1,0:T(8,128)S(1)}, u32[]{:S(2)}, u32[]{:S(2)}) collective-permute-start(f32[2,29,16,128]{3,2,1,0:T(8,128)S(1)} %pad_maximum_fusion.refs_0_), channel_id=1, source_target_pairs={{0,32},{1,33},{2,34},{3,35},{4,36},{5,37},{6,38},{7,39},{8,40},{9,... | collective-permute-start | bytes 1425416 | tf_op jit(solution)/shard_map/ppermute | solution.py:261
  14.0 11.6 %collective-permute-start.12 = (f32[50,16,128]{2,1,0:T(8,128)}, f32[50,16,128]{2,1,0:T(8,128)S(1)}, u32[]{:S(2)}, u32[]{:S(2)}) collective-permute-start(f32[50,16,128]{2,1,0:T(8,128)} %get-tuple-element.16.refs_0_), channel_id=1, source_target_pairs={{0,224},{1,225},{2,226},{3,227},{4,228},{5,229},{6,230},{7,231},{8... | collective-permute-start | bytes 1228808 | tf_op jit(solution)/shard_map/ppermute | solution.py:261
  18.0 18.4 %collective-permute-start.10 = (f32[50,16,128]{2,1,0:T(8,128)}, f32[50,16,128]{2,1,0:T(8,128)S(1)}, u32[]{:S(2)}, u32[]{:S(2)}) collective-permute-start(f32[50,16,128]{2,1,0:T(8,128)} %get-tuple-element.16.refs_0_), channel_id=1, source_target_pairs={{0,32},{1,33},{2,34},{3,35},{4,36},{5,37},{6,38},{7,39},{8,40},{9,... | collective-permute-start | bytes 1228808 | tf_op jit(solution)/shard_map/ppermute | solution.py:261
  18.0 18.4 %collective-permute-start.4 = (f32[2,29,16,128]{3,2,1,0:T(8,128)S(1)}, f32[2,29,16,128]{3,2,1,0:T(8,128)S(1)}, u32[]{:S(2)}, u32[]{:S(2)}) collective-permute-start(f32[2,29,16,128]{3,2,1,0:T(8,128)S(1)} %pad_maximum_fusion.refs_0_), channel_id=1, source_target_pairs={{0,224},{1,225},{2,226},{3,227},{4,228},{5,229},{6,230},{7,231},{8... | collective-permute-start | bytes 1425416 | tf_op jit(solution)/shard_map/ppermute | solution.py:261
  20.7 18.4 %collective-permute-start.9 = (f32[50,16,128]{2,1,0:T(8,128)}, f32[50,16,128]{2,1,0:T(8,128)S(1)}, u32[]{:S(2)}, u32[]{:S(2)}) collective-permute-start(f32[50,16,128]{2,1,0:T(8,128)} %get-tuple-element.16.refs_0_), channel_id=1, source_target_pairs={{0,16},{1,17},{2,18},{3,19},{4,20},{5,21},{6,22},{7,23},{8,24},{9,... | collective-permute-start | bytes 1228808 | tf_op jit(solution)/shard_map/ppermute | solution.py:261
  25.6 41.4 %copy-start.9 = (f32[50,16,128]{2,1,0:T(8,128)}, f32[50,16,128]{2,1,0:T(8,128)S(1)}, u32[]{:S(2)}) copy-start(f32[50,16,128]{2,1,0:T(8,128)S(1)} %collective-permute-done.12.refs_4_) | copy-start | bytes 1228804
  25.6 18.9 %collective-permute-start.16 = (f32[50,16,128]{2,1,0:T(8,128)S(1)}, f32[50,16,128]{2,1,0:T(8,128)S(1)}, u32[]{:S(2)}, u32[]{:S(2)}) collective-permute-start(f32[50,16,128]{2,1,0:T(8,128)S(1)} %collective-permute-done.12.refs_4_), channel_id=1, source_target_pairs={{0,224},{1,225},{2,226},{3,227},{4,228},{5,229},{6,230},{7,231},{8... | collective-permute-start | bytes 1228808 | tf_op jit(solution)/shard_map/ppermute | solution.py:261
  28.9 72.4 %copy-start.4 = (f32[2,29,16,128]{3,2,1,0:T(8,128)}, f32[2,29,16,128]{3,2,1,0:T(8,128)S(1)}, u32[]{:S(2)}) copy-start(f32[2,29,16,128]{3,2,1,0:T(8,128)S(1)} %collective-permute-done.1.refs_1_) | copy-start | bytes 1425412
  28.9 19.0 %collective-permute-start.2 = (f32[2,29,16,128]{3,2,1,0:T(8,128)S(1)}, f32[2,29,16,128]{3,2,1,0:T(8,128)S(1)}, u32[]{:S(2)}, u32[]{:S(2)}) collective-permute-start(f32[2,29,16,128]{3,2,1,0:T(8,128)S(1)} %collective-permute-done.1.refs_1_), channel_id=1, source_target_pairs={{0,32},{1,33},{2,34},{3,35},{4,36},{5,37},{6,38},{7,39},{8,40},{9,... | collective-permute-start | bytes 1425416 | tf_op jit(solution)/shard_map/ppermute | solution.py:261
  36.4 30.6 %copy-start.10 = (f32[50,16,128]{2,1,0:T(8,128)}, f32[50,16,128]{2,1,0:T(8,128)S(1)}, u32[]{:S(2)}) copy-start(f32[50,16,128]{2,1,0:T(8,128)S(1)} %collective-permute-done.10.refs_2_) | copy-start | bytes 1228804
  36.4 19.0 %collective-permute-start.14 = (f32[50,16,128]{2,1,0:T(8,128)S(1)}, f32[50,16,128]{2,1,0:T(8,128)S(1)}, u32[]{:S(2)}, u32[]{:S(2)}) collective-permute-start(f32[50,16,128]{2,1,0:T(8,128)S(1)} %collective-permute-done.10.refs_2_), channel_id=1, source_target_pairs={{0,32},{1,33},{2,34},{3,35},{4,36},{5,37},{6,38},{7,39},{8,40},{9,... | collective-permute-start | bytes 1228808 | tf_op jit(solution)/shard_map/ppermute | solution.py:261
  36.4 65.0 %copy-start.5 = (f32[2,29,16,128]{3,2,1,0:T(8,128)}, f32[2,29,16,128]{3,2,1,0:T(8,128)S(1)}, u32[]{:S(2)}) copy-start(f32[2,29,16,128]{3,2,1,0:T(8,128)S(1)} %collective-permute-done.4.refs_2_) | copy-start | bytes 1425412
  36.5 21.9 %collective-permute-start.5 = (f32[2,29,16,128]{3,2,1,0:T(8,128)S(1)}, f32[2,29,16,128]{3,2,1,0:T(8,128)S(1)}, u32[]{:S(2)}, u32[]{:S(2)}) collective-permute-start(f32[2,29,16,128]{3,2,1,0:T(8,128)S(1)} %collective-permute-done.4.refs_2_), channel_id=1, source_target_pairs={{0,224},{1,225},{2,226},{3,227},{4,228},{5,229},{6,230},{7,231},{8... | collective-permute-start | bytes 1425416 | tf_op jit(solution)/shard_map/ppermute | solution.py:261
  39.1 8.8 %copy-start.11 = (f32[50,16,128]{2,1,0:T(8,128)}, f32[50,16,128]{2,1,0:T(8,128)S(1)}, u32[]{:S(2)}) copy-start(f32[50,16,128]{2,1,0:T(8,128)S(1)} %collective-permute-done.9.refs_1_) | copy-start | bytes 1228804
  39.1 20.4 %collective-permute-start.11 = (f32[50,16,128]{2,1,0:T(8,128)S(1)}, f32[50,16,128]{2,1,0:T(8,128)S(1)}, u32[]{:S(2)}, u32[]{:S(2)}) collective-permute-start(f32[50,16,128]{2,1,0:T(8,128)S(1)} %collective-permute-done.10.refs_2_), channel_id=1, source_target_pairs={{0,16},{1,17},{2,18},{3,19},{4,20},{5,21},{6,22},{7,23},{8,24},{9,... | collective-permute-start | bytes 1228808 | tf_op jit(solution)/shard_map/ppermute | solution.py:261
  44.5 35.6 %copy-start.12 = (f32[50,16,128]{2,1,0:T(8,128)}, f32[50,16,128]{2,1,0:T(8,128)S(1)}, u32[]{:S(2)}) copy-start(f32[50,16,128]{2,1,0:T(8,128)S(1)} %collective-permute-done.16.refs_8_) | copy-start | bytes 1228804
  44.5 19.0 %collective-permute-start.20 = (f32[50,16,128]{2,1,0:T(8,128)S(1)}, f32[50,16,128]{2,1,0:T(8,128)S(1)}, u32[]{:S(2)}, u32[]{:S(2)}) collective-permute-start(f32[50,16,128]{2,1,0:T(8,128)S(1)} %collective-permute-done.16.refs_8_), channel_id=1, source_target_pairs={{0,224},{1,225},{2,226},{3,227},{4,228},{5,229},{6,230},{7,231},{8... | collective-permute-start | bytes 1228808 | tf_op jit(solution)/shard_map/ppermute | solution.py:261
  47.9 53.5 %copy-start.6 = (f32[2,29,16,128]{3,2,1,0:T(8,128)}, f32[2,29,16,128]{3,2,1,0:T(8,128)S(1)}, u32[]{:S(2)}) copy-start(f32[2,29,16,128]{3,2,1,0:T(8,128)S(1)} %collective-permute-done.2.refs_3_) | copy-start | bytes 1425412
  47.9 19.1 %collective-permute-start.3 = (f32[2,29,16,128]{3,2,1,0:T(8,128)S(1)}, f32[2,29,16,128]{3,2,1,0:T(8,128)S(1)}, u32[]{:S(2)}, u32[]{:S(2)}) collective-permute-start(f32[2,29,16,128]{3,2,1,0:T(8,128)S(1)} %collective-permute-done.2.refs_3_), channel_id=1, source_target_pairs={{0,32},{1,33},{2,34},{3,35},{4,36},{5,37},{6,38},{7,39},{8,40},{9,... | collective-permute-start | bytes 1425416 | tf_op jit(solution)/shard_map/ppermute | solution.py:261
  55.4 35.2 %copy-start.13 = (f32[50,16,128]{2,1,0:T(8,128)}, f32[50,16,128]{2,1,0:T(8,128)S(1)}, u32[]{:S(2)}) copy-start(f32[50,16,128]{2,1,0:T(8,128)S(1)} %collective-permute-done.14.refs_6_) | copy-start | bytes 1228804
  55.4 11.0 %collective-permute-start.13 = (f32[50,16,128]{2,1,0:T(8,128)S(1)}, f32[50,16,128]{2,1,0:T(8,128)S(1)}, u32[]{:S(2)}, u32[]{:S(2)}) collective-permute-start(f32[50,16,128]{2,1,0:T(8,128)S(1)} %collective-permute-done.12.refs_4_), channel_id=1, source_target_pairs={{0,16},{1,17},{2,18},{3,19},{4,20},{5,21},{6,22},{7,23},{8,24},{9,... | collective-permute-start | bytes 1228808 | tf_op jit(solution)/shard_map/ppermute | solution.py:261
  58.3 43.1 %copy-start.7 = (f32[2,29,16,128]{3,2,1,0:T(8,128)}, f32[2,29,16,128]{3,2,1,0:T(8,128)S(1)}, u32[]{:S(2)}) copy-start(f32[2,29,16,128]{3,2,1,0:T(8,128)S(1)} %collective-permute-done.5.refs_4_) | copy-start | bytes 1425412
  58.3 19.1 %collective-permute-start.6 = (f32[2,29,16,128]{3,2,1,0:T(8,128)S(1)}, f32[2,29,16,128]{3,2,1,0:T(8,128)S(1)}, u32[]{:S(2)}, u32[]{:S(2)}) collective-permute-start(f32[2,29,16,128]{3,2,1,0:T(8,128)S(1)} %collective-permute-done.5.refs_4_), channel_id=1, source_target_pairs={{0,224},{1,225},{2,226},{3,227},{4,228},{5,229},{6,230},{7,231},{8... | collective-permute-start | bytes 1425416 | tf_op jit(solution)/shard_map/ppermute | solution.py:261
  59.5 7.5 %copy-start.14 = (f32[50,16,128]{2,1,0:T(8,128)}, f32[50,16,128]{2,1,0:T(8,128)S(1)}, u32[]{:S(2)}) copy-start(f32[50,16,128]{2,1,0:T(8,128)S(1)} %collective-permute-done.11.refs_3_) | copy-start | bytes 1228804
  59.5 15.0 %collective-permute-start.18 = (f32[50,16,128]{2,1,0:T(8,128)S(1)}, f32[50,16,128]{2,1,0:T(8,128)}, u32[]{:S(2)}, u32[]{:S(2)}) collective-permute-start(f32[50,16,128]{2,1,0:T(8,128)S(1)} %collective-permute-done.14.refs_6_), channel_id=1, source_target_pairs={{0,32},{1,33},{2,34},{3,35},{4,36},{5,37},{6,38},{7,39},{8,40},{9,... | collective-permute-start | bytes 1228808 | tf_op jit(solution)/shard_map/ppermute | solution.py:261
  63.5 13.9 %copy-start.8 = (f32[50,16,128]{2,1,0:T(8,128)}, f32[50,16,128]{2,1,0:T(8,128)S(1)}, u32[]{:S(2)}) copy-start(f32[50,16,128]{2,1,0:T(8,128)S(1)} %collective-permute-done.20.refs_2_) | copy-start | bytes 1228804
  63.5 13.9 %collective-permute-start.21 = (f32[50,16,128]{2,1,0:T(8,128)S(1)}, f32[50,16,128]{2,1,0:T(8,128)}, u32[]{:S(2)}, u32[]{:S(2)}) collective-permute-start(f32[50,16,128]{2,1,0:T(8,128)S(1)} %collective-permute-done.20.refs_2_), channel_id=1, source_target_pairs={{0,16},{1,17},{2,18},{3,19},{4,20},{5,21},{6,22},{7,23},{8,24},{9,... | collective-permute-start | bytes 1228808 | tf_op jit(solution)/shard_map/ppermute | solution.py:261
  66.4 0.8 copy-start.15
  66.4 15.5 %collective-permute-start.15 = (f32[50,16,128]{2,1,0:T(8,128)S(1)}, f32[50,16,128]{2,1,0:T(8,128)S(1)}, u32[]{:S(2)}, u32[]{:S(2)}) collective-permute-start(f32[50,16,128]{2,1,0:T(8,128)S(1)} %collective-permute-done.14.refs_6_), channel_id=1, source_target_pairs={{0,16},{1,17},{2,18},{3,19},{4,20},{5,21},{6,22},{7,23},{8,24},{9,... | collective-permute-start | bytes 1228808 | tf_op jit(solution)/shard_map/ppermute | solution.py:261
  67.1 34.3 %copy-start.2 = (f32[2,29,16,128]{3,2,1,0:T(8,128)}, f32[2,29,16,128]{3,2,1,0:T(8,128)S(1)}, u32[]{:S(2)}) copy-start(f32[2,29,16,128]{3,2,1,0:T(8,128)S(1)} %collective-permute-done.3.refs_1_) | copy-start | bytes 1425412
  67.1 23.5 %collective-permute-start.17 = (f32[50,16,128]{2,1,0:T(8,128)S(1)}, f32[50,16,128]{2,1,0:T(8,128)S(1)}, u32[]{:S(2)}, u32[]{:S(2)}) collective-permute-start(f32[50,16,128]{2,1,0:T(8,128)S(1)} %collective-permute-done.16.refs_8_), channel_id=1, source_target_pairs={{0,16},{1,17},{2,18},{3,19},{4,20},{5,21},{6,22},{7,23},{8,24},{9,... | collective-permute-start | bytes 1228808 | tf_op jit(solution)/shard_map/ppermute | solution.py:261
  74.5 44.0 %collective-permute-start.19 = (f32[50,16,128]{2,1,0:T(8,128)}, f32[50,16,128]{2,1,0:T(8,128)}, u32[]{:S(2)}, u32[]{:S(2)}) collective-permute-start(f32[50,16,128]{2,1,0:T(8,128)} %collective-permute-done.18.refs_0_), channel_id=1, source_target_pairs={{0,16},{1,17},{2,18},{3,19},{4,20},{5,21},{6,22},{7,23},{8,24},{9,... | collective-permute-start | bytes 1228808 | tf_op jit(solution)/shard_map/ppermute | solution.py:261
  77.4 41.0 %collective-permute-start.22 = (f32[50,16,128]{2,1,0:T(8,128)}, f32[50,16,128]{2,1,0:T(8,128)}, u32[]{:S(2)}, u32[]{:S(2)}) collective-permute-start(f32[50,16,128]{2,1,0:T(8,128)} %collective-permute-done.18.refs_0_), channel_id=1, source_target_pairs={{0,32},{1,33},{2,34},{3,35},{4,36},{5,37},{6,38},{7,39},{8,40},{9,... | collective-permute-start | bytes 1228808 | tf_op jit(solution)/shard_map/ppermute | solution.py:261
  77.4 24.0 %copy-start.3 = (f32[2,29,16,128]{3,2,1,0:T(8,128)}, f32[2,29,16,128]{3,2,1,0:T(8,128)S(1)}, u32[]{:S(2)}) copy-start(f32[2,29,16,128]{3,2,1,0:T(8,128)S(1)} %collective-permute-done.6.refs_2_) | copy-start | bytes 1425412
  77.4 41.0 %collective-permute-start.23 = (f32[50,16,128]{2,1,0:T(8,128)}, f32[50,16,128]{2,1,0:T(8,128)}, u32[]{:S(2)}, u32[]{:S(2)}) collective-permute-start(f32[50,16,128]{2,1,0:T(8,128)} %collective-permute-done.21.refs_3_), channel_id=1, source_target_pairs={{0,224},{1,225},{2,226},{3,227},{4,228},{5,229},{6,230},{7,231},{8... | collective-permute-start | bytes 1228808 | tf_op jit(solution)/shard_map/ppermute | solution.py:261
  81.8 10.8 %copy-start.16 = (f32[50,16,128]{2,1,0:T(8,128)}, f32[50,16,128]{2,1,0:T(8,128)S(1)}, u32[]{:S(2)}) copy-start(f32[50,16,128]{2,1,0:T(8,128)S(1)} %collective-permute-done.15.refs_7_) | copy-start | bytes 1228804
  81.8 43.4 %collective-permute-start.7 = (f32[29,16,128]{2,1,0:T(8,128)}, f32[29,16,128]{2,1,0:T(8,128)}, u32[]{:S(2)}, u32[]{:S(2)}) collective-permute-start(f32[29,16,128]{2,1,0:T(8,128)} %slice_bitcast_fusion.1), channel_id=1, source_target_pairs={{0,32},{1,33},{2,34},{3,35},{4,36},{5,37},{6,38},{7,39},{8,40},{9,... | collective-permute-start | bytes 712712 | tf_op jit(solution)/shard_map/ppermute | solution.py:261
  90.6 2.0 %copy-start.17 = (f32[50,16,128]{2,1,0:T(8,128)}, f32[50,16,128]{2,1,0:T(8,128)S(1)}, u32[]{:S(2)}) copy-start(f32[50,16,128]{2,1,0:T(8,128)S(1)} %collective-permute-done.17.refs_9_) | copy-start | bytes 1228804
  90.6 34.7 %collective-permute-start.8 = (f32[29,16,128]{2,1,0:T(8,128)}, f32[29,16,128]{2,1,0:T(8,128)}, u32[]{:S(2)}, u32[]{:S(2)}) collective-permute-start(f32[29,16,128]{2,1,0:T(8,128)} %slice_bitcast_fusion), channel_id=1, source_target_pairs={{0,224},{1,225},{2,226},{3,227},{4,228},{5,229},{6,230},{7,231},{8... | collective-permute-start | bytes 712712 | tf_op jit(solution)/shard_map/ppermute | solution.py:261
  125.3 20.1 %copy-start.20 = (f32[64]{0:T(128)S(1)}, f32[64]{0:T(128)}, u32[]{:S(2)}) copy-start(f32[64]{0:T(128)} %param.9) | copy-start | bytes 772
  125.3 20.4 %copy-start.19 = (f32[1,16,4,64]{3,2,1,0:T(4,128)S(1)}, f32[1,16,4,64]{3,2,1,0:T(4,128)}, u32[]{:S(2)}) copy-start(f32[1,16,4,64]{3,2,1,0:T(4,128)} %param.7) | copy-start | bytes 49156
  125.3 21.1 %copy-start.21 = (f32[16]{0:T(128)S(1)}, f32[16]{0:T(128)}, u32[]{:S(2)}) copy-start(f32[16]{0:T(128)} %param.8) | copy-start | bytes 196
  130.1 24.9 %all-to-all-start = ((f32[16,32,256]{2,1,0:T(8,128)}), f32[16,32,256]{2,1,0:T(8,128)S(1)}, u32[]{:S(2)}, u32[]{:S(2)}) async-start(f32[16,32,256]{2,1,0:T(8,128)} %last.1), calls=%async_computation | async-start | bytes 1048576 | tf_op jit(solution)/shard_map/all_to_all | solution.py:301
  155.0 0.8 copy-start
  157.8 16.8 %all-to-all-start.1 = ((f32[16,8,128]{2,1,0:T(8,128)}), f32[16,8,128]{2,1,0:T(8,128)S(1)}, u32[]{:S(2)}, u32[]{:S(2)}) async-start(f32[16,8,128]{2,1,0:T(8,128)} %get-tuple-element.20), calls=%async_computation.1 | async-start | bytes 131072 | tf_op jit(solution)/shard_map/all_to_all | solution.py:303
  174.6 0.6 copy-start.18

commit v2 on v1

v2 whole, which is shorter than its diff:
```python
import jax
import jax.numpy as jnp
from jax import lax
from jax.experimental import pallas as pl
from jax.experimental.pallas import tpu as pltpu
from jax.sharding import PartitionSpec as P


NR, NC = 16, 16
NZ = 8
ND = 400
LANES = 128
NJ, NAB = 16, 256
TA, TB = 50, 29
F32, BF16 = jnp.float32, jnp.bfloat16
LAST_OUT = pltpu.VMEM

VMEM = pl.BlockSpec(memory_space=pltpu.VMEM)


def params(mib):
    return pltpu.CompilerParams(vmem_limit_bytes=mib << 20)


def on_chip(x):
    return pltpu.with_memory_space_constraint(x, pltpu.VMEM)


def rows_of_rest(x, n):
    parts = [x(c) for c in range(n)]
    if n < 8:
        parts.append(jnp.zeros(parts[0].shape[:-1] + (LANES - 16 * n,), F32))
    return jnp.concatenate(parts, axis=-1)


def pack_t_kernel(row_ref, t_ref, a_ref, b_ref):
    for ref, at, c0, n in ((a_ref, 0, 0, 8), (a_ref, 25, 8, 8), (b_ref, 0, 16, 8), (b_ref, 25, 24, 1)):
        for c in range(n):
            for s in range(3):
                ref[at + 3 * c + s] = t_ref[c0 + c, :, LANES * s : LANES * (s + 1)]
        ref[at + 3 * n] = rows_of_rest(lambda c: t_ref[c0 + c, :, 384:400], n)


def pack_t(row, t):
    return pl.pallas_call(
        pack_t_kernel,
        in_specs=[pl.BlockSpec(memory_space=pltpu.SMEM), VMEM],
        out_specs=(VMEM, VMEM),
        out_shape=(pltpu.VMEM((TA, NJ, LANES), F32), pltpu.VMEM((TB, NJ, LANES), F32)),
        compiler_params=params(4),
        name="pack_t",
    )(row, t)


def split(x):
    hi = x.astype(BF16)
    return hi, (x - hi.astype(F32)).astype(BF16)


def pack_v_group(v_ref, h_ref, l_ref, at, n):
    for c in range(n):
        for s in range(3):
            t = at + 3 * c + s
            h_ref[t], l_ref[t] = split(v_ref[c, :, LANES * s : LANES * (s + 1)])
    t = at + 3 * n
    h_ref[t], l_ref[t] = split(rows_of_rest(lambda c: v_ref[c, :, 384:400], n))


def rows_64(at):
    return pl.ds(pl.multiple_of(at * 64, 64), 64)


def pack_va_kernel(v_ref, h_ref, l_ref):
    tiles, rows = pl.ds(pl.program_id(0) * 25, 25), rows_64(pl.program_id(1))
    pack_v_group(v_ref, h_ref.at[tiles, rows], l_ref.at[tiles, rows], 0, 8)


def pack_vb_kernel(v_ref, w_ref, h_ref, l_ref):
    rows = rows_64(pl.program_id(0))
    pack_v_group(v_ref, h_ref.at[:, rows], l_ref.at[:, rows], 0, 8)
    pack_v_group(w_ref, h_ref.at[:, rows], l_ref.at[:, rows], 25, 1)


def pack_va(v):
    out = pltpu.VMEM((TA, NAB, LANES), BF16)
    return pl.pallas_call(
        pack_va_kernel,
        grid=(2, 4),
        in_specs=[pl.BlockSpec((None, 8, 64, ND), lambda g, a: (a, g, 0, 0))],
        out_specs=(VMEM, VMEM),
        out_shape=(out, out),
        compiler_params=params(8),
        name="pack_va",
    )(v)


def pack_vb(v):
    out = pltpu.VMEM((TB, NAB, LANES), BF16)
    return pl.pallas_call(
        pack_vb_kernel,
        grid=(4,),
        in_specs=[
            pl.BlockSpec((None, 8, 64, ND), lambda a: (a, 2, 0, 0)),
            pl.BlockSpec((None, 1, 64, ND), lambda a: (a, 24, 0, 0)),
        ],
        out_specs=(VMEM, VMEM),
        out_shape=(out, out),
        compiler_params=params(8),
        name="pack_vb",
    )(v, v)


def product(t_refs, vh_ref, vl_ref, first, n):
    cat = lambda ref: jnp.concatenate([ref[first + t] for t in range(n)], axis=-1)
    hi, lo = split(jnp.concatenate([cat(r) for r in t_refs], axis=0))
    vh, vl = cat(vh_ref), cat(vl_ref)
    dims = (((1,), (1,)), ((), ()))
    both = lax.dot_general(jnp.concatenate([hi, lo], axis=0), vh, dims, preferred_element_type=F32)
    m = hi.shape[0]
    return both[:m] + both[m:] + lax.dot_general(hi, vl, dims, preferred_element_type=F32)


def product_b(refs, vh, vl):
    total = product(refs, vh, vl, 0, 6)
    for first, n in ((6, 6), (12, 6), (18, 6), (24, 5)):
        total += product(refs, vh, vl, first, n)
    return total


def dot_a_kernel(*refs):
    *t_refs, vh, vl, out = refs
    step = lambda g: product(t_refs, vh, vl, g * 10, 10)
    out[...] = lax.fori_loop(1, TA // 10, lambda g, total: total + step(g), step(0))


def dot(kernel, blocks, vh, vl):
    args = [on_chip(x) for x in (*blocks, vh, vl)]
    return pl.pallas_call(
        kernel,
        in_specs=[VMEM] * len(args),
        out_specs=VMEM,
        out_shape=pltpu.VMEM((NJ * len(blocks), NAB), F32),
        compiler_params=params(8),
    )(*args)


def dot_b_kernel(*refs):
    *t_refs, vh, vl, out = refs
    out[...] = product_b(t_refs, vh, vl)


def absolute_row(row, dz, dy):
    return (((row >> 1) + dz) & (NZ - 1)) * 2 + ((row & 1) ^ dy)


def last_kernel(where, row_ref, *refs):
    *t_refs, vh, vl, pa1, pa2, pb, out, left, right = refs
    new = product_b(t_refs, vh, vl)
    row = row_ref[0]
    n_a, n_b = pa1.shape[0] // NJ, pb.shape[0] // NJ
    part = lambda x, q: x[NJ * q : NJ * (q + 1), :]
    for q, (dz, dy) in enumerate(where):
        block = part(pa1, q) if q < n_a else part(pa2, q - n_a)
        block += part(pb, q) if q < n_b else part(new, q - n_b)
        at = pl.ds(pl.multiple_of(absolute_row(row, dz, dy) * NJ, NJ), NJ)
        left[at, :] = block[:, :LANES]
        right[at, :] = block[:, LANES:]
    for k in range(NC):
        for ref, lanes in ((left, slice(0, LANES)), (right, slice(LANES, NAB))):
            out[k, :NJ, lanes] = ref[NJ * k : NJ * (k + 1), :]
            out[k, NJ:, lanes] = ref[pl.ds(k, NJ, stride=NJ), :]


def last(row, where, blocks, vh, vl, pa1, pa2, pb):
    args = [on_chip(x) for x in (*blocks, vh, vl, pa1, pa2, pb)]
    return pl.pallas_call(
        lambda *refs: last_kernel(where, *refs),
        in_specs=[pl.BlockSpec(memory_space=pltpu.SMEM)] + [VMEM] * len(args),
        out_specs=VMEM,
        out_shape=LAST_OUT((NC, 2 * NJ, NAB), F32),
        scratch_shapes=[pltpu.VMEM((NAB, LANES), F32)] * 2,
        compiler_params=params(8),
        name="last",
    )(row, *args)


def permute_lanes(x, source):
    lane = lax.broadcasted_iota(jnp.int32, (NAB, NAB), 1)
    one_hot = (lax.broadcasted_iota(jnp.int32, (NAB, NAB), 0) == source(lane)).astype(BF16)
    p1, r1 = x.astype(BF16), x - x.astype(BF16).astype(F32)
    p2 = r1.astype(BF16)
    p3 = (r1 - p2.astype(F32)).astype(BF16)
    y = jnp.dot(jnp.concatenate([p1, p2, p3], axis=0), one_hot, preferred_element_type=F32)
    m = x.shape[0]
    return y[:m] + y[m : 2 * m] + y[2 * m :]


def fold_kernel(r_ref, d_ref, e_ref):
    total = r_ref[0]
    for k in range(1, NC):
        total += r_ref[k]
    d_ref[...] = total[:NJ]
    mixed = permute_lanes(total[NJ:], lambda n: ((n >> 2) & 3) * 64 + (n >> 4) * 4 + (n & 3))
    zeros = jnp.zeros((8, LANES - 32), F32)
    for r in range(NR):
        lanes = slice(16 * r, 16 * (r + 1))
        e_ref[r] = jnp.concatenate([mixed[:8, lanes], mixed[8:, lanes], zeros], axis=-1)


def fold(r):
    return pl.pallas_call(
        fold_kernel,
        in_specs=[VMEM],
        out_specs=(VMEM, VMEM),
        out_shape=(pltpu.VMEM((NJ, NAB), F32), LAST_OUT((NR, 8, LANES), F32)),
        compiler_params=params(4),
        name="fold",
    )(on_chip(r))


def finish_kernel(d_ref, m_ref, rest_ref, den_ref, out_ref):
    halves = [
        jnp.concatenate([m_ref[r, :, 16 * h : 16 * (h + 1)] for r in range(NR)], axis=-1)
        for h in range(2)
    ]
    mirror = permute_lanes(
        jnp.concatenate(halves, axis=0), lambda n: ((n >> 2) & 15) * 16 + (n & 3) * 4 + (n >> 6)
    )
    value = (d_ref[...] + mirror + rest_ref[...]) / den_ref[...]
    for a in range(4):
        out_ref[:, a, :] = value[:, 64 * a : 64 * (a + 1)]


def finish(d, m, rest, den):
    args = [on_chip(x) for x in (d, m, rest, den)]
    return pl.pallas_call(
        finish_kernel,
        in_specs=[VMEM] * 4,
        out_specs=VMEM,
        out_shape=jax.ShapeDtypeStruct((NJ, 4, 64), F32),
        compiler_params=params(4),
        name="finish",
    )(*args)


AXES = ("row", "col")


def moves(dz=0, dy=0):
    pairs = []
    for z in range(NZ):
        for h in range(2):
            for k in range(NC):
                to = ((z + dz) % NZ * 2 + (h ^ dy)) * NC + k
                pairs.append(((z * 2 + h) * NC + k, to))
    return pairs


UP, DOWN, ACROSS = moves(dz=1), moves(dz=-1), moves(dy=1)


def send(x, where):
    return lax.ppermute(x, AXES, where)


def on_device(amplitudes, integrals, rest, occ_energy, vir_energy):
    row = lax.axis_index("row")
    col = lax.axis_index("col")
    row_1 = row.reshape(1)
    a0, b0 = pack_t(row_1, jnp.transpose(amplitudes, (0, 2, 1, 3))[0])
    v = jnp.transpose(integrals, (0, 2, 1, 3))
    v = pltpu.with_memory_space_constraint(v, pltpu.HBM)
    vah, val = pack_va(v)
    vbh, vbl = pack_vb(v)

    au, ad, yu, yd = [a0], [a0], [send(a0, ACROSS)], [None]
    bx = send(b0, ACROSS)
    bu, bd, cu, cd = [b0], [b0], [bx], [bx]
    for _ in range(3):
        for chain, way in (
            (au, UP), (ad, DOWN), (bu, UP), (bd, DOWN),
            (cu, UP), (cd, DOWN),
        ):
            chain.append(send(chain[-1], way))
        yu.append(send(au[-1], ACROSS))
        yd.append(send(ad[-1], ACROSS))
    a4 = send(au[3], UP)
    a4x = send(yd[3], DOWN)
    b4 = send(bu[3], UP)
    c4 = send(cd[3], DOWN)

    a_all, b_all, where = [a0, yu[0]], [b0, bx], [(0, 0), (0, 1)]
    for s in (1, 2, 3):
        a_all += [au[s], yu[s], ad[s], yd[s]]
        b_all += [bu[s], cu[s], bd[s], cd[s]]
        where += [(-s, 0), (-s, 1), (s, 0), (s, 1)]
    a_all += [a4, a4x]
    b_all += [b4, c4]
    where += [(4, 0), (4, 1)]
    pa1 = dot(dot_a_kernel, a_all[:N_A], vah, val)
    pa2 = dot(dot_a_kernel, a_all[N_A:], vah, val)
    pb = dot(dot_b_kernel, b_all[:N_B], vbh, vbl)
    partial = last(row_1, where, b_all[N_B:], vbh, vbl, pa1, pa2, pb)

    received = lax.all_to_all(partial, "col", 0, 0, tiled=True)
    direct, messages = fold(received)
    mirror = lax.all_to_all(messages, "row", 0, 0, tiled=True)

    vir_local = lax.dynamic_slice_in_dim(vir_energy, row * 4, 4, 0)
    occ_local = lax.dynamic_slice_in_dim(occ_energy, col, 1, 0)
    den = (
        vir_local[None, :, None] + vir_energy[None, None, :] - occ_local[:, None, None]
        - occ_energy[:, None, None]
    )
    out = finish(direct, mirror, rest.reshape(NJ, NAB), den.reshape(NJ, NAB))
    return out[None]


N_A, N_B = 14, 10


def solution(mesh):
    in_specs = (
        P("row", None, "col", None),
        P("row", None, "col", None),
        P("col", None, "row", None),
        P(),
        P(),
    )

    return jax.shard_map(
        on_device, mesh=mesh, in_specs=in_specs, out_specs=P("col", None, "row", None), check_vma=False
    )
```

time: 178 us -> 157 us (0.88)
  waiting for transfers between devices: 58 us -> 89.4 us
  starting transfers between devices: 68.6 us -> 43.7 us
  Pallas kernels: 43.2 us -> 20.8 us
  local copies, waits for them, and re-layouts: 4.59 us -> 2.17 us
    ppermute x24 -> x30, waiting for transfers between devices: 41.8 us -> 72 us  [send(): return lax.ppermute(x, AXES, where)]
    pallas_call x7, Pallas kernels: 29.5 us -> 11.5 us  [the longest x3 7.32 us: dot(): pl.pallas_call(kernel, in_specs=[VMEM] * len(args), out_specs=VMEM, out_s...]
    ppermute x24 -> x30, starting transfers between devices: 46.1 us -> 29.4 us  [send(): return lax.ppermute(x, AXES, where)]
    all_to_all x1, starting transfers between devices: 15.2 us -> 10 us  [on_device(): received = lax.all_to_all(partial, 'col', 0, 0, tiled=True)]
    all_to_all x1, starting transfers between devices: 7.37 us -> 4.29 us  [on_device(): mirror = lax.all_to_all(messages, 'row', 0, 0, tiled=True)]
    pallas_call x1, Pallas kernels: 8.8 us -> 6.07 us  [pack_va(): pl.pallas_call(pack_va_kernel, grid=(2, 4), in_specs=[pl.BlockSpec((None,...]
  transfers between devices with their start and end apart: 26 -> 32, of which waited for: 11 -> 15; matrix products, arithmetic and copies ran while one was open for 2% -> 1% of each run, Pallas kernels for 18% -> 11%
where the time goes in v2:
time: 157 us
  waiting for transfers between devices  89.4 us (57%)
  starting transfers between devices  43.7 us (28%)
  Pallas kernels  20.8 us (13%)
  local copies, waits for them, and re-layouts  2.17 us (1%)
    ppermute x30, waiting for transfers between devices, send(): return lax.ppermute(x, AXES, where)  72 us
    ppermute x30, starting transfers between devices, send(): return lax.ppermute(x, AXES, where)  29.4 us
    all_to_all x1, starting transfers between devices, on_device(): received = lax.all_to_all(partial, 'col', 0, 0, tiled=True)  10 us
    all_to_all x1, waiting for transfers between devices, on_device(): mirror = lax.all_to_all(messages, 'row', 0, 0, tiled=True)  9.37 us
    all_to_all x1, waiting for transfers between devices, on_device(): received = lax.all_to_all(partial, 'col', 0, 0, tiled=True)  8.02 us
    pallas_call x3, Pallas kernels, dot(): pl.pallas_call(kernel, in_specs=[VMEM] * len(args), out_specs=VMEM, out_s...  7.32 us
    pallas_call x1, Pallas kernels, pack_va(): pl.pallas_call(pack_va_kernel, grid=(2, 4), in_specs=[pl.BlockSpec((None,...  6.07 us
    all_to_all x1, starting transfers between devices, on_device(): mirror = lax.all_to_all(messages, 'row', 0, 0, tiled=True)  4.29 us
  transfers between devices with their start and end apart: 32, of which 15 were waited for; matrix products, arithmetic and copies ran while one was open for 1% of the time, Pallas kernels for 11%

profile of v2, /device:TPU:1, one launch (start us, length us, event | category | flops | bytes accessed | tf_op | source)
XLA Modules:
  0.0 156.9 jit_solution(16777172993955896165)
XLA Ops:
  0.0 1.1 copy-done
  1.1 0.1 pack_t.1
  1.3 6.5 %collective-permute-start.18 = (f32[50,16,128]{2,1,0:T(8,128)S(1)}, f32[50,16,128]{2,1,0:T(8,128)S(1)}, u32[]{:S(2)}, u32[]{:S(2)}) collective-permute-start(f32[50,16,128]{2,1,0:T(8,128)S(1)} %get-tuple-element.16.refs_0_), channel_id=1, source_target_pairs={{0,224},{1,225},{2,226},{3,227},{4,228},{5,229},{6,230},{7,231},{8... | collective-permute-start | bytes 1228808 | tf_op jit(solution)/shard_map/ppermute | solution.py:263
  7.7 2.9 %collective-permute-start.3 = (f32[29,16,128]{2,1,0:T(8,128)S(1)}, f32[29,16,128]{2,1,0:T(8,128)S(1)}, u32[]{:S(2)}, u32[]{:S(2)}) collective-permute-start(f32[29,16,128]{2,1,0:T(8,128)S(1)} %get-tuple-element.13.refs_0_), channel_id=1, source_target_pairs={{0,16},{1,17},{2,18},{3,19},{4,20},{5,21},{6,22},{7,23},{8,24},{9,... | collective-permute-start | bytes 712712 | tf_op jit(solution)/shard_map/ppermute | solution.py:263
  10.6 0.1 collective-permute-start.15
  10.7 0.0 collective-permute-start
  10.7 4.9 %collective-permute-done.3.refs_1_ = f32[29,16,128]{2,1,0:T(8,128)S(1)} collective-permute-done((f32[29,16,128]{2,1,0:T(8,128)S(1)}, f32[29,16,128]{2,1,0:T(8,128)S(1)}, u32[]{:S(2)}, u32[]{:S(2)}) %collective-permute-start.3) | collective-permute-done | bytes 237600 | tf_op jit(solution)/shard_map/ppermute | solution.py:263
  15.6 0.7 collective-permute-start.7
  16.4 2.9 %collective-permute-start.22 = (f32[50,16,128]{2,1,0:T(8,128)S(1)}, f32[50,16,128]{2,1,0:T(8,128)S(1)}, u32[]{:S(2)}, u32[]{:S(2)}) collective-permute-start(f32[50,16,128]{2,1,0:T(8,128)S(1)} %collective-permute-done.18.refs_4_), channel_id=1, source_target_pairs={{0,224},{1,225},{2,226},{3,227},{4,228},{5,229},{6,230},{7,231},{8... | collective-permute-start | bytes 1228808 | tf_op jit(solution)/shard_map/ppermute | solution.py:263
  19.3 7.4 %collective-permute-done.refs_2_ = f32[29,16,128]{2,1,0:T(8,128)S(1)} collective-permute-done((f32[29,16,128]{2,1,0:T(8,128)S(1)}, f32[29,16,128]{2,1,0:T(8,128)S(1)}, u32[]{:S(2)}, u32[]{:S(2)}) %collective-permute-start) | collective-permute-done | bytes 237600 | tf_op jit(solution)/shard_map/ppermute | solution.py:263
  26.7 0.0 collective-permute-done.7.refs_4_
  26.7 1.5 collective-permute-start.4
  28.2 0.1 collective-permute-start.1
  28.3 0.0 collective-permute-done.15.refs_1_
  28.3 0.1 collective-permute-start.20
  28.4 6.1 %collective-permute-done.10.refs_5_ = f32[29,16,128]{2,1,0:T(8,128)S(1)} collective-permute-done((f32[29,16,128]{2,1,0:T(8,128)S(1)}, f32[29,16,128]{2,1,0:T(8,128)S(1)}, u32[]{:S(2)}, u32[]{:S(2)}) %collective-permute-start.10) | collective-permute-done | bytes 237600 | tf_op jit(solution)/shard_map/ppermute | solution.py:263
  34.5 2.6 %collective-permute-start.8 = (f32[29,16,128]{2,1,0:T(8,128)S(1)}, f32[29,16,128]{2,1,0:T(8,128)S(1)}, u32[]{:S(2)}, u32[]{:S(2)}) collective-permute-start(f32[29,16,128]{2,1,0:T(8,128)S(1)} %collective-permute-done.7.refs_4_), channel_id=1, source_target_pairs={{0,224},{1,225},{2,226},{3,227},{4,228},{5,229},{6,230},{7,231},{8... | collective-permute-start | bytes 712712 | tf_op jit(solution)/shard_map/ppermute | solution.py:263
  37.1 0.0 collective-permute-start.11
  37.1 1.2 collective-permute-done.1.refs_6_
  38.3 0.3 collective-permute-start.5
  38.6 0.0 collective-permute-done.22.refs_8_
  38.6 2.4 %collective-permute-start.26 = (f32[50,16,128]{2,1,0:T(8,128)S(1)}, f32[50,16,128]{2,1,0:T(8,128)S(1)}, u32[]{:S(2)}, u32[]{:S(2)}) collective-permute-start(f32[50,16,128]{2,1,0:T(8,128)S(1)} %collective-permute-done.22.refs_8_), channel_id=1, source_target_pairs={{0,224},{1,225},{2,226},{3,227},{4,228},{5,229},{6,230},{7,231},{8... | collective-permute-start | bytes 1228808 | tf_op jit(solution)/shard_map/ppermute | solution.py:263
  41.0 0.0 collective-permute-done.8.refs_8_
  41.0 3.5 %collective-permute-done.11.refs_9_ = f32[29,16,128]{2,1,0:T(8,128)S(1)} collective-permute-done((f32[29,16,128]{2,1,0:T(8,128)S(1)}, f32[29,16,128]{2,1,0:T(8,128)S(1)}, u32[]{:S(2)}, u32[]{:S(2)}) %collective-permute-start.11) | collective-permute-done | bytes 237600 | tf_op jit(solution)/shard_map/ppermute | solution.py:263
  44.4 1.4 collective-permute-start.17
  45.8 6.3 %collective-permute-done.5.refs_7_ = f32[29,16,128]{2,1,0:T(8,128)S(1)} collective-permute-done((f32[29,16,128]{2,1,0:T(8,128)S(1)}, f32[29,16,128]{2,1,0:T(8,128)S(1)}, u32[]{:S(2)}, u32[]{:S(2)}) %collective-permute-start.5) | collective-permute-done | bytes 237600 | tf_op jit(solution)/shard_map/ppermute | solution.py:263
  52.2 0.0 collective-permute-start.24
  52.2 5.1 %collective-permute-done.2.refs_1_ = f32[29,16,128]{2,1,0:T(8,128)S(1)} collective-permute-done((f32[29,16,128]{2,1,0:T(8,128)S(1)}, f32[29,16,128]{2,1,0:T(8,128)S(1)}, u32[]{:S(2)}, u32[]{:S(2)}) %collective-permute-start.2) | collective-permute-done | bytes 237600 | tf_op jit(solution)/shard_map/ppermute | solution.py:263
  57.3 0.6 collective-permute-start.27
  57.8 2.4 %collective-permute-start.21 = (f32[50,16,128]{2,1,0:T(8,128)S(1)}, f32[50,16,128]{2,1,0:T(8,128)S(1)}, u32[]{:S(2)}, u32[]{:S(2)}) collective-permute-start(f32[50,16,128]{2,1,0:T(8,128)S(1)} %collective-permute-done.20.refs_6_), channel_id=1, source_target_pairs={{0,16},{1,17},{2,18},{3,19},{4,20},{5,21},{6,22},{7,23},{8,24},{9,... | collective-permute-start | bytes 1228808 | tf_op jit(solution)/shard_map/ppermute | solution.py:263
  60.2 4.7 %collective-permute-done.19.refs_5_ = f32[50,16,128]{2,1,0:T(8,128)S(1)} collective-permute-done((f32[50,16,128]{2,1,0:T(8,128)S(1)}, f32[50,16,128]{2,1,0:T(8,128)S(1)}, u32[]{:S(2)}, u32[]{:S(2)}) %collective-permute-start.19) | collective-permute-done | bytes 409632 | tf_op jit(solution)/shard_map/ppermute | solution.py:263
  64.9 1.1 collective-permute-done.24.refs_10_
  66.0 1.9 %collective-permute-start.25 = (f32[50,16,128]{2,1,0:T(8,128)S(1)}, f32[50,16,128]{2,1,0:T(8,128)S(1)}, u32[]{:S(2)}, u32[]{:S(2)}) collective-permute-start(f32[50,16,128]{2,1,0:T(8,128)S(1)} %collective-permute-done.24.refs_10_), channel_id=1, source_target_pairs={{0,16},{1,17},{2,18},{3,19},{4,20},{5,21},{6,22},{7,23},{8,24},{9,... | collective-permute-start | bytes 1228808 | tf_op jit(solution)/shard_map/ppermute | solution.py:263
  67.9 0.2 collective-permute-start.28
  68.1 5.6 %collective-permute-done.27.refs_13_ = f32[50,16,128]{2,1,0:T(8,128)S(1)} collective-permute-done((f32[50,16,128]{2,1,0:T(8,128)S(1)}, f32[50,16,128]{2,1,0:T(8,128)S(1)}, u32[]{:S(2)}, u32[]{:S(2)}) %collective-permute-start.27) | collective-permute-done | bytes 409632 | tf_op jit(solution)/shard_map/ppermute | solution.py:263
  73.7 8.8 %collective-permute-done.21.refs_7_ = f32[50,16,128]{2,1,0:T(8,128)S(1)} collective-permute-done((f32[50,16,128]{2,1,0:T(8,128)S(1)}, f32[50,16,128]{2,1,0:T(8,128)S(1)}, u32[]{:S(2)}, u32[]{:S(2)}) %collective-permute-start.21) | collective-permute-done | bytes 409632 | tf_op jit(solution)/shard_map/ppermute | solution.py:263
  82.5 8.8 %collective-permute-done.23.refs_9_ = f32[50,16,128]{2,1,0:T(8,128)S(1)} collective-permute-done((f32[50,16,128]{2,1,0:T(8,128)S(1)}, f32[50,16,128]{2,1,0:T(8,128)S(1)}, u32[]{:S(2)}, u32[]{:S(2)}) %collective-permute-start.23) | collective-permute-done | bytes 409632 | tf_op jit(solution)/shard_map/ppermute | solution.py:263
  91.2 0.2 collective-permute-start.6
  91.4 8.6 %collective-permute-done.25.refs_11_ = f32[50,16,128]{2,1,0:T(8,128)S(1)} collective-permute-done((f32[50,16,128]{2,1,0:T(8,128)S(1)}, f32[50,16,128]{2,1,0:T(8,128)S(1)}, u32[]{:S(2)}, u32[]{:S(2)}) %collective-permute-start.25) | collective-permute-done | bytes 409632 | tf_op jit(solution)/shard_map/ppermute | solution.py:263
  100.0 0.2 collective-permute-start.13
  100.2 2.5 %collective-permute-start.14 = (f32[29,16,128]{2,1,0:T(8,128)S(1)}, f32[29,16,128]{2,1,0:T(8,128)S(1)}, u32[]{:S(2)}, u32[]{:S(2)}) collective-permute-start(f32[29,16,128]{2,1,0:T(8,128)S(1)} %collective-permute-done.12.refs_4_), channel_id=1, source_target_pairs={{0,224},{1,225},{2,226},{3,227},{4,228},{5,229},{6,230},{7,231},{8... | collective-permute-start | bytes 712712 | tf_op jit(solution)/shard_map/ppermute | solution.py:263
  102.7 6.1 %pack_va.1 = (bf16[50,256,128]{2,1,0:T(8,128)(2,1)S(1)}, bf16[50,256,128]{2,1,0:T(8,128)(2,1)S(1)}) custom-call(f32[4,25,64,400]{3,2,1,0:T(8,128)} %bitcast.8), custom_call_target="tpu_custom_call" | custom-call | tf_op jit(solution)/shard_map/pack_va/pallas_call | solution.py:86
  108.8 3.2 %pack_vb.1 = (bf16[29,256,128]{2,1,0:T(8,128)(2,1)S(1)}, bf16[29,256,128]{2,1,0:T(8,128)(2,1)S(1)}) custom-call(f32[4,25,64,400]{3,2,1,0:T(8,128)} %bitcast.9, f32[4,25,64,400]{3,2,1,0:T(8,128)} %bitcast.10), custom_call_target="tpu_custom_call" | custom-call | tf_op jit(solution)/shard_map/pack_vb/pallas_call | solution.py:99
  112.0 1.4 shard_map.57.refs_11_
  113.4 3.4 %shard_map.55.refs_9_ = f32[224,256]{1,0:T(8,128)S(1)} custom-call(f32[50,16,128]{2,1,0:T(8,128)S(1)} %get-tuple-element.16.refs_0_, f32[50,16,128]{2,1,0:T(8,128)S(1)} %collective-permute-done.15.refs_1_, f32[50,16,128]{2,1,0:T(8,128)S(1)} %collective-permute-done.16.refs_2_, f32[50,16,128]{2,1,0:T(8,128)S(1)} %collective-permute-done.17.refs_3_, ...), custom_call_target="tpu_custom_call" | custom-call | tf_op jit(solution)/shard_map/pallas_call | solution.py:138
  116.9 2.5 %shard_map.56.refs_10_ = f32[32,256]{1,0:T(8,128)S(1)} custom-call(f32[50,16,128]{2,1,0:T(8,128)S(1)} %collective-permute-done.28.refs_0_, f32[50,16,128]{2,1,0:T(8,128)S(1)} %collective-permute-done.29.refs_1_, bf16[50,256,128]{2,1,0:T(8,128)(2,1)S(1)} %get-tuple-element.17.refs_14_.refs_2_, bf16[50,256,128]{2,1,0:T(8,128)(2,1)S(1)} %get-tuple-element.18.refs_15_.refs_3_), custom_call_target="tpu_custom_call" | custom-call | tf_op jit(solution)/shard_map/pallas_call | solution.py:138
  119.4 0.0 copy-start.2
  119.4 0.0 copy-start.1
  119.4 0.0 copy-start.3
  119.5 2.2 %last.1 = f32[16,32,256]{2,1,0:T(8,128)} custom-call(s32[1]{0:T(128)} %bitcast.row_ref.refs_0_, f32[29,16,128]{2,1,0:T(8,128)S(1)} %collective-permute-done.2.refs_1_, f32[29,16,128]{2,1,0:T(8,128)S(1)} %collective-permute-done.6.refs_2_, f32[29,16,128]{2,1,0:T(8,128)S(1)} %collective-permute-done.9.refs_3_, ...), custom_call_target="tpu_custom_call" | custom-call | tf_op jit(solution)/shard_map/last/pallas_call | solution.py:176
  121.7 10.0 %all-to-all-start = ((f32[16,32,256]{2,1,0:T(8,128)}), f32[16,32,256]{2,1,0:T(8,128)S(1)}, u32[]{:S(2)}, u32[]{:S(2)}) async-start(f32[16,32,256]{2,1,0:T(8,128)} %last.1), calls=%async_computation | async-start | bytes 1048576 | tf_op jit(solution)/shard_map/all_to_all | solution.py:305
  131.7 0.1 dynamic_slice.6
  131.8 0.1 broadcast_reduce_fusion
  131.8 0.1 add.30
  131.9 0.1 add.32
  132.0 0.1 reshape.44.rest_ref
  132.1 0.6 dynamic_slice.7
  132.7 0.6 add_subtract_fusion
  133.3 8.0 %all-to-all-done.r_ref = f32[16,32,256]{2,1,0:T(8,128)S(1)} async-done(((f32[16,32,256]{2,1,0:T(8,128)}), f32[16,32,256]{2,1,0:T(8,128)S(1)}, u32[]{:S(2)}, u32[]{:S(2)}) %all-to-all-start) | async-done | bytes 524320 | tf_op jit(solution)/shard_map/all_to_all | solution.py:305
  141.4 0.9 fold.1
  142.2 4.3 %all-to-all-start.1 = ((f32[16,8,128]{2,1,0:T(8,128)}), f32[16,8,128]{2,1,0:T(8,128)S(1)}, u32[]{:S(2)}, u32[]{:S(2)}) async-start(f32[16,8,128]{2,1,0:T(8,128)} %get-tuple-element.20), calls=%async_computation.1 | async-start | bytes 131072 | tf_op jit(solution)/shard_map/all_to_all | solution.py:307
  146.5 0.1 broadcast_subtract_fusion.den_ref
  146.6 9.4 %all-to-all-done.1.m_ref = f32[16,8,128]{2,1,0:T(8,128)S(1)} async-done(((f32[16,8,128]{2,1,0:T(8,128)}), f32[16,8,128]{2,1,0:T(8,128)S(1)}, u32[]{:S(2)}, u32[]{:S(2)}) %all-to-all-start.1) | async-done | bytes 65568 | tf_op jit(solution)/shard_map/all_to_all | solution.py:307
  156.0 0.9 finish.1
  (26 shorter events, 0.1 us)
Async XLA Ops:
  0.0 1.1 copy-start
  1.3 15.1 %collective-permute-start.18 = (f32[50,16,128]{2,1,0:T(8,128)S(1)}, f32[50,16,128]{2,1,0:T(8,128)S(1)}, u32[]{:S(2)}, u32[]{:S(2)}) collective-permute-start(f32[50,16,128]{2,1,0:T(8,128)S(1)} %get-tuple-element.16.refs_0_), channel_id=1, source_target_pairs={{0,224},{1,225},{2,226},{3,227},{4,228},{5,229},{6,230},{7,231},{8... | collective-permute-start | bytes 1228808 | tf_op jit(solution)/shard_map/ppermute | solution.py:263
  7.7 7.9 %collective-permute-start.3 = (f32[29,16,128]{2,1,0:T(8,128)S(1)}, f32[29,16,128]{2,1,0:T(8,128)S(1)}, u32[]{:S(2)}, u32[]{:S(2)}) collective-permute-start(f32[29,16,128]{2,1,0:T(8,128)S(1)} %get-tuple-element.13.refs_0_), channel_id=1, source_target_pairs={{0,16},{1,17},{2,18},{3,19},{4,20},{5,21},{6,22},{7,23},{8,24},{9,... | collective-permute-start | bytes 712712 | tf_op jit(solution)/shard_map/ppermute | solution.py:263
  10.6 17.6 %collective-permute-start.16 = (f32[50,16,128]{2,1,0:T(8,128)S(1)}, f32[50,16,128]{2,1,0:T(8,128)S(1)}, u32[]{:S(2)}, u32[]{:S(2)}) collective-permute-start(f32[50,16,128]{2,1,0:T(8,128)S(1)} %get-tuple-element.16.refs_0_), channel_id=1, source_target_pairs={{0,32},{1,33},{2,34},{3,35},{4,36},{5,37},{6,38},{7,39},{8,40},{9,... | collective-permute-start | bytes 1228808 | tf_op jit(solution)/shard_map/ppermute | solution.py:263
  10.6 17.6 %collective-permute-start.15 = (f32[50,16,128]{2,1,0:T(8,128)S(1)}, f32[50,16,128]{2,1,0:T(8,128)S(1)}, u32[]{:S(2)}, u32[]{:S(2)}) collective-permute-start(f32[50,16,128]{2,1,0:T(8,128)S(1)} %get-tuple-element.16.refs_0_), channel_id=1, source_target_pairs={{0,16},{1,17},{2,18},{3,19},{4,20},{5,21},{6,22},{7,23},{8,24},{9,... | collective-permute-start | bytes 1228808 | tf_op jit(solution)/shard_map/ppermute | solution.py:263
  10.7 16.0 %collective-permute-start = (f32[29,16,128]{2,1,0:T(8,128)S(1)}, f32[29,16,128]{2,1,0:T(8,128)S(1)}, u32[]{:S(2)}, u32[]{:S(2)}) collective-permute-start(f32[29,16,128]{2,1,0:T(8,128)S(1)} %get-tuple-element.13.refs_0_), channel_id=1, source_target_pairs={{0,32},{1,33},{2,34},{3,35},{4,36},{5,37},{6,38},{7,39},{8,40},{9,... | collective-permute-start | bytes 712712 | tf_op jit(solution)/shard_map/ppermute | solution.py:263
  15.6 11.1 %collective-permute-start.7 = (f32[29,16,128]{2,1,0:T(8,128)S(1)}, f32[29,16,128]{2,1,0:T(8,128)S(1)}, u32[]{:S(2)}, u32[]{:S(2)}) collective-permute-start(f32[29,16,128]{2,1,0:T(8,128)S(1)} %get-tuple-element.13.refs_0_), channel_id=1, source_target_pairs={{0,224},{1,225},{2,226},{3,227},{4,228},{5,229},{6,230},{7,231},{8... | collective-permute-start | bytes 712712 | tf_op jit(solution)/shard_map/ppermute | solution.py:263
  16.4 22.2 %collective-permute-start.22 = (f32[50,16,128]{2,1,0:T(8,128)S(1)}, f32[50,16,128]{2,1,0:T(8,128)S(1)}, u32[]{:S(2)}, u32[]{:S(2)}) collective-permute-start(f32[50,16,128]{2,1,0:T(8,128)S(1)} %collective-permute-done.18.refs_4_), channel_id=1, source_target_pairs={{0,224},{1,225},{2,226},{3,227},{4,228},{5,229},{6,230},{7,231},{8... | collective-permute-start | bytes 1228808 | tf_op jit(solution)/shard_map/ppermute | solution.py:263
  26.7 7.8 %collective-permute-start.10 = (f32[29,16,128]{2,1,0:T(8,128)S(1)}, f32[29,16,128]{2,1,0:T(8,128)S(1)}, u32[]{:S(2)}, u32[]{:S(2)}) collective-permute-start(f32[29,16,128]{2,1,0:T(8,128)S(1)} %collective-permute-done.3.refs_1_), channel_id=1, source_target_pairs={{0,224},{1,225},{2,226},{3,227},{4,228},{5,229},{6,230},{7,231},{8... | collective-permute-start | bytes 712712 | tf_op jit(solution)/shard_map/ppermute | solution.py:263
  26.7 10.3 %collective-permute-start.4 = (f32[29,16,128]{2,1,0:T(8,128)S(1)}, f32[29,16,128]{2,1,0:T(8,128)S(1)}, u32[]{:S(2)}, u32[]{:S(2)}) collective-permute-start(f32[29,16,128]{2,1,0:T(8,128)S(1)} %collective-permute-done.3.refs_1_), channel_id=1, source_target_pairs={{0,32},{1,33},{2,34},{3,35},{4,36},{5,37},{6,38},{7,39},{8,40},{9,... | collective-permute-start | bytes 712712 | tf_op jit(solution)/shard_map/ppermute | solution.py:263
  28.2 10.1 %collective-permute-start.1 = (f32[29,16,128]{2,1,0:T(8,128)S(1)}, f32[29,16,128]{2,1,0:T(8,128)S(1)}, u32[]{:S(2)}, u32[]{:S(2)}) collective-permute-start(f32[29,16,128]{2,1,0:T(8,128)S(1)} %collective-permute-done.refs_2_), channel_id=1, source_target_pairs={{0,32},{1,33},{2,34},{3,35},{4,36},{5,37},{6,38},{7,39},{8,40},{9,... | collective-permute-start | bytes 712712 | tf_op jit(solution)/shard_map/ppermute | solution.py:263
  28.3 23.9 %collective-permute-start.20 = (f32[50,16,128]{2,1,0:T(8,128)S(1)}, f32[50,16,128]{2,1,0:T(8,128)S(1)}, u32[]{:S(2)}, u32[]{:S(2)}) collective-permute-start(f32[50,16,128]{2,1,0:T(8,128)S(1)} %collective-permute-done.16.refs_2_), channel_id=1, source_target_pairs={{0,32},{1,33},{2,34},{3,35},{4,36},{5,37},{6,38},{7,39},{8,40},{9,... | collective-permute-start | bytes 1228808 | tf_op jit(solution)/shard_map/ppermute | solution.py:263
  34.5 6.4 %collective-permute-start.8 = (f32[29,16,128]{2,1,0:T(8,128)S(1)}, f32[29,16,128]{2,1,0:T(8,128)S(1)}, u32[]{:S(2)}, u32[]{:S(2)}) collective-permute-start(f32[29,16,128]{2,1,0:T(8,128)S(1)} %collective-permute-done.7.refs_4_), channel_id=1, source_target_pairs={{0,224},{1,225},{2,226},{3,227},{4,228},{5,229},{6,230},{7,231},{8... | collective-permute-start | bytes 712712 | tf_op jit(solution)/shard_map/ppermute | solution.py:263
  37.1 7.3 %collective-permute-start.11 = (f32[29,16,128]{2,1,0:T(8,128)S(1)}, f32[29,16,128]{2,1,0:T(8,128)S(1)}, u32[]{:S(2)}, u32[]{:S(2)}) collective-permute-start(f32[29,16,128]{2,1,0:T(8,128)S(1)} %collective-permute-done.10.refs_5_), channel_id=1, source_target_pairs={{0,224},{1,225},{2,226},{3,227},{4,228},{5,229},{6,230},{7,231},{8... | collective-permute-start | bytes 712712 | tf_op jit(solution)/shard_map/ppermute | solution.py:263
  38.3 13.9 %collective-permute-start.5 = (f32[29,16,128]{2,1,0:T(8,128)S(1)}, f32[29,16,128]{2,1,0:T(8,128)S(1)}, u32[]{:S(2)}, u32[]{:S(2)}) collective-permute-start(f32[29,16,128]{2,1,0:T(8,128)S(1)} %collective-permute-done.4.refs_3_), channel_id=1, source_target_pairs={{0,32},{1,33},{2,34},{3,35},{4,36},{5,37},{6,38},{7,39},{8,40},{9,... | collective-permute-start | bytes 712712 | tf_op jit(solution)/shard_map/ppermute | solution.py:263
  38.6 18.7 %collective-permute-start.26 = (f32[50,16,128]{2,1,0:T(8,128)S(1)}, f32[50,16,128]{2,1,0:T(8,128)S(1)}, u32[]{:S(2)}, u32[]{:S(2)}) collective-permute-start(f32[50,16,128]{2,1,0:T(8,128)S(1)} %collective-permute-done.22.refs_8_), channel_id=1, source_target_pairs={{0,224},{1,225},{2,226},{3,227},{4,228},{5,229},{6,230},{7,231},{8... | collective-permute-start | bytes 1228808 | tf_op jit(solution)/shard_map/ppermute | solution.py:263
  41.0 16.3 %collective-permute-start.2 = (f32[29,16,128]{2,1,0:T(8,128)S(1)}, f32[29,16,128]{2,1,0:T(8,128)S(1)}, u32[]{:S(2)}, u32[]{:S(2)}) collective-permute-start(f32[29,16,128]{2,1,0:T(8,128)S(1)} %collective-permute-done.1.refs_6_), channel_id=1, source_target_pairs={{0,32},{1,33},{2,34},{3,35},{4,36},{5,37},{6,38},{7,39},{8,40},{9,... | collective-permute-start | bytes 712712 | tf_op jit(solution)/shard_map/ppermute | solution.py:263
  44.4 13.4 %collective-permute-start.17 = (f32[50,16,128]{2,1,0:T(8,128)S(1)}, f32[50,16,128]{2,1,0:T(8,128)S(1)}, u32[]{:S(2)}, u32[]{:S(2)}) collective-permute-start(f32[50,16,128]{2,1,0:T(8,128)S(1)} %collective-permute-done.16.refs_2_), channel_id=1, source_target_pairs={{0,16},{1,17},{2,18},{3,19},{4,20},{5,21},{6,22},{7,23},{8,24},{9,... | collective-permute-start | bytes 1228808 | tf_op jit(solution)/shard_map/ppermute | solution.py:263
  52.2 12.8 %collective-permute-start.19 = (f32[50,16,128]{2,1,0:T(8,128)S(1)}, f32[50,16,128]{2,1,0:T(8,128)S(1)}, u32[]{:S(2)}, u32[]{:S(2)}) collective-permute-start(f32[50,16,128]{2,1,0:T(8,128)S(1)} %collective-permute-done.18.refs_4_), channel_id=1, source_target_pairs={{0,16},{1,17},{2,18},{3,19},{4,20},{5,21},{6,22},{7,23},{8,24},{9,... | collective-permute-start | bytes 1228808 | tf_op jit(solution)/shard_map/ppermute | solution.py:263
  52.2 13.8 %collective-permute-start.24 = (f32[50,16,128]{2,1,0:T(8,128)S(1)}, f32[50,16,128]{2,1,0:T(8,128)S(1)}, u32[]{:S(2)}, u32[]{:S(2)}) collective-permute-start(f32[50,16,128]{2,1,0:T(8,128)S(1)} %collective-permute-done.20.refs_6_), channel_id=1, source_target_pairs={{0,32},{1,33},{2,34},{3,35},{4,36},{5,37},{6,38},{7,39},{8,40},{9,... | collective-permute-start | bytes 1228808 | tf_op jit(solution)/shard_map/ppermute | solution.py:263
  57.2 10.6 %collective-permute-start.12 = (f32[29,16,128]{2,1,0:T(8,128)S(1)}, f32[29,16,128]{2,1,0:T(8,128)S(1)}, u32[]{:S(2)}, u32[]{:S(2)}) collective-permute-start(f32[29,16,128]{2,1,0:T(8,128)S(1)} %collective-permute-done.11.refs_9_), channel_id=1, source_target_pairs={{0,224},{1,225},{2,226},{3,227},{4,228},{5,229},{6,230},{7,231},{8... | collective-permute-start | bytes 712712 | tf_op jit(solution)/shard_map/ppermute | solution.py:263
  57.3 16.4 %collective-permute-start.27 = (f32[50,16,128]{2,1,0:T(8,128)S(1)}, f32[50,16,128]{2,1,0:T(8,128)S(1)}, u32[]{:S(2)}, u32[]{:S(2)}) collective-permute-start(f32[50,16,128]{2,1,0:T(8,128)S(1)} %collective-permute-done.26.refs_12_), channel_id=1, source_target_pairs={{0,16},{1,17},{2,18},{3,19},{4,20},{5,21},{6,22},{7,23},{8,24},{9,... | collective-permute-start | bytes 1228808 | tf_op jit(solution)/shard_map/ppermute | solution.py:263
  57.8 24.7 %collective-permute-start.21 = (f32[50,16,128]{2,1,0:T(8,128)S(1)}, f32[50,16,128]{2,1,0:T(8,128)S(1)}, u32[]{:S(2)}, u32[]{:S(2)}) collective-permute-start(f32[50,16,128]{2,1,0:T(8,128)S(1)} %collective-permute-done.20.refs_6_), channel_id=1, source_target_pairs={{0,16},{1,17},{2,18},{3,19},{4,20},{5,21},{6,22},{7,23},{8,24},{9,... | collective-permute-start | bytes 1228808 | tf_op jit(solution)/shard_map/ppermute | solution.py:263
  64.9 26.3 %collective-permute-start.23 = (f32[50,16,128]{2,1,0:T(8,128)S(1)}, f32[50,16,128]{2,1,0:T(8,128)S(1)}, u32[]{:S(2)}, u32[]{:S(2)}) collective-permute-start(f32[50,16,128]{2,1,0:T(8,128)S(1)} %collective-permute-done.22.refs_8_), channel_id=1, source_target_pairs={{0,16},{1,17},{2,18},{3,19},{4,20},{5,21},{6,22},{7,23},{8,24},{9,... | collective-permute-start | bytes 1228808 | tf_op jit(solution)/shard_map/ppermute | solution.py:263
  66.0 34.0 %collective-permute-start.25 = (f32[50,16,128]{2,1,0:T(8,128)S(1)}, f32[50,16,128]{2,1,0:T(8,128)S(1)}, u32[]{:S(2)}, u32[]{:S(2)}) collective-permute-start(f32[50,16,128]{2,1,0:T(8,128)S(1)} %collective-permute-done.24.refs_10_), channel_id=1, source_target_pairs={{0,16},{1,17},{2,18},{3,19},{4,20},{5,21},{6,22},{7,23},{8,24},{9,... | collective-permute-start | bytes 1228808 | tf_op jit(solution)/shard_map/ppermute | solution.py:263
  67.9 32.3 %collective-permute-start.28 = (f32[50,16,128]{2,1,0:T(8,128)S(1)}, f32[50,16,128]{2,1,0:T(8,128)S(1)}, u32[]{:S(2)}, u32[]{:S(2)}) collective-permute-start(f32[50,16,128]{2,1,0:T(8,128)S(1)} %collective-permute-done.24.refs_10_), channel_id=1, source_target_pairs={{0,32},{1,33},{2,34},{3,35},{4,36},{5,37},{6,38},{7,39},{8,40},{9,... | collective-permute-start | bytes 1228808 | tf_op jit(solution)/shard_map/ppermute | solution.py:263
  73.7 43.2 %collective-permute-start.29 = (f32[50,16,128]{2,1,0:T(8,128)S(1)}, f32[50,16,128]{2,1,0:T(8,128)S(1)}, u32[]{:S(2)}, u32[]{:S(2)}) collective-permute-start(f32[50,16,128]{2,1,0:T(8,128)S(1)} %collective-permute-done.27.refs_13_), channel_id=1, source_target_pairs={{0,224},{1,225},{2,226},{3,227},{4,228},{5,229},{6,230},{7,231},{8... | collective-permute-start | bytes 1228808 | tf_op jit(solution)/shard_map/ppermute | solution.py:263
  82.5 37.0 %collective-permute-start.9 = (f32[29,16,128]{2,1,0:T(8,128)S(1)}, f32[29,16,128]{2,1,0:T(8,128)S(1)}, u32[]{:S(2)}, u32[]{:S(2)}) collective-permute-start(f32[29,16,128]{2,1,0:T(8,128)S(1)} %collective-permute-done.8.refs_8_), channel_id=1, source_target_pairs={{0,224},{1,225},{2,226},{3,227},{4,228},{5,229},{6,230},{7,231},{8... | collective-permute-start | bytes 712712 | tf_op jit(solution)/shard_map/ppermute | solution.py:263
  91.2 28.2 %collective-permute-start.6 = (f32[29,16,128]{2,1,0:T(8,128)S(1)}, f32[29,16,128]{2,1,0:T(8,128)S(1)}, u32[]{:S(2)}, u32[]{:S(2)}) collective-permute-start(f32[29,16,128]{2,1,0:T(8,128)S(1)} %collective-permute-done.5.refs_7_), channel_id=1, source_target_pairs={{0,32},{1,33},{2,34},{3,35},{4,36},{5,37},{6,38},{7,39},{8,40},{9,... | collective-permute-start | bytes 712712 | tf_op jit(solution)/shard_map/ppermute | solution.py:263
  100.0 19.4 %collective-permute-start.13 = (f32[29,16,128]{2,1,0:T(8,128)S(1)}, f32[29,16,128]{2,1,0:T(8,128)S(1)}, u32[]{:S(2)}, u32[]{:S(2)}) collective-permute-start(f32[29,16,128]{2,1,0:T(8,128)S(1)} %collective-permute-done.2.refs_1_), channel_id=1, source_target_pairs={{0,32},{1,33},{2,34},{3,35},{4,36},{5,37},{6,38},{7,39},{8,40},{9,... | collective-permute-start | bytes 712712 | tf_op jit(solution)/shard_map/ppermute | solution.py:263
  100.2 19.2 %collective-permute-start.14 = (f32[29,16,128]{2,1,0:T(8,128)S(1)}, f32[29,16,128]{2,1,0:T(8,128)S(1)}, u32[]{:S(2)}, u32[]{:S(2)}) collective-permute-start(f32[29,16,128]{2,1,0:T(8,128)S(1)} %collective-permute-done.12.refs_4_), channel_id=1, source_target_pairs={{0,224},{1,225},{2,226},{3,227},{4,228},{5,229},{6,230},{7,231},{8... | collective-permute-start | bytes 712712 | tf_op jit(solution)/shard_map/ppermute | solution.py:263
  119.4 12.3 %copy-start.2 = (f32[64]{0:T(128)S(1)}, f32[64]{0:T(128)}, u32[]{:S(2)}) copy-start(f32[64]{0:T(128)} %param.9) | copy-start | bytes 772
  119.4 12.6 %copy-start.1 = (f32[1,16,4,64]{3,2,1,0:T(4,128)S(1)}, f32[1,16,4,64]{3,2,1,0:T(4,128)}, u32[]{:S(2)}) copy-start(f32[1,16,4,64]{3,2,1,0:T(4,128)} %param.7) | copy-start | bytes 49156
  119.4 12.7 %copy-start.3 = (f32[16]{0:T(128)S(1)}, f32[16]{0:T(128)}, u32[]{:S(2)}) copy-start(f32[16]{0:T(128)} %param.8) | copy-start | bytes 196
  121.7 19.7 %all-to-all-start = ((f32[16,32,256]{2,1,0:T(8,128)}), f32[16,32,256]{2,1,0:T(8,128)S(1)}, u32[]{:S(2)}, u32[]{:S(2)}) async-start(f32[16,32,256]{2,1,0:T(8,128)} %last.1), calls=%async_computation | async-start | bytes 1048576 | tf_op jit(solution)/shard_map/all_to_all | solution.py:305
  142.2 13.7 %all-to-all-start.1 = ((f32[16,8,128]{2,1,0:T(8,128)}), f32[16,8,128]{2,1,0:T(8,128)S(1)}, u32[]{:S(2)}, u32[]{:S(2)}) async-start(f32[16,8,128]{2,1,0:T(8,128)} %get-tuple-element.20), calls=%async_computation.1 | async-start | bytes 131072 | tf_op jit(solution)/shard_map/all_to_all | solution.py:307

commit v3 on v2

--- a/solution.py
+++ b/solution.py
@@ -11,7 +11,7 @@
 ND = 400
 LANES = 128
 NJ, NAB = 16, 256
-TA, TB = 50, 29
+TA, TB = 52, 27
 F32, BF16 = jnp.float32, jnp.bfloat16
 LAST_OUT = pltpu.VMEM
 
@@ -33,15 +33,19 @@
     return jnp.concatenate(parts, axis=-1)
 
 
-def pack_t_kernel(row_ref, t_ref, a_ref, b_ref):
-    for ref, at, c0, n in ((a_ref, 0, 0, 8), (a_ref, 25, 8, 8), (b_ref, 0, 16, 8), (b_ref, 25, 24, 1)):
-        for c in range(n):
+def pack_t_kernel(at_ref, t_ref, a_ref, b_ref):
+    for ref, at, c0 in ((a_ref, 0, 0), (a_ref, 25, 8), (b_ref, 0, 16)):
+        for c in range(8):
             for s in range(3):
                 ref[at + 3 * c + s] = t_ref[c0 + c, :, LANES * s : LANES * (s + 1)]
-        ref[at + 3 * n] = rows_of_rest(lambda c: t_ref[c0 + c, :, 384:400], n)
-
-
-def pack_t(row, t):
+        ref[at + 24] = rows_of_rest(lambda c: t_ref[c0 + c, :, 384:400], 8)
+    a_ref[50] = t_ref[24, :, :LANES]
+    a_ref[51] = t_ref[24, :, LANES : 2 * LANES]
+    b_ref[25] = t_ref[24, :, 2 * LANES : 384]
+    b_ref[26] = rows_of_rest(lambda c: t_ref[24, :, 384:400], 1)
+
+
+def pack_t(at, t):
     return pl.pallas_call(
         pack_t_kernel,
         in_specs=[pl.BlockSpec(memory_space=pltpu.SMEM), VMEM],
@@ -49,7 +53,7 @@
         out_shape=(pltpu.VMEM((TA, NJ, LANES), F32), pltpu.VMEM((TB, NJ, LANES), F32)),
         compiler_params=params(4),
         name="pack_t",
-    )(row, t)
+    )(at, t)
 
 
 def split(x):
@@ -57,28 +61,35 @@
     return hi, (x - hi.astype(F32)).astype(BF16)
 
 
-def pack_v_group(v_ref, h_ref, l_ref, at, n):
-    for c in range(n):
+def pack_v_group(v_ref, h_ref, l_ref):
+    for c in range(8):
         for s in range(3):
-            t = at + 3 * c + s
+            t = 3 * c + s
             h_ref[t], l_ref[t] = split(v_ref[c, :, LANES * s : LANES * (s + 1)])
-    t = at + 3 * n
-    h_ref[t], l_ref[t] = split(rows_of_rest(lambda c: v_ref[c, :, 384:400], n))
+    h_ref[24], l_ref[24] = split(rows_of_rest(lambda c: v_ref[c, :, 384:400], 8))
 
 
 def rows_64(at):
     return pl.ds(pl.multiple_of(at * 64, 64), 64)
 
 
-def pack_va_kernel(v_ref, h_ref, l_ref):
-    tiles, rows = pl.ds(pl.program_id(0) * 25, 25), rows_64(pl.program_id(1))
-    pack_v_group(v_ref, h_ref.at[tiles, rows], l_ref.at[tiles, rows], 0, 8)
+def pack_va_kernel(v_ref, w_ref, h_ref, l_ref):
+    group, rows = pl.program_id(0), rows_64(pl.program_id(1))
+    tiles = pl.ds(group * 25, 25)
+    pack_v_group(v_ref, h_ref.at[tiles, rows], l_ref.at[tiles, rows])
+
+    @pl.when(group == 1)
+    def _():
+        for s in range(2):
+            tile = split(w_ref[0, :, LANES * s : LANES * (s + 1)])
+            h_ref[50 + s, rows, :], l_ref[50 + s, rows, :] = tile
 
 
 def pack_vb_kernel(v_ref, w_ref, h_ref, l_ref):
     rows = rows_64(pl.program_id(0))
-    pack_v_group(v_ref, h_ref.at[:, rows], l_ref.at[:, rows], 0, 8)
-    pack_v_group(w_ref, h_ref.at[:, rows], l_ref.at[:, rows], 25, 1)
+    pack_v_group(v_ref, h_ref.at[:, rows], l_ref.at[:, rows])
+    h_ref[25, rows, :], l_ref[25, rows, :] = split(w_ref[0, :, 2 * LANES : 384])
+    h_ref[26, rows, :], l_ref[26, rows, :] = split(rows_of_rest(lambda c: w_ref[0, :, 384:400], 1))
 
 
 def pack_va(v):
@@ -86,12 +97,15 @@
     return pl.pallas_call(
         pack_va_kernel,
         grid=(2, 4),
-        in_specs=[pl.BlockSpec((None, 8, 64, ND), lambda g, a: (a, g, 0, 0))],
+        in_specs=[
+            pl.BlockSpec((None, 8, 64, ND), lambda g, a: (a, g, 0, 0)),
+            pl.BlockSpec((None, 1, 64, ND), lambda g, a: (a, 24, 0, 0)),
+        ],
         out_specs=(VMEM, VMEM),
         out_shape=(out, out),
         compiler_params=params(8),
         name="pack_va",
-    )(v)
+    )(v, v)
 
 
 def pack_vb(v):
@@ -122,7 +136,7 @@
 
 def product_b(refs, vh, vl):
     total = product(refs, vh, vl, 0, 6)
-    for first, n in ((6, 6), (12, 6), (18, 6), (24, 5)):
+    for first, n in ((6, 6), (12, 6), (18, 6), (24, 3)):
         total += product(refs, vh, vl, first, n)
     return total
 
@@ -130,7 +144,8 @@
 def dot_a_kernel(*refs):
     *t_refs, vh, vl, out = refs
     step = lambda g: product(t_refs, vh, vl, g * 10, 10)
-    out[...] = lax.fori_loop(1, TA // 10, lambda g, total: total + step(g), step(0))
+    total = lax.fori_loop(1, TA // 10, lambda g, total: total + step(g), step(0))
+    out[...] = total + product(t_refs, vh, vl, 50, 2)
 
 
 def dot(kernel, blocks, vh, vl):
@@ -153,10 +168,10 @@
     return (((row >> 1) + dz) & (NZ - 1)) * 2 + ((row & 1) ^ dy)
 
 
-def last_kernel(where, row_ref, *refs):
-    *t_refs, vh, vl, pa1, pa2, pb, out, left, right = refs
+def last_kernel(where, at_ref, *refs):
+    *t_refs, vh, vl, pa1, pa2, pb, keep, give, left, right = refs
     new = product_b(t_refs, vh, vl)
-    row = row_ref[0]
+    row, core = at_ref[0], at_ref[1] & 1
     n_a, n_b = pa1.shape[0] // NJ, pb.shape[0] // NJ
     part = lambda x, q: x[NJ * q : NJ * (q + 1), :]
     for q, (dz, dy) in enumerate(where):
@@ -165,23 +180,26 @@
         at = pl.ds(pl.multiple_of(absolute_row(row, dz, dy) * NJ, NJ), NJ)
         left[at, :] = block[:, :LANES]
         right[at, :] = block[:, LANES:]
-    for k in range(NC):
-        for ref, lanes in ((left, slice(0, LANES)), (right, slice(LANES, NAB))):
-            out[k, :NJ, lanes] = ref[NJ * k : NJ * (k + 1), :]
-            out[k, NJ:, lanes] = ref[pl.ds(k, NJ, stride=NJ), :]
-
-
-def last(row, where, blocks, vh, vl, pa1, pa2, pb):
+    for other, out in enumerate((keep, give)):
+        for m in range(NC // 2):
+            k = 2 * m + (core ^ other)
+            for ref, lanes in ((left, slice(0, LANES)), (right, slice(LANES, NAB))):
+                out[m, :NJ, lanes] = ref[pl.ds(pl.multiple_of(k * NJ, NJ), NJ), :]
+                out[m, NJ:, lanes] = ref[pl.ds(k, NJ, stride=NJ), :]
+
+
+def last(at, where, blocks, vh, vl, pa1, pa2, pb):
+    out = pltpu.VMEM((NC // 2, 2 * NJ, NAB), F32)
     args = [on_chip(x) for x in (*blocks, vh, vl, pa1, pa2, pb)]
     return pl.pallas_call(
         lambda *refs: last_kernel(where, *refs),
         in_specs=[pl.BlockSpec(memory_space=pltpu.SMEM)] + [VMEM] * len(args),
-        out_specs=VMEM,
-        out_shape=LAST_OUT((NC, 2 * NJ, NAB), F32),
+        out_specs=(VMEM, VMEM),
+        out_shape=(out, out),
         scratch_shapes=[pltpu.VMEM((NAB, LANES), F32)] * 2,
         compiler_params=params(8),
         name="last",
-    )(row, *args)
+    )(at, *args)
 
 
 def permute_lanes(x, source):
@@ -197,7 +215,7 @@
 
 def fold_kernel(r_ref, d_ref, e_ref):
     total = r_ref[0]
-    for k in range(1, NC):
+    for k in range(1, NC // 2):
         total += r_ref[k]
     d_ref[...] = total[:NJ]
     mixed = permute_lanes(total[NJ:], lambda n: ((n >> 2) & 3) * 64 + (n >> 4) * 4 + (n & 3))
@@ -257,6 +275,8 @@
 
 
 UP, DOWN, ACROSS = moves(dz=1), moves(dz=-1), moves(dy=1)
+OTHER_CORE = [(i, i ^ 1) for i in range(NR * NC)]
+SAME_CORE = [[r * NC + 2 * m + core for m in range(NC // 2)] for r in range(NR) for core in range(2)]
 
 
 def send(x, where):
@@ -266,8 +286,8 @@
 def on_device(amplitudes, integrals, rest, occ_energy, vir_energy):
     row = lax.axis_index("row")
     col = lax.axis_index("col")
-    row_1 = row.reshape(1)
-    a0, b0 = pack_t(row_1, jnp.transpose(amplitudes, (0, 2, 1, 3))[0])
+    at = jnp.stack([row, col])
+    a0, b0 = pack_t(at, jnp.transpose(amplitudes, (0, 2, 1, 3))[0])
     v = jnp.transpose(integrals, (0, 2, 1, 3))
     v = pltpu.with_memory_space_constraint(v, pltpu.HBM)
     vah, val = pack_va(v)
@@ -290,19 +310,22 @@
     c4 = send(cd[3], DOWN)
 
     a_all, b_all, where = [a0, yu[0]], [b0, bx], [(0, 0), (0, 1)]
-    for s in (1, 2, 3):
+    for s in (1, 2):
         a_all += [au[s], yu[s], ad[s], yd[s]]
         b_all += [bu[s], cu[s], bd[s], cd[s]]
         where += [(-s, 0), (-s, 1), (s, 0), (s, 1)]
-    a_all += [a4, a4x]
-    b_all += [b4, c4]
-    where += [(4, 0), (4, 1)]
+    a_all += [au[3], ad[3], yd[3], yu[3], a4, a4x]
+    b_all += [bu[3], bd[3], cd[3], cu[3], b4, c4]
+    where += [(-3, 0), (3, 0), (3, 1), (-3, 1), (4, 0), (4, 1)]
     pa1 = dot(dot_a_kernel, a_all[:N_A], vah, val)
     pa2 = dot(dot_a_kernel, a_all[N_A:], vah, val)
     pb = dot(dot_b_kernel, b_all[:N_B], vbh, vbl)
-    partial = last(row_1, where, b_all[N_B:], vbh, vbl, pa1, pa2, pb)
-
-    received = lax.all_to_all(partial, "col", 0, 0, tiled=True)
+    keep, give = last(at, where, b_all[N_B:], vbh, vbl, pa1, pa2, pb)
+
+    partial = keep + send(give, OTHER_CORE)
+    received = lax.all_to_all(
+        partial, AXES, 0, 0, axis_index_groups=SAME_CORE, tiled=True
+    )
     direct, messages = fold(received)
     mirror = lax.all_to_all(messages, "row", 0, 0, tiled=True)
 
@@ -316,7 +339,7 @@
     return out[None]
 
 
-N_A, N_B = 14, 10
+N_A, N_B = 13, 10
 
 
 def solution(mesh):

time: 157 us -> 163 us (1.038)
  waiting for transfers between devices: 89.4 us -> 94.1 us
    ppermute x30 -> x31, waiting for transfers between devices: 72 us -> 80.4 us  [send(): return lax.ppermute(x, AXES, where)]
    all_to_all x1, starting transfers between devices: 10 us -> 4.13 us  [on_device(): lax.all_to_all(partial, AXES, 0, 0, axis_index_groups=SAME_CORE, tiled=True)]
    ppermute x30 -> x31, starting transfers between devices: 29.4 us -> 34.1 us  [send(): return lax.ppermute(x, AXES, where)]
    all_to_all x1, waiting for transfers between devices: 8.02 us -> 4.35 us  [on_device(): lax.all_to_all(partial, AXES, 0, 0, axis_index_groups=SAME_CORE, tiled=True)]
  transfers between devices with their start and end apart: 32 -> 33, of which waited for: 15 -> 17; matrix products, arithmetic and copies ran while one was open for 1% -> 1% of each run, Pallas kernels for 11% -> 10%
where the time goes in v3:
time: 163 us; the launch traced here: 162 us
  waiting for transfers between devices  94.1 us (58%)
  starting transfers between devices  42.6 us (26%)
  Pallas kernels  21.4 us (13%)
  local copies, waits for them, and re-layouts  2.16 us (1%)
    ppermute x31, waiting for transfers between devices, send(): return lax.ppermute(x, AXES, where)  80.4 us
    ppermute x31, starting transfers between devices, send(): return lax.ppermute(x, AXES, where)  34.1 us
    all_to_all x1, waiting for transfers between devices, on_device(): mirror = lax.all_to_all(messages, 'row', 0, 0, tiled=True)  9.33 us
    pallas_call x3, Pallas kernels, dot(): pl.pallas_call(kernel, in_specs=[VMEM] * len(args), out_specs=VMEM, out_s...  7.59 us
    pallas_call x1, Pallas kernels, pack_va(): pl.pallas_call(pack_va_kernel, grid=(2, 4), in_specs=[pl.BlockSpec((None,...  6.18 us
    all_to_all x1, starting transfers between devices, on_device(): mirror = lax.all_to_all(messages, 'row', 0, 0, tiled=True)  4.37 us
    all_to_all x1, waiting for transfers between devices, on_device(): lax.all_to_all(partial, AXES, 0, 0, axis_index_groups=SAME_CORE, tiled=True)  4.35 us
    all_to_all x1, starting transfers between devices, on_device(): lax.all_to_all(partial, AXES, 0, 0, axis_index_groups=SAME_CORE, tiled=True)  4.13 us
  transfers between devices with their start and end apart: 33, of which 17 were waited for; matrix products, arithmetic and copies ran while one was open for 1% of the time, Pallas kernels for 10%

profile of v3, /device:TPU:1, one launch (start us, length us, event | category | flops | bytes accessed | tf_op | source)
XLA Modules:
  0.0 161.9 jit_solution(14595268314002721687)
XLA Ops:
  0.0 0.1 pad_add_fusion.at_ref.refs_0_
  0.1 1.1 copy-done
  1.2 0.7 pack_t.1
  1.9 6.5 %collective-permute-start.18 = (f32[52,16,128]{2,1,0:T(8,128)S(1)}, f32[52,16,128]{2,1,0:T(8,128)S(1)}, u32[]{:S(2)}, u32[]{:S(2)}) collective-permute-start(f32[52,16,128]{2,1,0:T(8,128)S(1)} %get-tuple-element.18.refs_0_), channel_id=1, source_target_pairs={{0,224},{1,225},{2,226},{3,227},{4,228},{5,229},{6,230},{7,231},{8... | collective-permute-start | bytes 1277960 | tf_op jit(solution)/shard_map/ppermute | solution.py:283
  8.3 2.9 %collective-permute-start.6 = (f32[27,16,128]{2,1,0:T(8,128)S(1)}, f32[27,16,128]{2,1,0:T(8,128)S(1)}, u32[]{:S(2)}, u32[]{:S(2)}) collective-permute-start(f32[27,16,128]{2,1,0:T(8,128)S(1)} %get-tuple-element.15.refs_0_), channel_id=1, source_target_pairs={{0,16},{1,17},{2,18},{3,19},{4,20},{5,21},{6,22},{7,23},{8,24},{9,... | collective-permute-start | bytes 663560 | tf_op jit(solution)/shard_map/ppermute | solution.py:283
  11.3 0.1 collective-permute-start.15
  11.3 0.0 collective-permute-start
  11.3 4.6 %collective-permute-done.6.refs_1_ = f32[27,16,128]{2,1,0:T(8,128)S(1)} collective-permute-done((f32[27,16,128]{2,1,0:T(8,128)S(1)}, f32[27,16,128]{2,1,0:T(8,128)S(1)}, u32[]{:S(2)}, u32[]{:S(2)}) %collective-permute-start.6) | collective-permute-done | bytes 221216 | tf_op jit(solution)/shard_map/ppermute | solution.py:283
  15.9 0.7 collective-permute-start.3
  16.6 0.2 collective-permute-done.18.refs_4_
  16.8 3.4 %collective-permute-start.22 = (f32[52,16,128]{2,1,0:T(8,128)S(1)}, f32[52,16,128]{2,1,0:T(8,128)S(1)}, u32[]{:S(2)}, u32[]{:S(2)}) collective-permute-start(f32[52,16,128]{2,1,0:T(8,128)S(1)} %collective-permute-done.18.refs_4_), channel_id=1, source_target_pairs={{0,224},{1,225},{2,226},{3,227},{4,228},{5,229},{6,230},{7,231},{8... | collective-permute-start | bytes 1277960 | tf_op jit(solution)/shard_map/ppermute | solution.py:283
  20.3 7.1 %collective-permute-done.refs_2_ = f32[27,16,128]{2,1,0:T(8,128)S(1)} collective-permute-done((f32[27,16,128]{2,1,0:T(8,128)S(1)}, f32[27,16,128]{2,1,0:T(8,128)S(1)}, u32[]{:S(2)}, u32[]{:S(2)}) %collective-permute-start) | collective-permute-done | bytes 221216 | tf_op jit(solution)/shard_map/ppermute | solution.py:283
  27.3 0.0 collective-permute-start.10
  27.4 0.0 collective-permute-done.3.refs_4_
  27.4 2.7 %collective-permute-start.7 = (f32[27,16,128]{2,1,0:T(8,128)S(1)}, f32[27,16,128]{2,1,0:T(8,128)S(1)}, u32[]{:S(2)}, u32[]{:S(2)}) collective-permute-start(f32[27,16,128]{2,1,0:T(8,128)S(1)} %collective-permute-done.6.refs_1_), channel_id=1, source_target_pairs={{0,224},{1,225},{2,226},{3,227},{4,228},{5,229},{6,230},{7,231},{8... | collective-permute-start | bytes 663560 | tf_op jit(solution)/shard_map/ppermute | solution.py:283
  30.0 0.0 collective-permute-done.16.refs_2_
  30.0 0.1 collective-permute-start.20
  30.1 3.2 %collective-permute-done.10.refs_3_ = f32[27,16,128]{2,1,0:T(8,128)S(1)} collective-permute-done((f32[27,16,128]{2,1,0:T(8,128)S(1)}, f32[27,16,128]{2,1,0:T(8,128)S(1)}, u32[]{:S(2)}, u32[]{:S(2)}) %collective-permute-start.10) | collective-permute-done | bytes 221216 | tf_op jit(solution)/shard_map/ppermute | solution.py:283
  33.3 1.7 %collective-permute-done.7.refs_5_ = f32[27,16,128]{2,1,0:T(8,128)S(1)} collective-permute-done((f32[27,16,128]{2,1,0:T(8,128)S(1)}, f32[27,16,128]{2,1,0:T(8,128)S(1)}, u32[]{:S(2)}, u32[]{:S(2)}) %collective-permute-start.7) | collective-permute-done | bytes 221216 | tf_op jit(solution)/shard_map/ppermute | solution.py:283
  35.1 3.6 %collective-permute-done.1.refs_6_ = f32[27,16,128]{2,1,0:T(8,128)S(1)} collective-permute-done((f32[27,16,128]{2,1,0:T(8,128)S(1)}, f32[27,16,128]{2,1,0:T(8,128)S(1)}, u32[]{:S(2)}, u32[]{:S(2)}) %collective-permute-start.1) | collective-permute-done | bytes 221216 | tf_op jit(solution)/shard_map/ppermute | solution.py:283
  38.7 1.3 collective-permute-start.25
  40.0 0.3 collective-permute-start.2
  40.2 12.3 %collective-permute-done.11.refs_7_ = f32[27,16,128]{2,1,0:T(8,128)S(1)} collective-permute-done((f32[27,16,128]{2,1,0:T(8,128)S(1)}, f32[27,16,128]{2,1,0:T(8,128)S(1)}, u32[]{:S(2)}, u32[]{:S(2)}) %collective-permute-start.11) | collective-permute-done | bytes 221216 | tf_op jit(solution)/shard_map/ppermute | solution.py:283
  52.6 0.1 collective-permute-start.17
  52.6 2.9 %collective-permute-start.19 = (f32[52,16,128]{2,1,0:T(8,128)S(1)}, f32[52,16,128]{2,1,0:T(8,128)S(1)}, u32[]{:S(2)}, u32[]{:S(2)}) collective-permute-start(f32[52,16,128]{2,1,0:T(8,128)S(1)} %collective-permute-done.18.refs_4_), channel_id=1, source_target_pairs={{0,16},{1,17},{2,18},{3,19},{4,20},{5,21},{6,22},{7,23},{8,24},{9,... | collective-permute-start | bytes 1277960 | tf_op jit(solution)/shard_map/ppermute | solution.py:283
  55.5 1.8 %collective-permute-done.2.refs_1_ = f32[27,16,128]{2,1,0:T(8,128)S(1)} collective-permute-done((f32[27,16,128]{2,1,0:T(8,128)S(1)}, f32[27,16,128]{2,1,0:T(8,128)S(1)}, u32[]{:S(2)}, u32[]{:S(2)}) %collective-permute-start.2) | collective-permute-done | bytes 221216 | tf_op jit(solution)/shard_map/ppermute | solution.py:283
  57.3 0.9 collective-permute-start.9
  58.2 0.1 collective-permute-start.26
  58.3 2.7 %collective-permute-done.17.refs_3_ = f32[52,16,128]{2,1,0:T(8,128)S(1)} collective-permute-done((f32[52,16,128]{2,1,0:T(8,128)S(1)}, f32[52,16,128]{2,1,0:T(8,128)S(1)}, u32[]{:S(2)}, u32[]{:S(2)}) %collective-permute-start.17) | collective-permute-done | bytes 426016 | tf_op jit(solution)/shard_map/ppermute | solution.py:283
  61.0 0.2 collective-permute-start.21
  61.2 8.5 %collective-permute-done.19.refs_5_ = f32[52,16,128]{2,1,0:T(8,128)S(1)} collective-permute-done((f32[52,16,128]{2,1,0:T(8,128)S(1)}, f32[52,16,128]{2,1,0:T(8,128)S(1)}, u32[]{:S(2)}, u32[]{:S(2)}) %collective-permute-start.19) | collective-permute-done | bytes 426016 | tf_op jit(solution)/shard_map/ppermute | solution.py:283
  69.7 0.1 collective-permute-start.23
  69.8 2.9 %collective-permute-start.27 = (f32[52,16,128]{2,1,0:T(8,128)S(1)}, f32[52,16,128]{2,1,0:T(8,128)S(1)}, u32[]{:S(2)}, u32[]{:S(2)}) collective-permute-start(f32[52,16,128]{2,1,0:T(8,128)S(1)} %collective-permute-done.24.refs_10_), channel_id=1, source_target_pairs={{0,16},{1,17},{2,18},{3,19},{4,20},{5,21},{6,22},{7,23},{8,24},{9,... | collective-permute-start | bytes 1277960 | tf_op jit(solution)/shard_map/ppermute | solution.py:283
  72.7 6.1 %collective-permute-done.26.refs_12_ = f32[52,16,128]{2,1,0:T(8,128)S(1)} collective-permute-done((f32[52,16,128]{2,1,0:T(8,128)S(1)}, f32[52,16,128]{2,1,0:T(8,128)S(1)}, u32[]{:S(2)}, u32[]{:S(2)}) %collective-permute-start.26) | collective-permute-done | bytes 426016 | tf_op jit(solution)/shard_map/ppermute | solution.py:283
  78.8 9.1 %collective-permute-done.21.refs_7_ = f32[52,16,128]{2,1,0:T(8,128)S(1)} collective-permute-done((f32[52,16,128]{2,1,0:T(8,128)S(1)}, f32[52,16,128]{2,1,0:T(8,128)S(1)}, u32[]{:S(2)}, u32[]{:S(2)}) %collective-permute-start.21) | collective-permute-done | bytes 426016 | tf_op jit(solution)/shard_map/ppermute | solution.py:283
  88.0 9.1 %collective-permute-done.23.refs_9_ = f32[52,16,128]{2,1,0:T(8,128)S(1)} collective-permute-done((f32[52,16,128]{2,1,0:T(8,128)S(1)}, f32[52,16,128]{2,1,0:T(8,128)S(1)}, u32[]{:S(2)}, u32[]{:S(2)}) %collective-permute-start.23) | collective-permute-done | bytes 426016 | tf_op jit(solution)/shard_map/ppermute | solution.py:283
  97.1 9.1 %collective-permute-done.27.refs_0_ = f32[52,16,128]{2,1,0:T(8,128)S(1)} collective-permute-done((f32[52,16,128]{2,1,0:T(8,128)S(1)}, f32[52,16,128]{2,1,0:T(8,128)S(1)}, u32[]{:S(2)}, u32[]{:S(2)}) %collective-permute-start.27) | collective-permute-done | bytes 426016 | tf_op jit(solution)/shard_map/ppermute | solution.py:283
  106.2 2.7 %collective-permute-start.14 = (f32[27,16,128]{2,1,0:T(8,128)S(1)}, f32[27,16,128]{2,1,0:T(8,128)S(1)}, u32[]{:S(2)}, u32[]{:S(2)}) collective-permute-start(f32[27,16,128]{2,1,0:T(8,128)S(1)} %collective-permute-done.9.refs_3_), channel_id=1, source_target_pairs={{0,224},{1,225},{2,226},{3,227},{4,228},{5,229},{6,230},{7,231},{8... | collective-permute-start | bytes 663560 | tf_op jit(solution)/shard_map/ppermute | solution.py:283
  108.9 6.2 %pack_va.1 = (bf16[52,256,128]{2,1,0:T(8,128)(2,1)S(1)}, bf16[52,256,128]{2,1,0:T(8,128)(2,1)S(1)}) custom-call(f32[4,25,64,400]{3,2,1,0:T(8,128)} %bitcast.9, f32[4,25,64,400]{3,2,1,0:T(8,128)} %bitcast.10), custom_call_target="tpu_custom_call" | custom-call | tf_op jit(solution)/shard_map/pack_va/pallas_call | solution.py:97
  115.1 3.2 %pack_vb.1 = (bf16[27,256,128]{2,1,0:T(8,128)(2,1)S(1)}, bf16[27,256,128]{2,1,0:T(8,128)(2,1)S(1)}) custom-call(f32[4,25,64,400]{3,2,1,0:T(8,128)} %bitcast.11, f32[4,25,64,400]{3,2,1,0:T(8,128)} %bitcast.12), custom_call_target="tpu_custom_call" | custom-call | tf_op jit(solution)/shard_map/pack_vb/pallas_call | solution.py:113
  118.3 1.3 shard_map.57.refs_11_
  119.6 3.5 %shard_map.55.refs_9_ = f32[208,256]{1,0:T(8,128)S(1)} custom-call(f32[52,16,128]{2,1,0:T(8,128)S(1)} %get-tuple-element.18.refs_0_, f32[52,16,128]{2,1,0:T(8,128)S(1)} %collective-permute-done.15.refs_1_, f32[52,16,128]{2,1,0:T(8,128)S(1)} %collective-permute-done.16.refs_2_, f32[52,16,128]{2,1,0:T(8,128)S(1)} %collective-permute-done.17.refs_3_, ...), custom_call_target="tpu_custom_call" | custom-call | tf_op jit(solution)/shard_map/pallas_call | solution.py:153
  123.2 2.8 %shard_map.56.refs_10_ = f32[48,256]{1,0:T(8,128)S(1)} custom-call(f32[52,16,128]{2,1,0:T(8,128)S(1)} %collective-permute-done.27.refs_0_, f32[52,16,128]{2,1,0:T(8,128)S(1)} %collective-permute-done.28.refs_1_, f32[52,16,128]{2,1,0:T(8,128)S(1)} %collective-permute-done.29.refs_2_, bf16[52,256,128]{2,1,0:T(8,128)(2,1)S(1)} %get-tuple-element.19.refs_13_.refs_3_, ...), custom_call_target="tpu_custom_call" | custom-call | tf_op jit(solution)/shard_map/pallas_call | solution.py:153
  125.9 0.0 copy-start.2
  125.9 0.0 copy-start.1
  126.0 0.0 copy-start.3
  126.0 1.9 %last.1 = (f32[8,32,256]{2,1,0:T(8,128)S(1)}, f32[8,32,256]{2,1,0:T(8,128)S(1)}) custom-call(s32[2]{0:T(128)S(1)} %pad_add_fusion.at_ref.refs_0_, f32[27,16,128]{2,1,0:T(8,128)S(1)} %collective-permute-done.2.refs_1_, f32[27,16,128]{2,1,0:T(8,128)S(1)} %collective-permute-done.5.refs_2_, f32[27,16,128]{2,1,0:T(8,128)S(1)} %collective-permute-done.9.refs_3_, ...), custom_call_target="tpu_custom_call" | custom-call | tf_op jit(solution)/shard_map/last/pallas_call | solution.py:194
  127.9 6.4 %collective-permute-start.30 = (f32[8,32,256]{2,1,0:T(8,128)S(1)}, f32[8,32,256]{2,1,0:T(8,128)S(1)}, u32[]{:S(2)}, u32[]{:S(2)}) collective-permute-start(f32[8,32,256]{2,1,0:T(8,128)S(1)} %get-tuple-element.22), channel_id=1, source_target_pairs={{0,1},{1,0},{2,3},{3,2},{4,5},{5,4},{6,7},{7,6},{8,9},{9,8},{10,11... | collective-permute-start | bytes 786440 | tf_op jit(solution)/shard_map/ppermute | solution.py:283
  134.3 0.1 dynamic_slice.6
  134.4 1.1 collective-permute-done.30
  135.5 0.7 add.31
  136.2 4.1 %all-to-all-start = ((f32[8,32,256]{2,1,0:T(8,128)}), f32[8,32,256]{2,1,0:T(8,128)S(1)}, u32[]{:S(2)}, u32[]{:S(2)}) async-start(f32[8,32,256]{2,1,0:T(8,128)} %add.31), calls=%async_computation | async-start | bytes 524288 | tf_op jit(solution)/shard_map/all_to_all | solution.py:326
  140.3 0.1 broadcast_reduce_fusion
  140.4 0.1 add.34
  140.5 0.1 add.36
  140.6 0.1 reshape.40.rest_ref
  140.7 0.6 dynamic_slice.7
  141.3 0.6 add_subtract_fusion
  141.9 4.4 %all-to-all-done.r_ref = f32[8,32,256]{2,1,0:T(8,128)S(1)} async-done(((f32[8,32,256]{2,1,0:T(8,128)}), f32[8,32,256]{2,1,0:T(8,128)S(1)}, u32[]{:S(2)}, u32[]{:S(2)}) %all-to-all-start) | async-done | bytes 262176 | tf_op jit(solution)/shard_map/all_to_all | solution.py:326
  146.3 0.9 fold.1
  147.2 4.4 %all-to-all-start.1 = ((f32[16,8,128]{2,1,0:T(8,128)}), f32[16,8,128]{2,1,0:T(8,128)S(1)}, u32[]{:S(2)}, u32[]{:S(2)}) async-start(f32[16,8,128]{2,1,0:T(8,128)} %get-tuple-element.24), calls=%async_computation.1 | async-start | bytes 131072 | tf_op jit(solution)/shard_map/all_to_all | solution.py:330
  151.5 0.1 broadcast_subtract_fusion.den_ref
  151.6 9.3 %all-to-all-done.1.m_ref = f32[16,8,128]{2,1,0:T(8,128)S(1)} async-done(((f32[16,8,128]{2,1,0:T(8,128)}), f32[16,8,128]{2,1,0:T(8,128)S(1)}, u32[]{:S(2)}, u32[]{:S(2)}) %all-to-all-start.1) | async-done | bytes 65568 | tf_op jit(solution)/shard_map/all_to_all | solution.py:330
  160.9 0.9 finish.1
  (30 shorter events, 0.1 us)
Async XLA Ops:
  0.1 1.1 copy-start
  1.9 15.0 %collective-permute-start.18 = (f32[52,16,128]{2,1,0:T(8,128)S(1)}, f32[52,16,128]{2,1,0:T(8,128)S(1)}, u32[]{:S(2)}, u32[]{:S(2)}) collective-permute-start(f32[52,16,128]{2,1,0:T(8,128)S(1)} %get-tuple-element.18.refs_0_), channel_id=1, source_target_pairs={{0,224},{1,225},{2,226},{3,227},{4,228},{5,229},{6,230},{7,231},{8... | collective-permute-start | bytes 1277960 | tf_op jit(solution)/shard_map/ppermute | solution.py:283
  8.3 7.5 %collective-permute-start.6 = (f32[27,16,128]{2,1,0:T(8,128)S(1)}, f32[27,16,128]{2,1,0:T(8,128)S(1)}, u32[]{:S(2)}, u32[]{:S(2)}) collective-permute-start(f32[27,16,128]{2,1,0:T(8,128)S(1)} %get-tuple-element.15.refs_0_), channel_id=1, source_target_pairs={{0,16},{1,17},{2,18},{3,19},{4,20},{5,21},{6,22},{7,23},{8,24},{9,... | collective-permute-start | bytes 663560 | tf_op jit(solution)/shard_map/ppermute | solution.py:283
  11.3 18.8 %collective-permute-start.16 = (f32[52,16,128]{2,1,0:T(8,128)S(1)}, f32[52,16,128]{2,1,0:T(8,128)S(1)}, u32[]{:S(2)}, u32[]{:S(2)}) collective-permute-start(f32[52,16,128]{2,1,0:T(8,128)S(1)} %get-tuple-element.18.refs_0_), channel_id=1, source_target_pairs={{0,32},{1,33},{2,34},{3,35},{4,36},{5,37},{6,38},{7,39},{8,40},{9,... | collective-permute-start | bytes 1277960 | tf_op jit(solution)/shard_map/ppermute | solution.py:283
  11.3 18.8 %collective-permute-start.15 = (f32[52,16,128]{2,1,0:T(8,128)S(1)}, f32[52,16,128]{2,1,0:T(8,128)S(1)}, u32[]{:S(2)}, u32[]{:S(2)}) collective-permute-start(f32[52,16,128]{2,1,0:T(8,128)S(1)} %get-tuple-element.18.refs_0_), channel_id=1, source_target_pairs={{0,16},{1,17},{2,18},{3,19},{4,20},{5,21},{6,22},{7,23},{8,24},{9,... | collective-permute-start | bytes 1277960 | tf_op jit(solution)/shard_map/ppermute | solution.py:283
  11.3 16.0 %collective-permute-start = (f32[27,16,128]{2,1,0:T(8,128)S(1)}, f32[27,16,128]{2,1,0:T(8,128)S(1)}, u32[]{:S(2)}, u32[]{:S(2)}) collective-permute-start(f32[27,16,128]{2,1,0:T(8,128)S(1)} %get-tuple-element.15.refs_0_), channel_id=1, source_target_pairs={{0,32},{1,33},{2,34},{3,35},{4,36},{5,37},{6,38},{7,39},{8,40},{9,... | collective-permute-start | bytes 663560 | tf_op jit(solution)/shard_map/ppermute | solution.py:283
  15.9 11.5 %collective-permute-start.3 = (f32[27,16,128]{2,1,0:T(8,128)S(1)}, f32[27,16,128]{2,1,0:T(8,128)S(1)}, u32[]{:S(2)}, u32[]{:S(2)}) collective-permute-start(f32[27,16,128]{2,1,0:T(8,128)S(1)} %get-tuple-element.15.refs_0_), channel_id=1, source_target_pairs={{0,224},{1,225},{2,226},{3,227},{4,228},{5,229},{6,230},{7,231},{8... | collective-permute-start | bytes 663560 | tf_op jit(solution)/shard_map/ppermute | solution.py:283
  16.8 21.8 %collective-permute-start.22 = (f32[52,16,128]{2,1,0:T(8,128)S(1)}, f32[52,16,128]{2,1,0:T(8,128)S(1)}, u32[]{:S(2)}, u32[]{:S(2)}) collective-permute-start(f32[52,16,128]{2,1,0:T(8,128)S(1)} %collective-permute-done.18.refs_4_), channel_id=1, source_target_pairs={{0,224},{1,225},{2,226},{3,227},{4,228},{5,229},{6,230},{7,231},{8... | collective-permute-start | bytes 1277960 | tf_op jit(solution)/shard_map/ppermute | solution.py:283
  27.3 6.0 %collective-permute-start.10 = (f32[27,16,128]{2,1,0:T(8,128)S(1)}, f32[27,16,128]{2,1,0:T(8,128)S(1)}, u32[]{:S(2)}, u32[]{:S(2)}) collective-permute-start(f32[27,16,128]{2,1,0:T(8,128)S(1)} %collective-permute-done.6.refs_1_), channel_id=1, source_target_pairs={{0,32},{1,33},{2,34},{3,35},{4,36},{5,37},{6,38},{7,39},{8,40},{9,... | collective-permute-start | bytes 663560 | tf_op jit(solution)/shard_map/ppermute | solution.py:283
  27.4 7.7 %collective-permute-start.7 = (f32[27,16,128]{2,1,0:T(8,128)S(1)}, f32[27,16,128]{2,1,0:T(8,128)S(1)}, u32[]{:S(2)}, u32[]{:S(2)}) collective-permute-start(f32[27,16,128]{2,1,0:T(8,128)S(1)} %collective-permute-done.6.refs_1_), channel_id=1, source_target_pairs={{0,224},{1,225},{2,226},{3,227},{4,228},{5,229},{6,230},{7,231},{8... | collective-permute-start | bytes 663560 | tf_op jit(solution)/shard_map/ppermute | solution.py:283
  30.0 8.7 %collective-permute-start.1 = (f32[27,16,128]{2,1,0:T(8,128)S(1)}, f32[27,16,128]{2,1,0:T(8,128)S(1)}, u32[]{:S(2)}, u32[]{:S(2)}) collective-permute-start(f32[27,16,128]{2,1,0:T(8,128)S(1)} %collective-permute-done.refs_2_), channel_id=1, source_target_pairs={{0,32},{1,33},{2,34},{3,35},{4,36},{5,37},{6,38},{7,39},{8,40},{9,... | collective-permute-start | bytes 663560 | tf_op jit(solution)/shard_map/ppermute | solution.py:283
  30.0 25.5 %collective-permute-start.20 = (f32[52,16,128]{2,1,0:T(8,128)S(1)}, f32[52,16,128]{2,1,0:T(8,128)S(1)}, u32[]{:S(2)}, u32[]{:S(2)}) collective-permute-start(f32[52,16,128]{2,1,0:T(8,128)S(1)} %collective-permute-done.16.refs_2_), channel_id=1, source_target_pairs={{0,32},{1,33},{2,34},{3,35},{4,36},{5,37},{6,38},{7,39},{8,40},{9,... | collective-permute-start | bytes 1277960 | tf_op jit(solution)/shard_map/ppermute | solution.py:283
  33.3 6.6 %collective-permute-start.4 = (f32[27,16,128]{2,1,0:T(8,128)S(1)}, f32[27,16,128]{2,1,0:T(8,128)S(1)}, u32[]{:S(2)}, u32[]{:S(2)}) collective-permute-start(f32[27,16,128]{2,1,0:T(8,128)S(1)} %collective-permute-done.3.refs_4_), channel_id=1, source_target_pairs={{0,224},{1,225},{2,226},{3,227},{4,228},{5,229},{6,230},{7,231},{8... | collective-permute-start | bytes 663560 | tf_op jit(solution)/shard_map/ppermute | solution.py:283
  35.1 17.5 %collective-permute-start.11 = (f32[27,16,128]{2,1,0:T(8,128)S(1)}, f32[27,16,128]{2,1,0:T(8,128)S(1)}, u32[]{:S(2)}, u32[]{:S(2)}) collective-permute-start(f32[27,16,128]{2,1,0:T(8,128)S(1)} %collective-permute-done.10.refs_3_), channel_id=1, source_target_pairs={{0,32},{1,33},{2,34},{3,35},{4,36},{5,37},{6,38},{7,39},{8,40},{9,... | collective-permute-start | bytes 663560 | tf_op jit(solution)/shard_map/ppermute | solution.py:283
  38.7 13.9 %collective-permute-start.8 = (f32[27,16,128]{2,1,0:T(8,128)S(1)}, f32[27,16,128]{2,1,0:T(8,128)S(1)}, u32[]{:S(2)}, u32[]{:S(2)}) collective-permute-start(f32[27,16,128]{2,1,0:T(8,128)S(1)} %collective-permute-done.7.refs_5_), channel_id=1, source_target_pairs={{0,224},{1,225},{2,226},{3,227},{4,228},{5,229},{6,230},{7,231},{8... | collective-permute-start | bytes 663560 | tf_op jit(solution)/shard_map/ppermute | solution.py:283
  38.7 19.5 %collective-permute-start.25 = (f32[52,16,128]{2,1,0:T(8,128)S(1)}, f32[52,16,128]{2,1,0:T(8,128)S(1)}, u32[]{:S(2)}, u32[]{:S(2)}) collective-permute-start(f32[52,16,128]{2,1,0:T(8,128)S(1)} %collective-permute-done.22.refs_8_), channel_id=1, source_target_pairs={{0,224},{1,225},{2,226},{3,227},{4,228},{5,229},{6,230},{7,231},{8... | collective-permute-start | bytes 1277960 | tf_op jit(solution)/shard_map/ppermute | solution.py:283
  40.0 17.3 %collective-permute-start.2 = (f32[27,16,128]{2,1,0:T(8,128)S(1)}, f32[27,16,128]{2,1,0:T(8,128)S(1)}, u32[]{:S(2)}, u32[]{:S(2)}) collective-permute-start(f32[27,16,128]{2,1,0:T(8,128)S(1)} %collective-permute-done.1.refs_6_), channel_id=1, source_target_pairs={{0,32},{1,33},{2,34},{3,35},{4,36},{5,37},{6,38},{7,39},{8,40},{9,... | collective-permute-start | bytes 663560 | tf_op jit(solution)/shard_map/ppermute | solution.py:283
  52.6 8.5 %collective-permute-start.17 = (f32[52,16,128]{2,1,0:T(8,128)S(1)}, f32[52,16,128]{2,1,0:T(8,128)S(1)}, u32[]{:S(2)}, u32[]{:S(2)}) collective-permute-start(f32[52,16,128]{2,1,0:T(8,128)S(1)} %collective-permute-done.16.refs_2_), channel_id=1, source_target_pairs={{0,16},{1,17},{2,18},{3,19},{4,20},{5,21},{6,22},{7,23},{8,24},{9,... | collective-permute-start | bytes 1277960 | tf_op jit(solution)/shard_map/ppermute | solution.py:283
  52.6 17.1 %collective-permute-start.19 = (f32[52,16,128]{2,1,0:T(8,128)S(1)}, f32[52,16,128]{2,1,0:T(8,128)S(1)}, u32[]{:S(2)}, u32[]{:S(2)}) collective-permute-start(f32[52,16,128]{2,1,0:T(8,128)S(1)} %collective-permute-done.18.refs_4_), channel_id=1, source_target_pairs={{0,16},{1,17},{2,18},{3,19},{4,20},{5,21},{6,22},{7,23},{8,24},{9,... | collective-permute-start | bytes 1277960 | tf_op jit(solution)/shard_map/ppermute | solution.py:283
  55.5 14.2 %collective-permute-start.24 = (f32[52,16,128]{2,1,0:T(8,128)S(1)}, f32[52,16,128]{2,1,0:T(8,128)S(1)}, u32[]{:S(2)}, u32[]{:S(2)}) collective-permute-start(f32[52,16,128]{2,1,0:T(8,128)S(1)} %collective-permute-done.20.refs_6_), channel_id=1, source_target_pairs={{0,32},{1,33},{2,34},{3,35},{4,36},{5,37},{6,38},{7,39},{8,40},{9,... | collective-permute-start | bytes 1277960 | tf_op jit(solution)/shard_map/ppermute | solution.py:283
  57.3 15.4 %collective-permute-start.9 = (f32[27,16,128]{2,1,0:T(8,128)S(1)}, f32[27,16,128]{2,1,0:T(8,128)S(1)}, u32[]{:S(2)}, u32[]{:S(2)}) collective-permute-start(f32[27,16,128]{2,1,0:T(8,128)S(1)} %collective-permute-done.8.refs_9_), channel_id=1, source_target_pairs={{0,224},{1,225},{2,226},{3,227},{4,228},{5,229},{6,230},{7,231},{8... | collective-permute-start | bytes 663560 | tf_op jit(solution)/shard_map/ppermute | solution.py:283
  58.2 20.6 %collective-permute-start.26 = (f32[52,16,128]{2,1,0:T(8,128)S(1)}, f32[52,16,128]{2,1,0:T(8,128)S(1)}, u32[]{:S(2)}, u32[]{:S(2)}) collective-permute-start(f32[52,16,128]{2,1,0:T(8,128)S(1)} %collective-permute-done.25.refs_11_), channel_id=1, source_target_pairs={{0,16},{1,17},{2,18},{3,19},{4,20},{5,21},{6,22},{7,23},{8,24},{9,... | collective-permute-start | bytes 1277960 | tf_op jit(solution)/shard_map/ppermute | solution.py:283
  61.0 26.9 %collective-permute-start.21 = (f32[52,16,128]{2,1,0:T(8,128)S(1)}, f32[52,16,128]{2,1,0:T(8,128)S(1)}, u32[]{:S(2)}, u32[]{:S(2)}) collective-permute-start(f32[52,16,128]{2,1,0:T(8,128)S(1)} %collective-permute-done.20.refs_6_), channel_id=1, source_target_pairs={{0,16},{1,17},{2,18},{3,19},{4,20},{5,21},{6,22},{7,23},{8,24},{9,... | collective-permute-start | bytes 1277960 | tf_op jit(solution)/shard_map/ppermute | solution.py:283
  69.7 27.4 %collective-permute-start.23 = (f32[52,16,128]{2,1,0:T(8,128)S(1)}, f32[52,16,128]{2,1,0:T(8,128)S(1)}, u32[]{:S(2)}, u32[]{:S(2)}) collective-permute-start(f32[52,16,128]{2,1,0:T(8,128)S(1)} %collective-permute-done.22.refs_8_), channel_id=1, source_target_pairs={{0,16},{1,17},{2,18},{3,19},{4,20},{5,21},{6,22},{7,23},{8,24},{9,... | collective-permute-start | bytes 1277960 | tf_op jit(solution)/shard_map/ppermute | solution.py:283
  69.8 36.5 %collective-permute-start.27 = (f32[52,16,128]{2,1,0:T(8,128)S(1)}, f32[52,16,128]{2,1,0:T(8,128)S(1)}, u32[]{:S(2)}, u32[]{:S(2)}) collective-permute-start(f32[52,16,128]{2,1,0:T(8,128)S(1)} %collective-permute-done.24.refs_10_), channel_id=1, source_target_pairs={{0,16},{1,17},{2,18},{3,19},{4,20},{5,21},{6,22},{7,23},{8,24},{9,... | collective-permute-start | bytes 1277960 | tf_op jit(solution)/shard_map/ppermute | solution.py:283
  72.7 33.5 %collective-permute-start.28 = (f32[52,16,128]{2,1,0:T(8,128)S(1)}, f32[52,16,128]{2,1,0:T(8,128)S(1)}, u32[]{:S(2)}, u32[]{:S(2)}) collective-permute-start(f32[52,16,128]{2,1,0:T(8,128)S(1)} %collective-permute-done.24.refs_10_), channel_id=1, source_target_pairs={{0,32},{1,33},{2,34},{3,35},{4,36},{5,37},{6,38},{7,39},{8,40},{9,... | collective-permute-start | bytes 1277960 | tf_op jit(solution)/shard_map/ppermute | solution.py:283
  78.8 44.3 %collective-permute-start.29 = (f32[52,16,128]{2,1,0:T(8,128)S(1)}, f32[52,16,128]{2,1,0:T(8,128)S(1)}, u32[]{:S(2)}, u32[]{:S(2)}) collective-permute-start(f32[52,16,128]{2,1,0:T(8,128)S(1)} %collective-permute-done.26.refs_12_), channel_id=1, source_target_pairs={{0,224},{1,225},{2,226},{3,227},{4,228},{5,229},{6,230},{7,231},{8... | collective-permute-start | bytes 1277960 | tf_op jit(solution)/shard_map/ppermute | solution.py:283
  87.9 38.0 %collective-permute-start.5 = (f32[27,16,128]{2,1,0:T(8,128)S(1)}, f32[27,16,128]{2,1,0:T(8,128)S(1)}, u32[]{:S(2)}, u32[]{:S(2)}) collective-permute-start(f32[27,16,128]{2,1,0:T(8,128)S(1)} %collective-permute-done.4.refs_8_), channel_id=1, source_target_pairs={{0,224},{1,225},{2,226},{3,227},{4,228},{5,229},{6,230},{7,231},{8... | collective-permute-start | bytes 663560 | tf_op jit(solution)/shard_map/ppermute | solution.py:283
  97.1 28.9 %collective-permute-start.12 = (f32[27,16,128]{2,1,0:T(8,128)S(1)}, f32[27,16,128]{2,1,0:T(8,128)S(1)}, u32[]{:S(2)}, u32[]{:S(2)}) collective-permute-start(f32[27,16,128]{2,1,0:T(8,128)S(1)} %collective-permute-done.11.refs_7_), channel_id=1, source_target_pairs={{0,32},{1,33},{2,34},{3,35},{4,36},{5,37},{6,38},{7,39},{8,40},{9,... | collective-permute-start | bytes 663560 | tf_op jit(solution)/shard_map/ppermute | solution.py:283
  106.2 19.8 %collective-permute-start.13 = (f32[27,16,128]{2,1,0:T(8,128)S(1)}, f32[27,16,128]{2,1,0:T(8,128)S(1)}, u32[]{:S(2)}, u32[]{:S(2)}) collective-permute-start(f32[27,16,128]{2,1,0:T(8,128)S(1)} %collective-permute-done.2.refs_1_), channel_id=1, source_target_pairs={{0,32},{1,33},{2,34},{3,35},{4,36},{5,37},{6,38},{7,39},{8,40},{9,... | collective-permute-start | bytes 663560 | tf_op jit(solution)/shard_map/ppermute | solution.py:283
  106.2 19.8 %collective-permute-start.14 = (f32[27,16,128]{2,1,0:T(8,128)S(1)}, f32[27,16,128]{2,1,0:T(8,128)S(1)}, u32[]{:S(2)}, u32[]{:S(2)}) collective-permute-start(f32[27,16,128]{2,1,0:T(8,128)S(1)} %collective-permute-done.9.refs_3_), channel_id=1, source_target_pairs={{0,224},{1,225},{2,226},{3,227},{4,228},{5,229},{6,230},{7,231},{8... | collective-permute-start | bytes 663560 | tf_op jit(solution)/shard_map/ppermute | solution.py:283
  125.9 8.4 %copy-start.2 = (f32[64]{0:T(128)S(1)}, f32[64]{0:T(128)}, u32[]{:S(2)}) copy-start(f32[64]{0:T(128)} %param.9) | copy-start | bytes 772
  125.9 14.6 %copy-start.1 = (f32[1,16,4,64]{3,2,1,0:T(4,128)S(1)}, f32[1,16,4,64]{3,2,1,0:T(4,128)}, u32[]{:S(2)}) copy-start(f32[1,16,4,64]{3,2,1,0:T(4,128)} %param.7) | copy-start | bytes 49156
  126.0 14.7 %copy-start.3 = (f32[16]{0:T(128)S(1)}, f32[16]{0:T(128)}, u32[]{:S(2)}) copy-start(f32[16]{0:T(128)} %param.8) | copy-start | bytes 196
  127.9 7.5 %collective-permute-start.30 = (f32[8,32,256]{2,1,0:T(8,128)S(1)}, f32[8,32,256]{2,1,0:T(8,128)S(1)}, u32[]{:S(2)}, u32[]{:S(2)}) collective-permute-start(f32[8,32,256]{2,1,0:T(8,128)S(1)} %get-tuple-element.22), channel_id=1, source_target_pairs={{0,1},{1,0},{2,3},{3,2},{4,5},{5,4},{6,7},{7,6},{8,9},{9,8},{10,11... | collective-permute-start | bytes 786440 | tf_op jit(solution)/shard_map/ppermute | solution.py:283
  136.2 10.1 %all-to-all-start = ((f32[8,32,256]{2,1,0:T(8,128)}), f32[8,32,256]{2,1,0:T(8,128)S(1)}, u32[]{:S(2)}, u32[]{:S(2)}) async-start(f32[8,32,256]{2,1,0:T(8,128)} %add.31), calls=%async_computation | async-start | bytes 524288 | tf_op jit(solution)/shard_map/all_to_all | solution.py:326
  147.2 13.8 %all-to-all-start.1 = ((f32[16,8,128]{2,1,0:T(8,128)}), f32[16,8,128]{2,1,0:T(8,128)S(1)}, u32[]{:S(2)}, u32[]{:S(2)}) async-start(f32[16,8,128]{2,1,0:T(8,128)} %get-tuple-element.24), calls=%async_computation.1 | async-start | bytes 131072 | tf_op jit(solution)/shard_map/all_to_all | solution.py:330

commit v4 on v3

--- a/solution.py
+++ b/solution.py
@@ -184,8 +184,8 @@
         for m in range(NC // 2):
             k = 2 * m + (core ^ other)
             for ref, lanes in ((left, slice(0, LANES)), (right, slice(LANES, NAB))):
-                out[m, :NJ, lanes] = ref[pl.ds(pl.multiple_of(k * NJ, NJ), NJ), :]
-                out[m, NJ:, lanes] = ref[pl.ds(k, NJ, stride=NJ), :]
+                out[(m - FIRST_CHIP) % 8, :NJ, lanes] = ref[pl.ds(pl.multiple_of(k * NJ, NJ), NJ), :]
+                out[(m - FIRST_CHIP) % 8, NJ:, lanes] = ref[pl.ds(k, NJ, stride=NJ), :]
 
 
 def last(at, where, blocks, vh, vl, pa1, pa2, pb):
@@ -222,7 +222,7 @@
     zeros = jnp.zeros((8, LANES - 32), F32)
     for r in range(NR):
         lanes = slice(16 * r, 16 * (r + 1))
-        e_ref[r] = jnp.concatenate([mixed[:8, lanes], mixed[8:, lanes], zeros], axis=-1)
+        e_ref[(r - FIRST_ROW) % NR] = jnp.concatenate([mixed[:8, lanes], mixed[8:, lanes], zeros], axis=-1)
 
 
 def fold(r):
@@ -238,7 +238,7 @@
 
 def finish_kernel(d_ref, m_ref, rest_ref, den_ref, out_ref):
     halves = [
-        jnp.concatenate([m_ref[r, :, 16 * h : 16 * (h + 1)] for r in range(NR)], axis=-1)
+        jnp.concatenate([m_ref[(r - FIRST_ROW) % NR, :, 16 * h : 16 * (h + 1)] for r in range(NR)], axis=-1)
         for h in range(2)
     ]
     mirror = permute_lanes(
@@ -276,7 +276,10 @@
 
 UP, DOWN, ACROSS = moves(dz=1), moves(dz=-1), moves(dy=1)
 OTHER_CORE = [(i, i ^ 1) for i in range(NR * NC)]
-SAME_CORE = [[r * NC + 2 * m + core for m in range(NC // 2)] for r in range(NR) for core in range(2)]
+FIRST_ROW = 9
+SAME_COLUMN = [[(FIRST_ROW + m) % NR * NC + k for m in range(NR)] for k in range(NC)]
+FIRST_CHIP = 5
+SAME_CORE = [[r * NC + (FIRST_CHIP + m) % 8 * 2 + core for m in range(NC // 2)] for r in range(NR) for core in range(2)]
 
 
 def send(x, where):
@@ -327,7 +330,7 @@
         partial, AXES, 0, 0, axis_index_groups=SAME_CORE, tiled=True
     )
     direct, messages = fold(received)
-    mirror = lax.all_to_all(messages, "row", 0, 0, tiled=True)
+    mirror = lax.all_to_all(messages, AXES, 0, 0, axis_index_groups=SAME_COLUMN, tiled=True)
 
     vir_local = lax.dynamic_slice_in_dim(vir_energy, row * 4, 4, 0)
     occ_local = lax.dynamic_slice_in_dim(occ_energy, col, 1, 0)

time: 163 us -> 161 us (0.988)
  waiting for transfers between devices: 94.1 us -> 85.4 us
  starting transfers between devices: 42.6 us -> 49.3 us
    all_to_all x1, waiting for transfers between devices: 9.33 us -> 2.36 us  [on_device(): lax.all_to_all(messages, AXES, 0, 0, axis_index_groups=SAME_COLUMN, tiled...]
    all_to_all x1, starting transfers between devices: 4.37 us -> 9.07 us  [on_device(): lax.all_to_all(messages, AXES, 0, 0, axis_index_groups=SAME_COLUMN, tiled...]
    all_to_all x1, starting transfers between devices: 4.13 us -> 6.18 us  [on_device(): lax.all_to_all(partial, AXES, 0, 0, axis_index_groups=SAME_CORE, tiled=True)]
    all_to_all x1, waiting for transfers between devices: 4.35 us -> 2.63 us  [on_device(): lax.all_to_all(partial, AXES, 0, 0, axis_index_groups=SAME_CORE, tiled=True)]
  transfers between devices with their start and end apart: 33 -> 33, of which waited for: 17 -> 17; matrix products, arithmetic and copies ran while one was open for 1% -> 1% of each run, Pallas kernels for 10% -> 11%
where the time goes in v4:
time: 161 us; the launch traced here: 160 us
  waiting for transfers between devices  85.4 us (53%)
  starting transfers between devices  49.3 us (31%)
  Pallas kernels  21.4 us (13%)
  local copies, waits for them, and re-layouts  2.16 us (1%)
    ppermute x31, waiting for transfers between devices, send(): return lax.ppermute(x, AXES, where)  80.4 us
    ppermute x31, starting transfers between devices, send(): return lax.ppermute(x, AXES, where)  34.1 us
    all_to_all x1, starting transfers between devices, on_device(): lax.all_to_all(messages, AXES, 0, 0, axis_index_groups=SAME_COLUMN, tiled...  9.07 us
    pallas_call x3, Pallas kernels, dot(): pl.pallas_call(kernel, in_specs=[VMEM] * len(args), out_specs=VMEM, out_s...  7.59 us
    pallas_call x1, Pallas kernels, pack_va(): pl.pallas_call(pack_va_kernel, grid=(2, 4), in_specs=[pl.BlockSpec((None,...  6.18 us
    all_to_all x1, starting transfers between devices, on_device(): lax.all_to_all(partial, AXES, 0, 0, axis_index_groups=SAME_CORE, tiled=True)  6.18 us
    pallas_call x1, Pallas kernels, pack_vb(): pl.pallas_call(pack_vb_kernel, grid=(4,), in_specs=[pl.BlockSpec((None, 8...  3.23 us
  transfers between devices with their start and end apart: 33, of which 17 were waited for; matrix products, arithmetic and copies ran while one was open for 1% of the time, Pallas kernels for 11%

profile of v4, /device:TPU:1, one launch (start us, length us, event | category | flops | bytes accessed | tf_op | source)
XLA Modules:
  0.0 159.9 jit_solution(2410503704310140656)
XLA Ops:
  0.0 0.1 pad_add_fusion.at_ref.refs_0_
  0.1 1.1 copy-done
  1.2 0.7 pack_t.1
  1.9 6.5 %collective-permute-start.18 = (f32[52,16,128]{2,1,0:T(8,128)S(1)}, f32[52,16,128]{2,1,0:T(8,128)S(1)}, u32[]{:S(2)}, u32[]{:S(2)}) collective-permute-start(f32[52,16,128]{2,1,0:T(8,128)S(1)} %get-tuple-element.18.refs_0_), channel_id=1, source_target_pairs={{0,224},{1,225},{2,226},{3,227},{4,228},{5,229},{6,230},{7,231},{8... | collective-permute-start | bytes 1277960 | tf_op jit(solution)/shard_map/ppermute | solution.py:286
  8.3 2.9 %collective-permute-start.6 = (f32[27,16,128]{2,1,0:T(8,128)S(1)}, f32[27,16,128]{2,1,0:T(8,128)S(1)}, u32[]{:S(2)}, u32[]{:S(2)}) collective-permute-start(f32[27,16,128]{2,1,0:T(8,128)S(1)} %get-tuple-element.15.refs_0_), channel_id=1, source_target_pairs={{0,16},{1,17},{2,18},{3,19},{4,20},{5,21},{6,22},{7,23},{8,24},{9,... | collective-permute-start | bytes 663560 | tf_op jit(solution)/shard_map/ppermute | solution.py:286
  11.3 0.1 collective-permute-start.15
  11.3 0.0 collective-permute-start
  11.3 4.6 %collective-permute-done.6.refs_1_ = f32[27,16,128]{2,1,0:T(8,128)S(1)} collective-permute-done((f32[27,16,128]{2,1,0:T(8,128)S(1)}, f32[27,16,128]{2,1,0:T(8,128)S(1)}, u32[]{:S(2)}, u32[]{:S(2)}) %collective-permute-start.6) | collective-permute-done | bytes 221216 | tf_op jit(solution)/shard_map/ppermute | solution.py:286
  15.9 0.7 collective-permute-start.3
  16.6 0.2 collective-permute-done.18.refs_4_
  16.8 3.4 %collective-permute-start.22 = (f32[52,16,128]{2,1,0:T(8,128)S(1)}, f32[52,16,128]{2,1,0:T(8,128)S(1)}, u32[]{:S(2)}, u32[]{:S(2)}) collective-permute-start(f32[52,16,128]{2,1,0:T(8,128)S(1)} %collective-permute-done.18.refs_4_), channel_id=1, source_target_pairs={{0,224},{1,225},{2,226},{3,227},{4,228},{5,229},{6,230},{7,231},{8... | collective-permute-start | bytes 1277960 | tf_op jit(solution)/shard_map/ppermute | solution.py:286
  20.3 7.1 %collective-permute-done.refs_2_ = f32[27,16,128]{2,1,0:T(8,128)S(1)} collective-permute-done((f32[27,16,128]{2,1,0:T(8,128)S(1)}, f32[27,16,128]{2,1,0:T(8,128)S(1)}, u32[]{:S(2)}, u32[]{:S(2)}) %collective-permute-start) | collective-permute-done | bytes 221216 | tf_op jit(solution)/shard_map/ppermute | solution.py:286
  27.3 0.0 collective-permute-start.10
  27.4 0.0 collective-permute-done.3.refs_4_
  27.4 2.7 %collective-permute-start.7 = (f32[27,16,128]{2,1,0:T(8,128)S(1)}, f32[27,16,128]{2,1,0:T(8,128)S(1)}, u32[]{:S(2)}, u32[]{:S(2)}) collective-permute-start(f32[27,16,128]{2,1,0:T(8,128)S(1)} %collective-permute-done.6.refs_1_), channel_id=1, source_target_pairs={{0,224},{1,225},{2,226},{3,227},{4,228},{5,229},{6,230},{7,231},{8... | collective-permute-start | bytes 663560 | tf_op jit(solution)/shard_map/ppermute | solution.py:286
  30.0 0.0 collective-permute-done.16.refs_2_
  30.0 0.1 collective-permute-start.20
  30.1 3.2 %collective-permute-done.10.refs_3_ = f32[27,16,128]{2,1,0:T(8,128)S(1)} collective-permute-done((f32[27,16,128]{2,1,0:T(8,128)S(1)}, f32[27,16,128]{2,1,0:T(8,128)S(1)}, u32[]{:S(2)}, u32[]{:S(2)}) %collective-permute-start.10) | collective-permute-done | bytes 221216 | tf_op jit(solution)/shard_map/ppermute | solution.py:286
  33.3 1.7 %collective-permute-done.7.refs_5_ = f32[27,16,128]{2,1,0:T(8,128)S(1)} collective-permute-done((f32[27,16,128]{2,1,0:T(8,128)S(1)}, f32[27,16,128]{2,1,0:T(8,128)S(1)}, u32[]{:S(2)}, u32[]{:S(2)}) %collective-permute-start.7) | collective-permute-done | bytes 221216 | tf_op jit(solution)/shard_map/ppermute | solution.py:286
  35.1 3.6 %collective-permute-done.1.refs_6_ = f32[27,16,128]{2,1,0:T(8,128)S(1)} collective-permute-done((f32[27,16,128]{2,1,0:T(8,128)S(1)}, f32[27,16,128]{2,1,0:T(8,128)S(1)}, u32[]{:S(2)}, u32[]{:S(2)}) %collective-permute-start.1) | collective-permute-done | bytes 221216 | tf_op jit(solution)/shard_map/ppermute | solution.py:286
  38.7 1.3 collective-permute-start.25
  40.0 0.3 collective-permute-start.2
  40.2 12.3 %collective-permute-done.11.refs_7_ = f32[27,16,128]{2,1,0:T(8,128)S(1)} collective-permute-done((f32[27,16,128]{2,1,0:T(8,128)S(1)}, f32[27,16,128]{2,1,0:T(8,128)S(1)}, u32[]{:S(2)}, u32[]{:S(2)}) %collective-permute-start.11) | collective-permute-done | bytes 221216 | tf_op jit(solution)/shard_map/ppermute | solution.py:286
  52.6 0.1 collective-permute-start.17
  52.6 2.9 %collective-permute-start.19 = (f32[52,16,128]{2,1,0:T(8,128)S(1)}, f32[52,16,128]{2,1,0:T(8,128)S(1)}, u32[]{:S(2)}, u32[]{:S(2)}) collective-permute-start(f32[52,16,128]{2,1,0:T(8,128)S(1)} %collective-permute-done.18.refs_4_), channel_id=1, source_target_pairs={{0,16},{1,17},{2,18},{3,19},{4,20},{5,21},{6,22},{7,23},{8,24},{9,... | collective-permute-start | bytes 1277960 | tf_op jit(solution)/shard_map/ppermute | solution.py:286
  55.5 1.8 %collective-permute-done.2.refs_1_ = f32[27,16,128]{2,1,0:T(8,128)S(1)} collective-permute-done((f32[27,16,128]{2,1,0:T(8,128)S(1)}, f32[27,16,128]{2,1,0:T(8,128)S(1)}, u32[]{:S(2)}, u32[]{:S(2)}) %collective-permute-start.2) | collective-permute-done | bytes 221216 | tf_op jit(solution)/shard_map/ppermute | solution.py:286
  57.3 0.9 collective-permute-start.9
  58.2 0.1 collective-permute-start.26
  58.3 2.7 %collective-permute-done.17.refs_3_ = f32[52,16,128]{2,1,0:T(8,128)S(1)} collective-permute-done((f32[52,16,128]{2,1,0:T(8,128)S(1)}, f32[52,16,128]{2,1,0:T(8,128)S(1)}, u32[]{:S(2)}, u32[]{:S(2)}) %collective-permute-start.17) | collective-permute-done | bytes 426016 | tf_op jit(solution)/shard_map/ppermute | solution.py:286
  61.0 0.2 collective-permute-start.21
  61.2 8.5 %collective-permute-done.19.refs_5_ = f32[52,16,128]{2,1,0:T(8,128)S(1)} collective-permute-done((f32[52,16,128]{2,1,0:T(8,128)S(1)}, f32[52,16,128]{2,1,0:T(8,128)S(1)}, u32[]{:S(2)}, u32[]{:S(2)}) %collective-permute-start.19) | collective-permute-done | bytes 426016 | tf_op jit(solution)/shard_map/ppermute | solution.py:286
  69.7 0.1 collective-permute-start.23
  69.8 2.9 %collective-permute-start.27 = (f32[52,16,128]{2,1,0:T(8,128)S(1)}, f32[52,16,128]{2,1,0:T(8,128)S(1)}, u32[]{:S(2)}, u32[]{:S(2)}) collective-permute-start(f32[52,16,128]{2,1,0:T(8,128)S(1)} %collective-permute-done.24.refs_10_), channel_id=1, source_target_pairs={{0,16},{1,17},{2,18},{3,19},{4,20},{5,21},{6,22},{7,23},{8,24},{9,... | collective-permute-start | bytes 1277960 | tf_op jit(solution)/shard_map/ppermute | solution.py:286
  72.7 6.1 %collective-permute-done.26.refs_12_ = f32[52,16,128]{2,1,0:T(8,128)S(1)} collective-permute-done((f32[52,16,128]{2,1,0:T(8,128)S(1)}, f32[52,16,128]{2,1,0:T(8,128)S(1)}, u32[]{:S(2)}, u32[]{:S(2)}) %collective-permute-start.26) | collective-permute-done | bytes 426016 | tf_op jit(solution)/shard_map/ppermute | solution.py:286
  78.8 9.1 %collective-permute-done.21.refs_7_ = f32[52,16,128]{2,1,0:T(8,128)S(1)} collective-permute-done((f32[52,16,128]{2,1,0:T(8,128)S(1)}, f32[52,16,128]{2,1,0:T(8,128)S(1)}, u32[]{:S(2)}, u32[]{:S(2)}) %collective-permute-start.21) | collective-permute-done | bytes 426016 | tf_op jit(solution)/shard_map/ppermute | solution.py:286
  88.0 9.1 %collective-permute-done.23.refs_9_ = f32[52,16,128]{2,1,0:T(8,128)S(1)} collective-permute-done((f32[52,16,128]{2,1,0:T(8,128)S(1)}, f32[52,16,128]{2,1,0:T(8,128)S(1)}, u32[]{:S(2)}, u32[]{:S(2)}) %collective-permute-start.23) | collective-permute-done | bytes 426016 | tf_op jit(solution)/shard_map/ppermute | solution.py:286
  97.1 9.1 %collective-permute-done.27.refs_0_ = f32[52,16,128]{2,1,0:T(8,128)S(1)} collective-permute-done((f32[52,16,128]{2,1,0:T(8,128)S(1)}, f32[52,16,128]{2,1,0:T(8,128)S(1)}, u32[]{:S(2)}, u32[]{:S(2)}) %collective-permute-start.27) | collective-permute-done | bytes 426016 | tf_op jit(solution)/shard_map/ppermute | solution.py:286
  106.2 2.7 %collective-permute-start.14 = (f32[27,16,128]{2,1,0:T(8,128)S(1)}, f32[27,16,128]{2,1,0:T(8,128)S(1)}, u32[]{:S(2)}, u32[]{:S(2)}) collective-permute-start(f32[27,16,128]{2,1,0:T(8,128)S(1)} %collective-permute-done.9.refs_3_), channel_id=1, source_target_pairs={{0,224},{1,225},{2,226},{3,227},{4,228},{5,229},{6,230},{7,231},{8... | collective-permute-start | bytes 663560 | tf_op jit(solution)/shard_map/ppermute | solution.py:286
  108.9 6.2 %pack_va.1 = (bf16[52,256,128]{2,1,0:T(8,128)(2,1)S(1)}, bf16[52,256,128]{2,1,0:T(8,128)(2,1)S(1)}) custom-call(f32[4,25,64,400]{3,2,1,0:T(8,128)} %bitcast.9, f32[4,25,64,400]{3,2,1,0:T(8,128)} %bitcast.10), custom_call_target="tpu_custom_call" | custom-call | tf_op jit(solution)/shard_map/pack_va/pallas_call | solution.py:97
  115.1 3.2 %pack_vb.1 = (bf16[27,256,128]{2,1,0:T(8,128)(2,1)S(1)}, bf16[27,256,128]{2,1,0:T(8,128)(2,1)S(1)}) custom-call(f32[4,25,64,400]{3,2,1,0:T(8,128)} %bitcast.11, f32[4,25,64,400]{3,2,1,0:T(8,128)} %bitcast.12), custom_call_target="tpu_custom_call" | custom-call | tf_op jit(solution)/shard_map/pack_vb/pallas_call | solution.py:113
  118.3 1.3 shard_map.57.refs_11_
  119.6 3.5 %shard_map.55.refs_9_ = f32[208,256]{1,0:T(8,128)S(1)} custom-call(f32[52,16,128]{2,1,0:T(8,128)S(1)} %get-tuple-element.18.refs_0_, f32[52,16,128]{2,1,0:T(8,128)S(1)} %collective-permute-done.15.refs_1_, f32[52,16,128]{2,1,0:T(8,128)S(1)} %collective-permute-done.16.refs_2_, f32[52,16,128]{2,1,0:T(8,128)S(1)} %collective-permute-done.17.refs_3_, ...), custom_call_target="tpu_custom_call" | custom-call | tf_op jit(solution)/shard_map/pallas_call | solution.py:153
  123.2 2.8 %shard_map.56.refs_10_ = f32[48,256]{1,0:T(8,128)S(1)} custom-call(f32[52,16,128]{2,1,0:T(8,128)S(1)} %collective-permute-done.27.refs_0_, f32[52,16,128]{2,1,0:T(8,128)S(1)} %collective-permute-done.28.refs_1_, f32[52,16,128]{2,1,0:T(8,128)S(1)} %collective-permute-done.29.refs_2_, bf16[52,256,128]{2,1,0:T(8,128)(2,1)S(1)} %get-tuple-element.19.refs_13_.refs_3_, ...), custom_call_target="tpu_custom_call" | custom-call | tf_op jit(solution)/shard_map/pallas_call | solution.py:153
  125.9 0.0 copy-start.2
  125.9 0.0 copy-start.1
  126.0 0.0 copy-start.3
  126.0 1.9 %last.1 = (f32[8,32,256]{2,1,0:T(8,128)S(1)}, f32[8,32,256]{2,1,0:T(8,128)S(1)}) custom-call(s32[2]{0:T(128)S(1)} %pad_add_fusion.at_ref.refs_0_, f32[27,16,128]{2,1,0:T(8,128)S(1)} %collective-permute-done.2.refs_1_, f32[27,16,128]{2,1,0:T(8,128)S(1)} %collective-permute-done.5.refs_2_, f32[27,16,128]{2,1,0:T(8,128)S(1)} %collective-permute-done.9.refs_3_, ...), custom_call_target="tpu_custom_call" | custom-call | tf_op jit(solution)/shard_map/last/pallas_call | solution.py:194
  127.9 6.4 %collective-permute-start.30 = (f32[8,32,256]{2,1,0:T(8,128)S(1)}, f32[8,32,256]{2,1,0:T(8,128)S(1)}, u32[]{:S(2)}, u32[]{:S(2)}) collective-permute-start(f32[8,32,256]{2,1,0:T(8,128)S(1)} %get-tuple-element.22), channel_id=1, source_target_pairs={{0,1},{1,0},{2,3},{3,2},{4,5},{5,4},{6,7},{7,6},{8,9},{9,8},{10,11... | collective-permute-start | bytes 786440 | tf_op jit(solution)/shard_map/ppermute | solution.py:286
  134.3 0.1 dynamic_slice.6
  134.4 1.1 collective-permute-done.30
  135.5 0.7 add.31
  136.2 6.2 %all-to-all-start = ((f32[8,32,256]{2,1,0:T(8,128)}), f32[8,32,256]{2,1,0:T(8,128)S(1)}, u32[]{:S(2)}, u32[]{:S(2)}) async-start(f32[8,32,256]{2,1,0:T(8,128)} %add.31), calls=%async_computation | async-start | bytes 524288 | tf_op jit(solution)/shard_map/all_to_all | solution.py:329
  142.4 0.1 broadcast_reduce_fusion
  142.5 0.1 add.34
  142.6 0.1 add.36
  142.6 0.1 reshape.40.rest_ref
  142.7 0.6 dynamic_slice.7
  143.3 0.6 add_subtract_fusion
  144.0 2.6 %all-to-all-done.r_ref = f32[8,32,256]{2,1,0:T(8,128)S(1)} async-done(((f32[8,32,256]{2,1,0:T(8,128)}), f32[8,32,256]{2,1,0:T(8,128)S(1)}, u32[]{:S(2)}, u32[]{:S(2)}) %all-to-all-start) | async-done | bytes 262176 | tf_op jit(solution)/shard_map/all_to_all | solution.py:329
  146.6 0.9 fold.1
  147.5 9.1 %all-to-all-start.1 = ((f32[16,8,128]{2,1,0:T(8,128)}), f32[16,8,128]{2,1,0:T(8,128)S(1)}, u32[]{:S(2)}, u32[]{:S(2)}) async-start(f32[16,8,128]{2,1,0:T(8,128)} %get-tuple-element.24), calls=%async_computation.1 | async-start | bytes 131072 | tf_op jit(solution)/shard_map/all_to_all | solution.py:333
  156.6 0.1 broadcast_subtract_fusion.den_ref
  156.6 2.4 %all-to-all-done.1.m_ref = f32[16,8,128]{2,1,0:T(8,128)S(1)} async-done(((f32[16,8,128]{2,1,0:T(8,128)}), f32[16,8,128]{2,1,0:T(8,128)S(1)}, u32[]{:S(2)}, u32[]{:S(2)}) %all-to-all-start.1) | async-done | bytes 65568 | tf_op jit(solution)/shard_map/all_to_all | solution.py:333
  159.0 0.9 finish.1
  (30 shorter events, 0.1 us)
Async XLA Ops:
  0.1 1.1 copy-start
  1.9 15.0 %collective-permute-start.18 = (f32[52,16,128]{2,1,0:T(8,128)S(1)}, f32[52,16,128]{2,1,0:T(8,128)S(1)}, u32[]{:S(2)}, u32[]{:S(2)}) collective-permute-start(f32[52,16,128]{2,1,0:T(8,128)S(1)} %get-tuple-element.18.refs_0_), channel_id=1, source_target_pairs={{0,224},{1,225},{2,226},{3,227},{4,228},{5,229},{6,230},{7,231},{8... | collective-permute-start | bytes 1277960 | tf_op jit(solution)/shard_map/ppermute | solution.py:286
  8.3 7.5 %collective-permute-start.6 = (f32[27,16,128]{2,1,0:T(8,128)S(1)}, f32[27,16,128]{2,1,0:T(8,128)S(1)}, u32[]{:S(2)}, u32[]{:S(2)}) collective-permute-start(f32[27,16,128]{2,1,0:T(8,128)S(1)} %get-tuple-element.15.refs_0_), channel_id=1, source_target_pairs={{0,16},{1,17},{2,18},{3,19},{4,20},{5,21},{6,22},{7,23},{8,24},{9,... | collective-permute-start | bytes 663560 | tf_op jit(solution)/shard_map/ppermute | solution.py:286
  11.3 18.8 %collective-permute-start.16 = (f32[52,16,128]{2,1,0:T(8,128)S(1)}, f32[52,16,128]{2,1,0:T(8,128)S(1)}, u32[]{:S(2)}, u32[]{:S(2)}) collective-permute-start(f32[52,16,128]{2,1,0:T(8,128)S(1)} %get-tuple-element.18.refs_0_), channel_id=1, source_target_pairs={{0,32},{1,33},{2,34},{3,35},{4,36},{5,37},{6,38},{7,39},{8,40},{9,... | collective-permute-start | bytes 1277960 | tf_op jit(solution)/shard_map/ppermute | solution.py:286
  11.3 18.8 %collective-permute-start.15 = (f32[52,16,128]{2,1,0:T(8,128)S(1)}, f32[52,16,128]{2,1,0:T(8,128)S(1)}, u32[]{:S(2)}, u32[]{:S(2)}) collective-permute-start(f32[52,16,128]{2,1,0:T(8,128)S(1)} %get-tuple-element.18.refs_0_), channel_id=1, source_target_pairs={{0,16},{1,17},{2,18},{3,19},{4,20},{5,21},{6,22},{7,23},{8,24},{9,... | collective-permute-start | bytes 1277960 | tf_op jit(solution)/shard_map/ppermute | solution.py:286
  11.3 16.0 %collective-permute-start = (f32[27,16,128]{2,1,0:T(8,128)S(1)}, f32[27,16,128]{2,1,0:T(8,128)S(1)}, u32[]{:S(2)}, u32[]{:S(2)}) collective-permute-start(f32[27,16,128]{2,1,0:T(8,128)S(1)} %get-tuple-element.15.refs_0_), channel_id=1, source_target_pairs={{0,32},{1,33},{2,34},{3,35},{4,36},{5,37},{6,38},{7,39},{8,40},{9,... | collective-permute-start | bytes 663560 | tf_op jit(solution)/shard_map/ppermute | solution.py:286
  15.9 11.5 %collective-permute-start.3 = (f32[27,16,128]{2,1,0:T(8,128)S(1)}, f32[27,16,128]{2,1,0:T(8,128)S(1)}, u32[]{:S(2)}, u32[]{:S(2)}) collective-permute-start(f32[27,16,128]{2,1,0:T(8,128)S(1)} %get-tuple-element.15.refs_0_), channel_id=1, source_target_pairs={{0,224},{1,225},{2,226},{3,227},{4,228},{5,229},{6,230},{7,231},{8... | collective-permute-start | bytes 663560 | tf_op jit(solution)/shard_map/ppermute | solution.py:286
  16.8 21.8 %collective-permute-start.22 = (f32[52,16,128]{2,1,0:T(8,128)S(1)}, f32[52,16,128]{2,1,0:T(8,128)S(1)}, u32[]{:S(2)}, u32[]{:S(2)}) collective-permute-start(f32[52,16,128]{2,1,0:T(8,128)S(1)} %collective-permute-done.18.refs_4_), channel_id=1, source_target_pairs={{0,224},{1,225},{2,226},{3,227},{4,228},{5,229},{6,230},{7,231},{8... | collective-permute-start | bytes 1277960 | tf_op jit(solution)/shard_map/ppermute | solution.py:286
  27.3 6.0 %collective-permute-start.10 = (f32[27,16,128]{2,1,0:T(8,128)S(1)}, f32[27,16,128]{2,1,0:T(8,128)S(1)}, u32[]{:S(2)}, u32[]{:S(2)}) collective-permute-start(f32[27,16,128]{2,1,0:T(8,128)S(1)} %collective-permute-done.6.refs_1_), channel_id=1, source_target_pairs={{0,32},{1,33},{2,34},{3,35},{4,36},{5,37},{6,38},{7,39},{8,40},{9,... | collective-permute-start | bytes 663560 | tf_op jit(solution)/shard_map/ppermute | solution.py:286
  27.4 7.7 %collective-permute-start.7 = (f32[27,16,128]{2,1,0:T(8,128)S(1)}, f32[27,16,128]{2,1,0:T(8,128)S(1)}, u32[]{:S(2)}, u32[]{:S(2)}) collective-permute-start(f32[27,16,128]{2,1,0:T(8,128)S(1)} %collective-permute-done.6.refs_1_), channel_id=1, source_target_pairs={{0,224},{1,225},{2,226},{3,227},{4,228},{5,229},{6,230},{7,231},{8... | collective-permute-start | bytes 663560 | tf_op jit(solution)/shard_map/ppermute | solution.py:286
  30.0 8.7 %collective-permute-start.1 = (f32[27,16,128]{2,1,0:T(8,128)S(1)}, f32[27,16,128]{2,1,0:T(8,128)S(1)}, u32[]{:S(2)}, u32[]{:S(2)}) collective-permute-start(f32[27,16,128]{2,1,0:T(8,128)S(1)} %collective-permute-done.refs_2_), channel_id=1, source_target_pairs={{0,32},{1,33},{2,34},{3,35},{4,36},{5,37},{6,38},{7,39},{8,40},{9,... | collective-permute-start | bytes 663560 | tf_op jit(solution)/shard_map/ppermute | solution.py:286
  30.0 25.5 %collective-permute-start.20 = (f32[52,16,128]{2,1,0:T(8,128)S(1)}, f32[52,16,128]{2,1,0:T(8,128)S(1)}, u32[]{:S(2)}, u32[]{:S(2)}) collective-permute-start(f32[52,16,128]{2,1,0:T(8,128)S(1)} %collective-permute-done.16.refs_2_), channel_id=1, source_target_pairs={{0,32},{1,33},{2,34},{3,35},{4,36},{5,37},{6,38},{7,39},{8,40},{9,... | collective-permute-start | bytes 1277960 | tf_op jit(solution)/shard_map/ppermute | solution.py:286
  33.3 6.6 %collective-permute-start.4 = (f32[27,16,128]{2,1,0:T(8,128)S(1)}, f32[27,16,128]{2,1,0:T(8,128)S(1)}, u32[]{:S(2)}, u32[]{:S(2)}) collective-permute-start(f32[27,16,128]{2,1,0:T(8,128)S(1)} %collective-permute-done.3.refs_4_), channel_id=1, source_target_pairs={{0,224},{1,225},{2,226},{3,227},{4,228},{5,229},{6,230},{7,231},{8... | collective-permute-start | bytes 663560 | tf_op jit(solution)/shard_map/ppermute | solution.py:286
  35.1 17.5 %collective-permute-start.11 = (f32[27,16,128]{2,1,0:T(8,128)S(1)}, f32[27,16,128]{2,1,0:T(8,128)S(1)}, u32[]{:S(2)}, u32[]{:S(2)}) collective-permute-start(f32[27,16,128]{2,1,0:T(8,128)S(1)} %collective-permute-done.10.refs_3_), channel_id=1, source_target_pairs={{0,32},{1,33},{2,34},{3,35},{4,36},{5,37},{6,38},{7,39},{8,40},{9,... | collective-permute-start | bytes 663560 | tf_op jit(solution)/shard_map/ppermute | solution.py:286
  38.7 13.9 %collective-permute-start.8 = (f32[27,16,128]{2,1,0:T(8,128)S(1)}, f32[27,16,128]{2,1,0:T(8,128)S(1)}, u32[]{:S(2)}, u32[]{:S(2)}) collective-permute-start(f32[27,16,128]{2,1,0:T(8,128)S(1)} %collective-permute-done.7.refs_5_), channel_id=1, source_target_pairs={{0,224},{1,225},{2,226},{3,227},{4,228},{5,229},{6,230},{7,231},{8... | collective-permute-start | bytes 663560 | tf_op jit(solution)/shard_map/ppermute | solution.py:286
  38.7 19.5 %collective-permute-start.25 = (f32[52,16,128]{2,1,0:T(8,128)S(1)}, f32[52,16,128]{2,1,0:T(8,128)S(1)}, u32[]{:S(2)}, u32[]{:S(2)}) collective-permute-start(f32[52,16,128]{2,1,0:T(8,128)S(1)} %collective-permute-done.22.refs_8_), channel_id=1, source_target_pairs={{0,224},{1,225},{2,226},{3,227},{4,228},{5,229},{6,230},{7,231},{8... | collective-permute-start | bytes 1277960 | tf_op jit(solution)/shard_map/ppermute | solution.py:286
  40.0 17.3 %collective-permute-start.2 = (f32[27,16,128]{2,1,0:T(8,128)S(1)}, f32[27,16,128]{2,1,0:T(8,128)S(1)}, u32[]{:S(2)}, u32[]{:S(2)}) collective-permute-start(f32[27,16,128]{2,1,0:T(8,128)S(1)} %collective-permute-done.1.refs_6_), channel_id=1, source_target_pairs={{0,32},{1,33},{2,34},{3,35},{4,36},{5,37},{6,38},{7,39},{8,40},{9,... | collective-permute-start | bytes 663560 | tf_op jit(solution)/shard_map/ppermute | solution.py:286
  52.6 8.5 %collective-permute-start.17 = (f32[52,16,128]{2,1,0:T(8,128)S(1)}, f32[52,16,128]{2,1,0:T(8,128)S(1)}, u32[]{:S(2)}, u32[]{:S(2)}) collective-permute-start(f32[52,16,128]{2,1,0:T(8,128)S(1)} %collective-permute-done.16.refs_2_), channel_id=1, source_target_pairs={{0,16},{1,17},{2,18},{3,19},{4,20},{5,21},{6,22},{7,23},{8,24},{9,... | collective-permute-start | bytes 1277960 | tf_op jit(solution)/shard_map/ppermute | solution.py:286
  52.6 17.1 %collective-permute-start.19 = (f32[52,16,128]{2,1,0:T(8,128)S(1)}, f32[52,16,128]{2,1,0:T(8,128)S(1)}, u32[]{:S(2)}, u32[]{:S(2)}) collective-permute-start(f32[52,16,128]{2,1,0:T(8,128)S(1)} %collective-permute-done.18.refs_4_), channel_id=1, source_target_pairs={{0,16},{1,17},{2,18},{3,19},{4,20},{5,21},{6,22},{7,23},{8,24},{9,... | collective-permute-start | bytes 1277960 | tf_op jit(solution)/shard_map/ppermute | solution.py:286
  55.5 14.2 %collective-permute-start.24 = (f32[52,16,128]{2,1,0:T(8,128)S(1)}, f32[52,16,128]{2,1,0:T(8,128)S(1)}, u32[]{:S(2)}, u32[]{:S(2)}) collective-permute-start(f32[52,16,128]{2,1,0:T(8,128)S(1)} %collective-permute-done.20.refs_6_), channel_id=1, source_target_pairs={{0,32},{1,33},{2,34},{3,35},{4,36},{5,37},{6,38},{7,39},{8,40},{9,... | collective-permute-start | bytes 1277960 | tf_op jit(solution)/shard_map/ppermute | solution.py:286
  57.3 15.4 %collective-permute-start.9 = (f32[27,16,128]{2,1,0:T(8,128)S(1)}, f32[27,16,128]{2,1,0:T(8,128)S(1)}, u32[]{:S(2)}, u32[]{:S(2)}) collective-permute-start(f32[27,16,128]{2,1,0:T(8,128)S(1)} %collective-permute-done.8.refs_9_), channel_id=1, source_target_pairs={{0,224},{1,225},{2,226},{3,227},{4,228},{5,229},{6,230},{7,231},{8... | collective-permute-start | bytes 663560 | tf_op jit(solution)/shard_map/ppermute | solution.py:286
  58.2 20.6 %collective-permute-start.26 = (f32[52,16,128]{2,1,0:T(8,128)S(1)}, f32[52,16,128]{2,1,0:T(8,128)S(1)}, u32[]{:S(2)}, u32[]{:S(2)}) collective-permute-start(f32[52,16,128]{2,1,0:T(8,128)S(1)} %collective-permute-done.25.refs_11_), channel_id=1, source_target_pairs={{0,16},{1,17},{2,18},{3,19},{4,20},{5,21},{6,22},{7,23},{8,24},{9,... | collective-permute-start | bytes 1277960 | tf_op jit(solution)/shard_map/ppermute | solution.py:286
  61.0 26.9 %collective-permute-start.21 = (f32[52,16,128]{2,1,0:T(8,128)S(1)}, f32[52,16,128]{2,1,0:T(8,128)S(1)}, u32[]{:S(2)}, u32[]{:S(2)}) collective-permute-start(f32[52,16,128]{2,1,0:T(8,128)S(1)} %collective-permute-done.20.refs_6_), channel_id=1, source_target_pairs={{0,16},{1,17},{2,18},{3,19},{4,20},{5,21},{6,22},{7,23},{8,24},{9,... | collective-permute-start | bytes 1277960 | tf_op jit(solution)/shard_map/ppermute | solution.py:286
  69.7 27.4 %collective-permute-start.23 = (f32[52,16,128]{2,1,0:T(8,128)S(1)}, f32[52,16,128]{2,1,0:T(8,128)S(1)}, u32[]{:S(2)}, u32[]{:S(2)}) collective-permute-start(f32[52,16,128]{2,1,0:T(8,128)S(1)} %collective-permute-done.22.refs_8_), channel_id=1, source_target_pairs={{0,16},{1,17},{2,18},{3,19},{4,20},{5,21},{6,22},{7,23},{8,24},{9,... | collective-permute-start | bytes 1277960 | tf_op jit(solution)/shard_map/ppermute | solution.py:286
  69.8 36.5 %collective-permute-start.27 = (f32[52,16,128]{2,1,0:T(8,128)S(1)}, f32[52,16,128]{2,1,0:T(8,128)S(1)}, u32[]{:S(2)}, u32[]{:S(2)}) collective-permute-start(f32[52,16,128]{2,1,0:T(8,128)S(1)} %collective-permute-done.24.refs_10_), channel_id=1, source_target_pairs={{0,16},{1,17},{2,18},{3,19},{4,20},{5,21},{6,22},{7,23},{8,24},{9,... | collective-permute-start | bytes 1277960 | tf_op jit(solution)/shard_map/ppermute | solution.py:286
  72.7 33.5 %collective-permute-start.28 = (f32[52,16,128]{2,1,0:T(8,128)S(1)}, f32[52,16,128]{2,1,0:T(8,128)S(1)}, u32[]{:S(2)}, u32[]{:S(2)}) collective-permute-start(f32[52,16,128]{2,1,0:T(8,128)S(1)} %collective-permute-done.24.refs_10_), channel_id=1, source_target_pairs={{0,32},{1,33},{2,34},{3,35},{4,36},{5,37},{6,38},{7,39},{8,40},{9,... | collective-permute-start | bytes 1277960 | tf_op jit(solution)/shard_map/ppermute | solution.py:286
  78.8 44.3 %collective-permute-start.29 = (f32[52,16,128]{2,1,0:T(8,128)S(1)}, f32[52,16,128]{2,1,0:T(8,128)S(1)}, u32[]{:S(2)}, u32[]{:S(2)}) collective-permute-start(f32[52,16,128]{2,1,0:T(8,128)S(1)} %collective-permute-done.26.refs_12_), channel_id=1, source_target_pairs={{0,224},{1,225},{2,226},{3,227},{4,228},{5,229},{6,230},{7,231},{8... | collective-permute-start | bytes 1277960 | tf_op jit(solution)/shard_map/ppermute | solution.py:286
  87.9 38.0 %collective-permute-start.5 = (f32[27,16,128]{2,1,0:T(8,128)S(1)}, f32[27,16,128]{2,1,0:T(8,128)S(1)}, u32[]{:S(2)}, u32[]{:S(2)}) collective-permute-start(f32[27,16,128]{2,1,0:T(8,128)S(1)} %collective-permute-done.4.refs_8_), channel_id=1, source_target_pairs={{0,224},{1,225},{2,226},{3,227},{4,228},{5,229},{6,230},{7,231},{8... | collective-permute-start | bytes 663560 | tf_op jit(solution)/shard_map/ppermute | solution.py:286
  97.1 28.9 %collective-permute-start.12 = (f32[27,16,128]{2,1,0:T(8,128)S(1)}, f32[27,16,128]{2,1,0:T(8,128)S(1)}, u32[]{:S(2)}, u32[]{:S(2)}) collective-permute-start(f32[27,16,128]{2,1,0:T(8,128)S(1)} %collective-permute-done.11.refs_7_), channel_id=1, source_target_pairs={{0,32},{1,33},{2,34},{3,35},{4,36},{5,37},{6,38},{7,39},{8,40},{9,... | collective-permute-start | bytes 663560 | tf_op jit(solution)/shard_map/ppermute | solution.py:286
  106.2 19.8 %collective-permute-start.13 = (f32[27,16,128]{2,1,0:T(8,128)S(1)}, f32[27,16,128]{2,1,0:T(8,128)S(1)}, u32[]{:S(2)}, u32[]{:S(2)}) collective-permute-start(f32[27,16,128]{2,1,0:T(8,128)S(1)} %collective-permute-done.2.refs_1_), channel_id=1, source_target_pairs={{0,32},{1,33},{2,34},{3,35},{4,36},{5,37},{6,38},{7,39},{8,40},{9,... | collective-permute-start | bytes 663560 | tf_op jit(solution)/shard_map/ppermute | solution.py:286
  106.2 19.8 %collective-permute-start.14 = (f32[27,16,128]{2,1,0:T(8,128)S(1)}, f32[27,16,128]{2,1,0:T(8,128)S(1)}, u32[]{:S(2)}, u32[]{:S(2)}) collective-permute-start(f32[27,16,128]{2,1,0:T(8,128)S(1)} %collective-permute-done.9.refs_3_), channel_id=1, source_target_pairs={{0,224},{1,225},{2,226},{3,227},{4,228},{5,229},{6,230},{7,231},{8... | collective-permute-start | bytes 663560 | tf_op jit(solution)/shard_map/ppermute | solution.py:286
  125.9 8.4 %copy-start.2 = (f32[64]{0:T(128)S(1)}, f32[64]{0:T(128)}, u32[]{:S(2)}) copy-start(f32[64]{0:T(128)} %param.9) | copy-start | bytes 772
  125.9 16.7 %copy-start.1 = (f32[1,16,4,64]{3,2,1,0:T(4,128)S(1)}, f32[1,16,4,64]{3,2,1,0:T(4,128)}, u32[]{:S(2)}) copy-start(f32[1,16,4,64]{3,2,1,0:T(4,128)} %param.7) | copy-start | bytes 49156
  126.0 16.8 %copy-start.3 = (f32[16]{0:T(128)S(1)}, f32[16]{0:T(128)}, u32[]{:S(2)}) copy-start(f32[16]{0:T(128)} %param.8) | copy-start | bytes 196
  127.9 7.5 %collective-permute-start.30 = (f32[8,32,256]{2,1,0:T(8,128)S(1)}, f32[8,32,256]{2,1,0:T(8,128)S(1)}, u32[]{:S(2)}, u32[]{:S(2)}) collective-permute-start(f32[8,32,256]{2,1,0:T(8,128)S(1)} %get-tuple-element.22), channel_id=1, source_target_pairs={{0,1},{1,0},{2,3},{3,2},{4,5},{5,4},{6,7},{7,6},{8,9},{9,8},{10,11... | collective-permute-start | bytes 786440 | tf_op jit(solution)/shard_map/ppermute | solution.py:286
  136.2 10.4 %all-to-all-start = ((f32[8,32,256]{2,1,0:T(8,128)}), f32[8,32,256]{2,1,0:T(8,128)S(1)}, u32[]{:S(2)}, u32[]{:S(2)}) async-start(f32[8,32,256]{2,1,0:T(8,128)} %add.31), calls=%async_computation | async-start | bytes 524288 | tf_op jit(solution)/shard_map/all_to_all | solution.py:329
  147.5 11.5 %all-to-all-start.1 = ((f32[16,8,128]{2,1,0:T(8,128)}), f32[16,8,128]{2,1,0:T(8,128)S(1)}, u32[]{:S(2)}, u32[]{:S(2)}) async-start(f32[16,8,128]{2,1,0:T(8,128)} %get-tuple-element.24), calls=%async_computation.1 | async-start | bytes 131072 | tf_op jit(solution)/shard_map/all_to_all | solution.py:333

commit v5 on v4

--- a/solution.py
+++ b/solution.py
@@ -141,11 +141,15 @@
     return total
 
 
+def product_a(refs, vh, vl):
+    step = lambda g: product(refs, vh, vl, g * 10, 10)
+    total = lax.fori_loop(1, TA // 10, lambda g, total: total + step(g), step(0))
+    return total + product(refs, vh, vl, 50, 2)
+
+
 def dot_a_kernel(*refs):
     *t_refs, vh, vl, out = refs
-    step = lambda g: product(t_refs, vh, vl, g * 10, 10)
-    total = lax.fori_loop(1, TA // 10, lambda g, total: total + step(g), step(0))
-    out[...] = total + product(t_refs, vh, vl, 50, 2)
+    out[...] = product_a(t_refs, vh, vl)
 
 
 def dot(kernel, blocks, vh, vl):
@@ -169,14 +173,16 @@
 
 
 def last_kernel(where, at_ref, *refs):
-    *t_refs, vh, vl, pa1, pa2, pb, keep, give, left, right = refs
-    new = product_b(t_refs, vh, vl)
+    *t_refs, vah, val, vbh, vbl, pa1, pb, keep, give, left, right = refs
+    n_late = len(where) - pa1.shape[0] // NJ
+    new_a = product_a(t_refs[:n_late], vah, val)
+    new_b = product_b(t_refs[n_late:], vbh, vbl)
     row, core = at_ref[0], at_ref[1] & 1
     n_a, n_b = pa1.shape[0] // NJ, pb.shape[0] // NJ
     part = lambda x, q: x[NJ * q : NJ * (q + 1), :]
     for q, (dz, dy) in enumerate(where):
-        block = part(pa1, q) if q < n_a else part(pa2, q - n_a)
-        block += part(pb, q) if q < n_b else part(new, q - n_b)
+        block = part(pa1, q) if q < n_a else part(new_a, q - n_a)
+        block += part(pb, q) if q < n_b else part(new_b, q - n_b)
         at = pl.ds(pl.multiple_of(absolute_row(row, dz, dy) * NJ, NJ), NJ)
         left[at, :] = block[:, :LANES]
         right[at, :] = block[:, LANES:]
@@ -188,9 +194,9 @@
                 out[(m - FIRST_CHIP) % 8, NJ:, lanes] = ref[pl.ds(k, NJ, stride=NJ), :]
 
 
-def last(at, where, blocks, vh, vl, pa1, pa2, pb):
+def last(at, where, blocks, v, pa1, pb):
     out = pltpu.VMEM((NC // 2, 2 * NJ, NAB), F32)
-    args = [on_chip(x) for x in (*blocks, vh, vl, pa1, pa2, pb)]
+    args = [on_chip(x) for x in (*blocks, *v, pa1, pb)]
     return pl.pallas_call(
         lambda *refs: last_kernel(where, *refs),
         in_specs=[pl.BlockSpec(memory_space=pltpu.SMEM)] + [VMEM] * len(args),
@@ -290,7 +296,8 @@
     row = lax.axis_index("row")
     col = lax.axis_index("col")
     at = jnp.stack([row, col])
-    a0, b0 = pack_t(at, jnp.transpose(amplitudes, (0, 2, 1, 3))[0])
+    t = jnp.transpose(amplitudes, (0, 2, 1, 3))[0]
+    a0, b0 = pack_t(at, pltpu.with_memory_space_constraint(t, pltpu.HBM))
     v = jnp.transpose(integrals, (0, 2, 1, 3))
     v = pltpu.with_memory_space_constraint(v, pltpu.HBM)
     vah, val = pack_va(v)
@@ -321,9 +328,9 @@
     b_all += [bu[3], bd[3], cd[3], cu[3], b4, c4]
     where += [(-3, 0), (3, 0), (3, 1), (-3, 1), (4, 0), (4, 1)]
     pa1 = dot(dot_a_kernel, a_all[:N_A], vah, val)
-    pa2 = dot(dot_a_kernel, a_all[N_A:], vah, val)
     pb = dot(dot_b_kernel, b_all[:N_B], vbh, vbl)
-    keep, give = last(at, where, b_all[N_B:], vbh, vbl, pa1, pa2, pb)
+    v_all = vah, val, vbh, vbl
+    keep, give = last(at, where, a_all[N_A:] + b_all[N_B:], v_all, pa1, pb)
 
     partial = keep + send(give, OTHER_CORE)
     received = lax.all_to_all(

time: 161 us -> 149 us (0.925)
  waiting for transfers between devices: 85.4 us -> 53.8 us
  starting transfers between devices: 49.3 us -> 69.5 us
    ppermute x31, waiting for transfers between devices: 80.4 us -> 48.8 us  [send(): return lax.ppermute(x, AXES, where)]
    ppermute x31, starting transfers between devices: 34.1 us -> 52.8 us  [send(): return lax.ppermute(x, AXES, where)]
    pallas_call x3 -> x2, Pallas kernels: 7.59 us -> 4.88 us  [dot(): pl.pallas_call(kernel, in_specs=[VMEM] * len(args), out_specs=VMEM, out_s...]
    pallas_call x1, Pallas kernels: 1.9 us -> 4.53 us  [last(): pl.pallas_call(lambda *refs: last_kernel(where, *refs), in_specs=[pl.Bloc...]
  transfers between devices with their start and end apart: 33 -> 33, of which waited for: 17 -> 16; matrix products, arithmetic and copies ran while one was open for 1% -> 1% of each run, Pallas kernels for 11% -> 10%
where the time goes in v5:
time: 149 us; the launch traced here: 148 us
  starting transfers between devices  69.5 us (47%)
  waiting for transfers between devices  53.8 us (36%)
  Pallas kernels  21.9 us (15%)
  other arithmetic  1.54 us (1%)
    ppermute x31, starting transfers between devices, send(): return lax.ppermute(x, AXES, where)  52.8 us
    ppermute x31, waiting for transfers between devices, send(): return lax.ppermute(x, AXES, where)  48.8 us
    all_to_all x1, starting transfers between devices, on_device(): lax.all_to_all(messages, AXES, 0, 0, axis_index_groups=SAME_COLUMN, tiled...  9.63 us
    all_to_all x1, starting transfers between devices, on_device(): lax.all_to_all(partial, AXES, 0, 0, axis_index_groups=SAME_CORE, tiled=True)  7.08 us
    pallas_call x1, Pallas kernels, pack_va(): pl.pallas_call(pack_va_kernel, grid=(2, 4), in_specs=[pl.BlockSpec((None,...  6.18 us
    pallas_call x2, Pallas kernels, dot(): pl.pallas_call(kernel, in_specs=[VMEM] * len(args), out_specs=VMEM, out_s...  4.88 us
    pallas_call x1, Pallas kernels, last(): pl.pallas_call(lambda *refs: last_kernel(where, *refs), in_specs=[pl.Bloc...  4.53 us
    pallas_call x1, Pallas kernels, pack_vb(): pl.pallas_call(pack_vb_kernel, grid=(4,), in_specs=[pl.BlockSpec((None, 8...  3.23 us
  transfers between devices with their start and end apart: 33, of which 16 were waited for; matrix products, arithmetic and copies ran while one was open for 1% of the time, Pallas kernels for 10%

profile of v5, /device:TPU:1, one launch (start us, length us, event | category | flops | bytes accessed | tf_op | source)
XLA Modules:
  0.0 147.9 jit_solution(1281495241715504966)
XLA Ops:
  0.0 0.1 pad_add_fusion.at_ref.refs_0_
  0.1 1.3 pack_t.1
  1.3 6.5 %collective-permute-start.5 = (f32[52,16,128]{2,1,0:T(8,128)S(1)}, f32[52,16,128]{2,1,0:T(8,128)S(1)}, u32[]{:S(2)}, u32[]{:S(2)}) collective-permute-start(f32[52,16,128]{2,1,0:T(8,128)S(1)} %get-tuple-element.15.refs_0_), channel_id=1, source_target_pairs={{0,224},{1,225},{2,226},{3,227},{4,228},{5,229},{6,230},{7,231},{8... | collective-permute-start | bytes 1277960 | tf_op jit(solution)/shard_map/ppermute | solution.py:292
  7.8 2.9 %collective-permute-start.16 = (f32[27,16,128]{2,1,0:T(8,128)S(1)}, f32[27,16,128]{2,1,0:T(8,128)S(1)}, u32[]{:S(2)}, u32[]{:S(2)}) collective-permute-start(f32[27,16,128]{2,1,0:T(8,128)S(1)} %get-tuple-element.16.refs_0_), channel_id=1, source_target_pairs={{0,16},{1,17},{2,18},{3,19},{4,20},{5,21},{6,22},{7,23},{8,24},{9,... | collective-permute-start | bytes 663560 | tf_op jit(solution)/shard_map/ppermute | solution.py:292
  10.7 0.0 collective-permute-start
  10.7 0.1 collective-permute-start.25
  10.8 0.0 collective-permute-start.10
  10.8 4.6 %collective-permute-done.16.refs_1_ = f32[27,16,128]{2,1,0:T(8,128)S(1)} collective-permute-done((f32[27,16,128]{2,1,0:T(8,128)S(1)}, f32[27,16,128]{2,1,0:T(8,128)S(1)}, u32[]{:S(2)}, u32[]{:S(2)}) %collective-permute-start.16) | collective-permute-done | bytes 221216 | tf_op jit(solution)/shard_map/ppermute | solution.py:292
  15.4 0.7 collective-permute-start.13
  16.1 0.2 collective-permute-done.5.refs_4_
  16.3 3.4 %collective-permute-start.6 = (f32[52,16,128]{2,1,0:T(8,128)S(1)}, f32[52,16,128]{2,1,0:T(8,128)S(1)}, u32[]{:S(2)}, u32[]{:S(2)}) collective-permute-start(f32[52,16,128]{2,1,0:T(8,128)S(1)} %collective-permute-done.5.refs_4_), channel_id=1, source_target_pairs={{0,224},{1,225},{2,226},{3,227},{4,228},{5,229},{6,230},{7,231},{8... | collective-permute-start | bytes 1277960 | tf_op jit(solution)/shard_map/ppermute | solution.py:292
  19.7 7.1 %collective-permute-done.10.refs_2_ = f32[27,16,128]{2,1,0:T(8,128)S(1)} collective-permute-done((f32[27,16,128]{2,1,0:T(8,128)S(1)}, f32[27,16,128]{2,1,0:T(8,128)S(1)}, u32[]{:S(2)}, u32[]{:S(2)}) %collective-permute-start.10) | collective-permute-done | bytes 221216 | tf_op jit(solution)/shard_map/ppermute | solution.py:292
  26.8 0.0 collective-permute-start.17
  26.8 0.0 collective-permute-done.13.refs_4_
  26.8 1.5 collective-permute-start.20
  28.3 0.1 collective-permute-start.11
  28.4 2.6 %collective-permute-start.14 = (f32[27,16,128]{2,1,0:T(8,128)S(1)}, f32[27,16,128]{2,1,0:T(8,128)S(1)}, u32[]{:S(2)}, u32[]{:S(2)}) collective-permute-start(f32[27,16,128]{2,1,0:T(8,128)S(1)} %collective-permute-done.13.refs_4_), channel_id=1, source_target_pairs={{0,224},{1,225},{2,226},{3,227},{4,228},{5,229},{6,230},{7,231},{8... | collective-permute-start | bytes 663560 | tf_op jit(solution)/shard_map/ppermute | solution.py:292
  31.0 3.3 %collective-permute-done.17.refs_5_ = f32[27,16,128]{2,1,0:T(8,128)S(1)} collective-permute-done((f32[27,16,128]{2,1,0:T(8,128)S(1)}, f32[27,16,128]{2,1,0:T(8,128)S(1)}, u32[]{:S(2)}, u32[]{:S(2)}) %collective-permute-start.17) | collective-permute-done | bytes 221216 | tf_op jit(solution)/shard_map/ppermute | solution.py:292
  34.3 3.3 %collective-permute-start.18 = (f32[27,16,128]{2,1,0:T(8,128)S(1)}, f32[27,16,128]{2,1,0:T(8,128)S(1)}, u32[]{:S(2)}, u32[]{:S(2)}) collective-permute-start(f32[27,16,128]{2,1,0:T(8,128)S(1)} %collective-permute-done.17.refs_5_), channel_id=1, source_target_pairs={{0,224},{1,225},{2,226},{3,227},{4,228},{5,229},{6,230},{7,231},{8... | collective-permute-start | bytes 663560 | tf_op jit(solution)/shard_map/ppermute | solution.py:292
  37.5 0.1 collective-permute-done.11.refs_6_
  37.7 1.3 collective-permute-done.14.refs_8_
  39.0 3.3 %collective-permute-start.7 = (f32[52,16,128]{2,1,0:T(8,128)S(1)}, f32[52,16,128]{2,1,0:T(8,128)S(1)}, u32[]{:S(2)}, u32[]{:S(2)}) collective-permute-start(f32[52,16,128]{2,1,0:T(8,128)S(1)} %collective-permute-done.6.refs_8_), channel_id=1, source_target_pairs={{0,224},{1,225},{2,226},{3,227},{4,228},{5,229},{6,230},{7,231},{8... | collective-permute-start | bytes 1277960 | tf_op jit(solution)/shard_map/ppermute | solution.py:292
  42.3 1.5 %collective-permute-done.18.refs_9_ = f32[27,16,128]{2,1,0:T(8,128)S(1)} collective-permute-done((f32[27,16,128]{2,1,0:T(8,128)S(1)}, f32[27,16,128]{2,1,0:T(8,128)S(1)}, u32[]{:S(2)}, u32[]{:S(2)}) %collective-permute-start.18) | collective-permute-done | bytes 221216 | tf_op jit(solution)/shard_map/ppermute | solution.py:292
  43.7 3.2 %collective-permute-start.15 = (f32[27,16,128]{2,1,0:T(8,128)S(1)}, f32[27,16,128]{2,1,0:T(8,128)S(1)}, u32[]{:S(2)}, u32[]{:S(2)}) collective-permute-start(f32[27,16,128]{2,1,0:T(8,128)S(1)} %collective-permute-done.14.refs_8_), channel_id=1, source_target_pairs={{0,224},{1,225},{2,226},{3,227},{4,228},{5,229},{6,230},{7,231},{8... | collective-permute-start | bytes 663560 | tf_op jit(solution)/shard_map/ppermute | solution.py:292
  47.0 2.9 %collective-permute-start.26 = (f32[52,16,128]{2,1,0:T(8,128)S(1)}, f32[52,16,128]{2,1,0:T(8,128)S(1)}, u32[]{:S(2)}, u32[]{:S(2)}) collective-permute-start(f32[52,16,128]{2,1,0:T(8,128)S(1)} %collective-permute-done.refs_2_), channel_id=1, source_target_pairs={{0,16},{1,17},{2,18},{3,19},{4,20},{5,21},{6,22},{7,23},{8,24},{9,... | collective-permute-start | bytes 1277960 | tf_op jit(solution)/shard_map/ppermute | solution.py:292
  49.9 0.1 collective-permute-start.27
  50.0 7.6 %collective-permute-done.15.refs_5_ = f32[27,16,128]{2,1,0:T(8,128)S(1)} collective-permute-done((f32[27,16,128]{2,1,0:T(8,128)S(1)}, f32[27,16,128]{2,1,0:T(8,128)S(1)}, u32[]{:S(2)}, u32[]{:S(2)}) %collective-permute-start.15) | collective-permute-done | bytes 221216 | tf_op jit(solution)/shard_map/ppermute | solution.py:292
  57.6 2.6 %collective-permute-start.19 = (f32[27,16,128]{2,1,0:T(8,128)S(1)}, f32[27,16,128]{2,1,0:T(8,128)S(1)}, u32[]{:S(2)}, u32[]{:S(2)}) collective-permute-start(f32[27,16,128]{2,1,0:T(8,128)S(1)} %collective-permute-done.18.refs_9_), channel_id=1, source_target_pairs={{0,224},{1,225},{2,226},{3,227},{4,228},{5,229},{6,230},{7,231},{8... | collective-permute-start | bytes 663560 | tf_op jit(solution)/shard_map/ppermute | solution.py:292
  60.2 2.6 %collective-permute-start.8 = (f32[52,16,128]{2,1,0:T(8,128)S(1)}, f32[52,16,128]{2,1,0:T(8,128)S(1)}, u32[]{:S(2)}, u32[]{:S(2)}) collective-permute-start(f32[52,16,128]{2,1,0:T(8,128)S(1)} %collective-permute-done.7.refs_11_), channel_id=1, source_target_pairs={{0,16},{1,17},{2,18},{3,19},{4,20},{5,21},{6,22},{7,23},{8,24},{9,... | collective-permute-start | bytes 1277960 | tf_op jit(solution)/shard_map/ppermute | solution.py:292
  62.8 0.5 collective-permute-start.28
  63.3 0.5 collective-permute-done.27.refs_5_
  63.8 2.6 %collective-permute-start.29 = (f32[52,16,128]{2,1,0:T(8,128)S(1)}, f32[52,16,128]{2,1,0:T(8,128)S(1)}, u32[]{:S(2)}, u32[]{:S(2)}) collective-permute-start(f32[52,16,128]{2,1,0:T(8,128)S(1)} %collective-permute-done.6.refs_8_), channel_id=1, source_target_pairs={{0,16},{1,17},{2,18},{3,19},{4,20},{5,21},{6,22},{7,23},{8,24},{9,... | collective-permute-start | bytes 1277960 | tf_op jit(solution)/shard_map/ppermute | solution.py:292
  66.4 3.2 %collective-permute-done.2.refs_10_ = f32[52,16,128]{2,1,0:T(8,128)S(1)} collective-permute-done((f32[52,16,128]{2,1,0:T(8,128)S(1)}, f32[52,16,128]{2,1,0:T(8,128)S(1)}, u32[]{:S(2)}, u32[]{:S(2)}) %collective-permute-start.2) | collective-permute-done | bytes 426016 | tf_op jit(solution)/shard_map/ppermute | solution.py:292
  69.5 1.5 %collective-permute-start.3 = (f32[52,16,128]{2,1,0:T(8,128)S(1)}, f32[52,16,128]{2,1,0:T(8,128)S(1)}, u32[]{:S(2)}, u32[]{:S(2)}) collective-permute-start(f32[52,16,128]{2,1,0:T(8,128)S(1)} %collective-permute-done.2.refs_10_), channel_id=1, source_target_pairs={{0,16},{1,17},{2,18},{3,19},{4,20},{5,21},{6,22},{7,23},{8,24},{9,... | collective-permute-start | bytes 1277960 | tf_op jit(solution)/shard_map/ppermute | solution.py:292
  71.0 4.0 %collective-permute-done.22.refs_7_ = f32[27,16,128]{2,1,0:T(8,128)S(1)} collective-permute-done((f32[27,16,128]{2,1,0:T(8,128)S(1)}, f32[27,16,128]{2,1,0:T(8,128)S(1)}, u32[]{:S(2)}, u32[]{:S(2)}) %collective-permute-start.22) | collective-permute-done | bytes 221216 | tf_op jit(solution)/shard_map/ppermute | solution.py:292
  75.0 2.7 %collective-permute-start.9 = (f32[52,16,128]{2,1,0:T(8,128)S(1)}, f32[52,16,128]{2,1,0:T(8,128)S(1)}, u32[]{:S(2)}, u32[]{:S(2)}) collective-permute-start(f32[52,16,128]{2,1,0:T(8,128)S(1)} %collective-permute-done.8.refs_12_), channel_id=1, source_target_pairs={{0,224},{1,225},{2,226},{3,227},{4,228},{5,229},{6,230},{7,231},{8... | collective-permute-start | bytes 1277960 | tf_op jit(solution)/shard_map/ppermute | solution.py:292
  77.7 5.1 %collective-permute-done.28.refs_7_ = f32[52,16,128]{2,1,0:T(8,128)S(1)} collective-permute-done((f32[52,16,128]{2,1,0:T(8,128)S(1)}, f32[52,16,128]{2,1,0:T(8,128)S(1)}, u32[]{:S(2)}, u32[]{:S(2)}) %collective-permute-start.28) | collective-permute-done | bytes 426016 | tf_op jit(solution)/shard_map/ppermute | solution.py:292
  82.8 9.1 %collective-permute-done.29.refs_9_ = f32[52,16,128]{2,1,0:T(8,128)S(1)} collective-permute-done((f32[52,16,128]{2,1,0:T(8,128)S(1)}, f32[52,16,128]{2,1,0:T(8,128)S(1)}, u32[]{:S(2)}, u32[]{:S(2)}) %collective-permute-start.29) | collective-permute-done | bytes 426016 | tf_op jit(solution)/shard_map/ppermute | solution.py:292
  91.9 2.6 %collective-permute-start.24 = (f32[27,16,128]{2,1,0:T(8,128)S(1)}, f32[27,16,128]{2,1,0:T(8,128)S(1)}, u32[]{:S(2)}, u32[]{:S(2)}) collective-permute-start(f32[27,16,128]{2,1,0:T(8,128)S(1)} %collective-permute-done.19.refs_6_), channel_id=1, source_target_pairs={{0,224},{1,225},{2,226},{3,227},{4,228},{5,229},{6,230},{7,231},{8... | collective-permute-start | bytes 663560 | tf_op jit(solution)/shard_map/ppermute | solution.py:292
  94.5 6.2 %pack_va.1 = (bf16[52,256,128]{2,1,0:T(8,128)(2,1)S(1)}, bf16[52,256,128]{2,1,0:T(8,128)(2,1)S(1)}) custom-call(f32[4,25,64,400]{3,2,1,0:T(8,128)} %bitcast.8, f32[4,25,64,400]{3,2,1,0:T(8,128)} %bitcast.9), custom_call_target="tpu_custom_call" | custom-call | tf_op jit(solution)/shard_map/pack_va/pallas_call | solution.py:97
  100.7 3.2 %pack_vb.1 = (bf16[27,256,128]{2,1,0:T(8,128)(2,1)S(1)}, bf16[27,256,128]{2,1,0:T(8,128)(2,1)S(1)}) custom-call(f32[4,25,64,400]{3,2,1,0:T(8,128)} %bitcast.10, f32[4,25,64,400]{3,2,1,0:T(8,128)} %bitcast.11), custom_call_target="tpu_custom_call" | custom-call | tf_op jit(solution)/shard_map/pack_vb/pallas_call | solution.py:113
  103.9 1.3 shard_map.56.refs_15_
  105.2 3.6 %shard_map.55.refs_14_ = f32[208,256]{1,0:T(8,128)S(1)} custom-call(f32[52,16,128]{2,1,0:T(8,128)S(1)} %get-tuple-element.15.refs_0_, f32[52,16,128]{2,1,0:T(8,128)S(1)} %collective-permute-done.25.refs_1_, f32[52,16,128]{2,1,0:T(8,128)S(1)} %collective-permute-done.refs_2_, f32[52,16,128]{2,1,0:T(8,128)S(1)} %collective-permute-done.26.refs_3_, ...), custom_call_target="tpu_custom_call" | custom-call | tf_op jit(solution)/shard_map/pallas_call | solution.py:157
  108.8 0.0 copy-start.1
  108.8 0.0 copy-start
  108.8 0.0 copy-start.2
  108.9 4.5 %last.1 = (f32[8,32,256]{2,1,0:T(8,128)S(1)}, f32[8,32,256]{2,1,0:T(8,128)S(1)}) custom-call(s32[2]{0:T(128)S(1)} %pad_add_fusion.at_ref.refs_0_, f32[52,16,128]{2,1,0:T(8,128)S(1)} %collective-permute-done.3.refs_1_, f32[52,16,128]{2,1,0:T(8,128)S(1)} %collective-permute-done.4.refs_2_, f32[52,16,128]{2,1,0:T(8,128)S(1)} %collective-permute-done.9.refs_3_, ...), custom_call_target="tpu_custom_call" | custom-call | tf_op jit(solution)/shard_map/last/pallas_call | solution.py:200
  113.4 7.4 %collective-permute-start.30 = (f32[8,32,256]{2,1,0:T(8,128)S(1)}, f32[8,32,256]{2,1,0:T(8,128)S(1)}, u32[]{:S(2)}, u32[]{:S(2)}) collective-permute-start(f32[8,32,256]{2,1,0:T(8,128)S(1)} %get-tuple-element.22), channel_id=1, source_target_pairs={{0,1},{1,0},{2,3},{3,2},{4,5},{5,4},{6,7},{7,6},{8,9},{9,8},{10,11... | collective-permute-start | bytes 786440 | tf_op jit(solution)/shard_map/ppermute | solution.py:292
  120.8 0.1 dynamic_slice.6
  120.9 1.1 collective-permute-done.30
  122.0 0.7 add.31
  122.7 7.1 %all-to-all-start = ((f32[8,32,256]{2,1,0:T(8,128)}), f32[8,32,256]{2,1,0:T(8,128)S(1)}, u32[]{:S(2)}, u32[]{:S(2)}) async-start(f32[8,32,256]{2,1,0:T(8,128)} %add.31), calls=%async_computation | async-start | bytes 524288 | tf_op jit(solution)/shard_map/all_to_all | solution.py:336
  129.8 0.1 broadcast_reduce_fusion
  129.9 0.1 add.34
  130.0 0.1 add.36
  130.1 0.1 reshape.40.rest_ref
  130.2 0.6 dynamic_slice.7
  130.7 0.6 add_subtract_fusion
  131.4 2.6 %all-to-all-done.r_ref = f32[8,32,256]{2,1,0:T(8,128)S(1)} async-done(((f32[8,32,256]{2,1,0:T(8,128)}), f32[8,32,256]{2,1,0:T(8,128)S(1)}, u32[]{:S(2)}, u32[]{:S(2)}) %all-to-all-start) | async-done | bytes 262176 | tf_op jit(solution)/shard_map/all_to_all | solution.py:336
  134.0 0.9 fold.1
  134.9 9.6 %all-to-all-start.1 = ((f32[16,8,128]{2,1,0:T(8,128)}), f32[16,8,128]{2,1,0:T(8,128)S(1)}, u32[]{:S(2)}, u32[]{:S(2)}) async-start(f32[16,8,128]{2,1,0:T(8,128)} %get-tuple-element.24), calls=%async_computation.1 | async-start | bytes 131072 | tf_op jit(solution)/shard_map/all_to_all | solution.py:340
  144.5 0.1 broadcast_subtract_fusion.den_ref
  144.6 2.4 %all-to-all-done.1.m_ref = f32[16,8,128]{2,1,0:T(8,128)S(1)} async-done(((f32[16,8,128]{2,1,0:T(8,128)}), f32[16,8,128]{2,1,0:T(8,128)S(1)}, u32[]{:S(2)}, u32[]{:S(2)}) %all-to-all-start.1) | async-done | bytes 65568 | tf_op jit(solution)/shard_map/all_to_all | solution.py:340
  147.0 0.9 finish.1
  (27 shorter events, 0.1 us)
Async XLA Ops:
  1.3 15.0 %collective-permute-start.5 = (f32[52,16,128]{2,1,0:T(8,128)S(1)}, f32[52,16,128]{2,1,0:T(8,128)S(1)}, u32[]{:S(2)}, u32[]{:S(2)}) collective-permute-start(f32[52,16,128]{2,1,0:T(8,128)S(1)} %get-tuple-element.15.refs_0_), channel_id=1, source_target_pairs={{0,224},{1,225},{2,226},{3,227},{4,228},{5,229},{6,230},{7,231},{8... | collective-permute-start | bytes 1277960 | tf_op jit(solution)/shard_map/ppermute | solution.py:292
  7.8 7.5 %collective-permute-start.16 = (f32[27,16,128]{2,1,0:T(8,128)S(1)}, f32[27,16,128]{2,1,0:T(8,128)S(1)}, u32[]{:S(2)}, u32[]{:S(2)}) collective-permute-start(f32[27,16,128]{2,1,0:T(8,128)S(1)} %get-tuple-element.16.refs_0_), channel_id=1, source_target_pairs={{0,16},{1,17},{2,18},{3,19},{4,20},{5,21},{6,22},{7,23},{8,24},{9,... | collective-permute-start | bytes 663560 | tf_op jit(solution)/shard_map/ppermute | solution.py:292
  10.7 17.6 %collective-permute-start = (f32[52,16,128]{2,1,0:T(8,128)S(1)}, f32[52,16,128]{2,1,0:T(8,128)S(1)}, u32[]{:S(2)}, u32[]{:S(2)}) collective-permute-start(f32[52,16,128]{2,1,0:T(8,128)S(1)} %get-tuple-element.15.refs_0_), channel_id=1, source_target_pairs={{0,32},{1,33},{2,34},{3,35},{4,36},{5,37},{6,38},{7,39},{8,40},{9,... | collective-permute-start | bytes 1277960 | tf_op jit(solution)/shard_map/ppermute | solution.py:292
  10.7 17.6 %collective-permute-start.25 = (f32[52,16,128]{2,1,0:T(8,128)S(1)}, f32[52,16,128]{2,1,0:T(8,128)S(1)}, u32[]{:S(2)}, u32[]{:S(2)}) collective-permute-start(f32[52,16,128]{2,1,0:T(8,128)S(1)} %get-tuple-element.15.refs_0_), channel_id=1, source_target_pairs={{0,16},{1,17},{2,18},{3,19},{4,20},{5,21},{6,22},{7,23},{8,24},{9,... | collective-permute-start | bytes 1277960 | tf_op jit(solution)/shard_map/ppermute | solution.py:292
  10.8 16.0 %collective-permute-start.10 = (f32[27,16,128]{2,1,0:T(8,128)S(1)}, f32[27,16,128]{2,1,0:T(8,128)S(1)}, u32[]{:S(2)}, u32[]{:S(2)}) collective-permute-start(f32[27,16,128]{2,1,0:T(8,128)S(1)} %get-tuple-element.16.refs_0_), channel_id=1, source_target_pairs={{0,32},{1,33},{2,34},{3,35},{4,36},{5,37},{6,38},{7,39},{8,40},{9,... | collective-permute-start | bytes 663560 | tf_op jit(solution)/shard_map/ppermute | solution.py:292
  15.4 11.5 %collective-permute-start.13 = (f32[27,16,128]{2,1,0:T(8,128)S(1)}, f32[27,16,128]{2,1,0:T(8,128)S(1)}, u32[]{:S(2)}, u32[]{:S(2)}) collective-permute-start(f32[27,16,128]{2,1,0:T(8,128)S(1)} %get-tuple-element.16.refs_0_), channel_id=1, source_target_pairs={{0,224},{1,225},{2,226},{3,227},{4,228},{5,229},{6,230},{7,231},{8... | collective-permute-start | bytes 663560 | tf_op jit(solution)/shard_map/ppermute | solution.py:292
  16.3 22.7 %collective-permute-start.6 = (f32[52,16,128]{2,1,0:T(8,128)S(1)}, f32[52,16,128]{2,1,0:T(8,128)S(1)}, u32[]{:S(2)}, u32[]{:S(2)}) collective-permute-start(f32[52,16,128]{2,1,0:T(8,128)S(1)} %collective-permute-done.5.refs_4_), channel_id=1, source_target_pairs={{0,224},{1,225},{2,226},{3,227},{4,228},{5,229},{6,230},{7,231},{8... | collective-permute-start | bytes 1277960 | tf_op jit(solution)/shard_map/ppermute | solution.py:292
  26.8 7.4 %collective-permute-start.17 = (f32[27,16,128]{2,1,0:T(8,128)S(1)}, f32[27,16,128]{2,1,0:T(8,128)S(1)}, u32[]{:S(2)}, u32[]{:S(2)}) collective-permute-start(f32[27,16,128]{2,1,0:T(8,128)S(1)} %collective-permute-done.16.refs_1_), channel_id=1, source_target_pairs={{0,224},{1,225},{2,226},{3,227},{4,228},{5,229},{6,230},{7,231},{8... | collective-permute-start | bytes 663560 | tf_op jit(solution)/shard_map/ppermute | solution.py:292
  26.8 10.7 %collective-permute-start.20 = (f32[27,16,128]{2,1,0:T(8,128)S(1)}, f32[27,16,128]{2,1,0:T(8,128)S(1)}, u32[]{:S(2)}, u32[]{:S(2)}) collective-permute-start(f32[27,16,128]{2,1,0:T(8,128)S(1)} %collective-permute-done.16.refs_1_), channel_id=1, source_target_pairs={{0,32},{1,33},{2,34},{3,35},{4,36},{5,37},{6,38},{7,39},{8,40},{9,... | collective-permute-start | bytes 663560 | tf_op jit(solution)/shard_map/ppermute | solution.py:292
  28.3 9.4 %collective-permute-start.11 = (f32[27,16,128]{2,1,0:T(8,128)S(1)}, f32[27,16,128]{2,1,0:T(8,128)S(1)}, u32[]{:S(2)}, u32[]{:S(2)}) collective-permute-start(f32[27,16,128]{2,1,0:T(8,128)S(1)} %collective-permute-done.10.refs_2_), channel_id=1, source_target_pairs={{0,32},{1,33},{2,34},{3,35},{4,36},{5,37},{6,38},{7,39},{8,40},{9,... | collective-permute-start | bytes 663560 | tf_op jit(solution)/shard_map/ppermute | solution.py:292
  28.4 10.6 %collective-permute-start.14 = (f32[27,16,128]{2,1,0:T(8,128)S(1)}, f32[27,16,128]{2,1,0:T(8,128)S(1)}, u32[]{:S(2)}, u32[]{:S(2)}) collective-permute-start(f32[27,16,128]{2,1,0:T(8,128)S(1)} %collective-permute-done.13.refs_4_), channel_id=1, source_target_pairs={{0,224},{1,225},{2,226},{3,227},{4,228},{5,229},{6,230},{7,231},{8... | collective-permute-start | bytes 663560 | tf_op jit(solution)/shard_map/ppermute | solution.py:292
  34.3 9.5 %collective-permute-start.18 = (f32[27,16,128]{2,1,0:T(8,128)S(1)}, f32[27,16,128]{2,1,0:T(8,128)S(1)}, u32[]{:S(2)}, u32[]{:S(2)}) collective-permute-start(f32[27,16,128]{2,1,0:T(8,128)S(1)} %collective-permute-done.17.refs_5_), channel_id=1, source_target_pairs={{0,224},{1,225},{2,226},{3,227},{4,228},{5,229},{6,230},{7,231},{8... | collective-permute-start | bytes 663560 | tf_op jit(solution)/shard_map/ppermute | solution.py:292
  37.5 9.4 %collective-permute-start.21 = (f32[27,16,128]{2,1,0:T(8,128)S(1)}, f32[27,16,128]{2,1,0:T(8,128)S(1)}, u32[]{:S(2)}, u32[]{:S(2)}) collective-permute-start(f32[27,16,128]{2,1,0:T(8,128)S(1)} %collective-permute-done.20.refs_3_), channel_id=1, source_target_pairs={{0,32},{1,33},{2,34},{3,35},{4,36},{5,37},{6,38},{7,39},{8,40},{9,... | collective-permute-start | bytes 663560 | tf_op jit(solution)/shard_map/ppermute | solution.py:292
  37.7 12.2 %collective-permute-start.12 = (f32[27,16,128]{2,1,0:T(8,128)S(1)}, f32[27,16,128]{2,1,0:T(8,128)S(1)}, u32[]{:S(2)}, u32[]{:S(2)}) collective-permute-start(f32[27,16,128]{2,1,0:T(8,128)S(1)} %collective-permute-done.11.refs_6_), channel_id=1, source_target_pairs={{0,32},{1,33},{2,34},{3,35},{4,36},{5,37},{6,38},{7,39},{8,40},{9,... | collective-permute-start | bytes 663560 | tf_op jit(solution)/shard_map/ppermute | solution.py:292
  39.0 21.2 %collective-permute-start.1 = (f32[52,16,128]{2,1,0:T(8,128)S(1)}, f32[52,16,128]{2,1,0:T(8,128)S(1)}, u32[]{:S(2)}, u32[]{:S(2)}) collective-permute-start(f32[52,16,128]{2,1,0:T(8,128)S(1)} %collective-permute-done.refs_2_), channel_id=1, source_target_pairs={{0,32},{1,33},{2,34},{3,35},{4,36},{5,37},{6,38},{7,39},{8,40},{9,... | collective-permute-start | bytes 1277960 | tf_op jit(solution)/shard_map/ppermute | solution.py:292
  39.0 21.2 %collective-permute-start.7 = (f32[52,16,128]{2,1,0:T(8,128)S(1)}, f32[52,16,128]{2,1,0:T(8,128)S(1)}, u32[]{:S(2)}, u32[]{:S(2)}) collective-permute-start(f32[52,16,128]{2,1,0:T(8,128)S(1)} %collective-permute-done.6.refs_8_), channel_id=1, source_target_pairs={{0,224},{1,225},{2,226},{3,227},{4,228},{5,229},{6,230},{7,231},{8... | collective-permute-start | bytes 1277960 | tf_op jit(solution)/shard_map/ppermute | solution.py:292
  43.7 13.9 %collective-permute-start.15 = (f32[27,16,128]{2,1,0:T(8,128)S(1)}, f32[27,16,128]{2,1,0:T(8,128)S(1)}, u32[]{:S(2)}, u32[]{:S(2)}) collective-permute-start(f32[27,16,128]{2,1,0:T(8,128)S(1)} %collective-permute-done.14.refs_8_), channel_id=1, source_target_pairs={{0,224},{1,225},{2,226},{3,227},{4,228},{5,229},{6,230},{7,231},{8... | collective-permute-start | bytes 663560 | tf_op jit(solution)/shard_map/ppermute | solution.py:292
  47.0 15.8 %collective-permute-start.26 = (f32[52,16,128]{2,1,0:T(8,128)S(1)}, f32[52,16,128]{2,1,0:T(8,128)S(1)}, u32[]{:S(2)}, u32[]{:S(2)}) collective-permute-start(f32[52,16,128]{2,1,0:T(8,128)S(1)} %collective-permute-done.refs_2_), channel_id=1, source_target_pairs={{0,16},{1,17},{2,18},{3,19},{4,20},{5,21},{6,22},{7,23},{8,24},{9,... | collective-permute-start | bytes 1277960 | tf_op jit(solution)/shard_map/ppermute | solution.py:292
  49.9 13.9 %collective-permute-start.27 = (f32[52,16,128]{2,1,0:T(8,128)S(1)}, f32[52,16,128]{2,1,0:T(8,128)S(1)}, u32[]{:S(2)}, u32[]{:S(2)}) collective-permute-start(f32[52,16,128]{2,1,0:T(8,128)S(1)} %collective-permute-done.5.refs_4_), channel_id=1, source_target_pairs={{0,16},{1,17},{2,18},{3,19},{4,20},{5,21},{6,22},{7,23},{8,24},{9,... | collective-permute-start | bytes 1277960 | tf_op jit(solution)/shard_map/ppermute | solution.py:292
  57.6 8.8 %collective-permute-start.19 = (f32[27,16,128]{2,1,0:T(8,128)S(1)}, f32[27,16,128]{2,1,0:T(8,128)S(1)}, u32[]{:S(2)}, u32[]{:S(2)}) collective-permute-start(f32[27,16,128]{2,1,0:T(8,128)S(1)} %collective-permute-done.18.refs_9_), channel_id=1, source_target_pairs={{0,224},{1,225},{2,226},{3,227},{4,228},{5,229},{6,230},{7,231},{8... | collective-permute-start | bytes 663560 | tf_op jit(solution)/shard_map/ppermute | solution.py:292
  60.2 9.3 %collective-permute-start.2 = (f32[52,16,128]{2,1,0:T(8,128)S(1)}, f32[52,16,128]{2,1,0:T(8,128)S(1)}, u32[]{:S(2)}, u32[]{:S(2)}) collective-permute-start(f32[52,16,128]{2,1,0:T(8,128)S(1)} %collective-permute-done.1.refs_6_), channel_id=1, source_target_pairs={{0,32},{1,33},{2,34},{3,35},{4,36},{5,37},{6,38},{7,39},{8,40},{9,... | collective-permute-start | bytes 1277960 | tf_op jit(solution)/shard_map/ppermute | solution.py:292
  60.2 14.8 %collective-permute-start.8 = (f32[52,16,128]{2,1,0:T(8,128)S(1)}, f32[52,16,128]{2,1,0:T(8,128)S(1)}, u32[]{:S(2)}, u32[]{:S(2)}) collective-permute-start(f32[52,16,128]{2,1,0:T(8,128)S(1)} %collective-permute-done.7.refs_11_), channel_id=1, source_target_pairs={{0,16},{1,17},{2,18},{3,19},{4,20},{5,21},{6,22},{7,23},{8,24},{9,... | collective-permute-start | bytes 1277960 | tf_op jit(solution)/shard_map/ppermute | solution.py:292
  62.8 20.0 %collective-permute-start.28 = (f32[52,16,128]{2,1,0:T(8,128)S(1)}, f32[52,16,128]{2,1,0:T(8,128)S(1)}, u32[]{:S(2)}, u32[]{:S(2)}) collective-permute-start(f32[52,16,128]{2,1,0:T(8,128)S(1)} %collective-permute-done.1.refs_6_), channel_id=1, source_target_pairs={{0,16},{1,17},{2,18},{3,19},{4,20},{5,21},{6,22},{7,23},{8,24},{9,... | collective-permute-start | bytes 1277960 | tf_op jit(solution)/shard_map/ppermute | solution.py:292
  63.8 28.1 %collective-permute-start.29 = (f32[52,16,128]{2,1,0:T(8,128)S(1)}, f32[52,16,128]{2,1,0:T(8,128)S(1)}, u32[]{:S(2)}, u32[]{:S(2)}) collective-permute-start(f32[52,16,128]{2,1,0:T(8,128)S(1)} %collective-permute-done.6.refs_8_), channel_id=1, source_target_pairs={{0,16},{1,17},{2,18},{3,19},{4,20},{5,21},{6,22},{7,23},{8,24},{9,... | collective-permute-start | bytes 1277960 | tf_op jit(solution)/shard_map/ppermute | solution.py:292
  66.4 8.7 %collective-permute-start.22 = (f32[27,16,128]{2,1,0:T(8,128)S(1)}, f32[27,16,128]{2,1,0:T(8,128)S(1)}, u32[]{:S(2)}, u32[]{:S(2)}) collective-permute-start(f32[27,16,128]{2,1,0:T(8,128)S(1)} %collective-permute-done.21.refs_7_), channel_id=1, source_target_pairs={{0,32},{1,33},{2,34},{3,35},{4,36},{5,37},{6,38},{7,39},{8,40},{9,... | collective-permute-start | bytes 663560 | tf_op jit(solution)/shard_map/ppermute | solution.py:292
  69.5 39.3 %collective-permute-start.3 = (f32[52,16,128]{2,1,0:T(8,128)S(1)}, f32[52,16,128]{2,1,0:T(8,128)S(1)}, u32[]{:S(2)}, u32[]{:S(2)}) collective-permute-start(f32[52,16,128]{2,1,0:T(8,128)S(1)} %collective-permute-done.2.refs_10_), channel_id=1, source_target_pairs={{0,16},{1,17},{2,18},{3,19},{4,20},{5,21},{6,22},{7,23},{8,24},{9,... | collective-permute-start | bytes 1277960 | tf_op jit(solution)/shard_map/ppermute | solution.py:292
  75.0 33.9 %collective-permute-start.4 = (f32[52,16,128]{2,1,0:T(8,128)S(1)}, f32[52,16,128]{2,1,0:T(8,128)S(1)}, u32[]{:S(2)}, u32[]{:S(2)}) collective-permute-start(f32[52,16,128]{2,1,0:T(8,128)S(1)} %collective-permute-done.2.refs_10_), channel_id=1, source_target_pairs={{0,32},{1,33},{2,34},{3,35},{4,36},{5,37},{6,38},{7,39},{8,40},{9,... | collective-permute-start | bytes 1277960 | tf_op jit(solution)/shard_map/ppermute | solution.py:292
  75.0 33.9 %collective-permute-start.9 = (f32[52,16,128]{2,1,0:T(8,128)S(1)}, f32[52,16,128]{2,1,0:T(8,128)S(1)}, u32[]{:S(2)}, u32[]{:S(2)}) collective-permute-start(f32[52,16,128]{2,1,0:T(8,128)S(1)} %collective-permute-done.8.refs_12_), channel_id=1, source_target_pairs={{0,224},{1,225},{2,226},{3,227},{4,228},{5,229},{6,230},{7,231},{8... | collective-permute-start | bytes 1277960 | tf_op jit(solution)/shard_map/ppermute | solution.py:292
  82.8 26.1 %collective-permute-start.23 = (f32[27,16,128]{2,1,0:T(8,128)S(1)}, f32[27,16,128]{2,1,0:T(8,128)S(1)}, u32[]{:S(2)}, u32[]{:S(2)}) collective-permute-start(f32[27,16,128]{2,1,0:T(8,128)S(1)} %collective-permute-done.12.refs_4_), channel_id=1, source_target_pairs={{0,32},{1,33},{2,34},{3,35},{4,36},{5,37},{6,38},{7,39},{8,40},{9,... | collective-permute-start | bytes 663560 | tf_op jit(solution)/shard_map/ppermute | solution.py:292
  91.9 16.9 %collective-permute-start.24 = (f32[27,16,128]{2,1,0:T(8,128)S(1)}, f32[27,16,128]{2,1,0:T(8,128)S(1)}, u32[]{:S(2)}, u32[]{:S(2)}) collective-permute-start(f32[27,16,128]{2,1,0:T(8,128)S(1)} %collective-permute-done.19.refs_6_), channel_id=1, source_target_pairs={{0,224},{1,225},{2,226},{3,227},{4,228},{5,229},{6,230},{7,231},{8... | collective-permute-start | bytes 663560 | tf_op jit(solution)/shard_map/ppermute | solution.py:292
  108.8 12.0 %copy-start.1 = (f32[64]{0:T(128)S(1)}, f32[64]{0:T(128)}, u32[]{:S(2)}) copy-start(f32[64]{0:T(128)} %param.9) | copy-start | bytes 772
  108.8 21.2 %copy-start = (f32[1,16,4,64]{3,2,1,0:T(4,128)S(1)}, f32[1,16,4,64]{3,2,1,0:T(4,128)}, u32[]{:S(2)}) copy-start(f32[1,16,4,64]{3,2,1,0:T(4,128)} %param.7) | copy-start | bytes 49156
  108.8 21.3 %copy-start.2 = (f32[16]{0:T(128)S(1)}, f32[16]{0:T(128)}, u32[]{:S(2)}) copy-start(f32[16]{0:T(128)} %param.8) | copy-start | bytes 196
  113.4 8.5 %collective-permute-start.30 = (f32[8,32,256]{2,1,0:T(8,128)S(1)}, f32[8,32,256]{2,1,0:T(8,128)S(1)}, u32[]{:S(2)}, u32[]{:S(2)}) collective-permute-start(f32[8,32,256]{2,1,0:T(8,128)S(1)} %get-tuple-element.22), channel_id=1, source_target_pairs={{0,1},{1,0},{2,3},{3,2},{4,5},{5,4},{6,7},{7,6},{8,9},{9,8},{10,11... | collective-permute-start | bytes 786440 | tf_op jit(solution)/shard_map/ppermute | solution.py:292
  122.7 11.3 %all-to-all-start = ((f32[8,32,256]{2,1,0:T(8,128)}), f32[8,32,256]{2,1,0:T(8,128)S(1)}, u32[]{:S(2)}, u32[]{:S(2)}) async-start(f32[8,32,256]{2,1,0:T(8,128)} %add.31), calls=%async_computation | async-start | bytes 524288 | tf_op jit(solution)/shard_map/all_to_all | solution.py:336
  134.9 12.1 %all-to-all-start.1 = ((f32[16,8,128]{2,1,0:T(8,128)}), f32[16,8,128]{2,1,0:T(8,128)S(1)}, u32[]{:S(2)}, u32[]{:S(2)}) async-start(f32[16,8,128]{2,1,0:T(8,128)} %get-tuple-element.24), calls=%async_computation.1 | async-start | bytes 131072 | tf_op jit(solution)/shard_map/all_to_all | solution.py:340

commit v6 on v5

--- a/solution.py
+++ b/solution.py
@@ -219,26 +219,31 @@
     return y[:m] + y[m : 2 * m] + y[2 * m :]
 
 
-def fold_kernel(r_ref, d_ref, e_ref):
-    total = r_ref[0]
+def sum_rows(r_ref, rows):
+    total = r_ref[0, rows, :]
     for k in range(1, NC // 2):
-        total += r_ref[k]
-    d_ref[...] = total[:NJ]
-    mixed = permute_lanes(total[NJ:], lambda n: ((n >> 2) & 3) * 64 + (n >> 4) * 4 + (n & 3))
+        total += r_ref[k, rows, :]
+    return total
+
+
+def fold_kernel(r_ref, e_ref):
+    mixed = permute_lanes(
+        sum_rows(r_ref, slice(NJ, 2 * NJ)),
+        lambda n: ((n >> 2) & 3) * 64 + (n >> 4) * 4 + (n & 3),
+    )
     zeros = jnp.zeros((8, LANES - 32), F32)
     for r in range(NR):
         lanes = slice(16 * r, 16 * (r + 1))
         e_ref[(r - FIRST_ROW) % NR] = jnp.concatenate([mixed[:8, lanes], mixed[8:, lanes], zeros], axis=-1)
 
 
-def fold(r):
-    return pl.pallas_call(
-        fold_kernel,
-        in_specs=[VMEM],
-        out_specs=(VMEM, VMEM),
-        out_shape=(pltpu.VMEM((NJ, NAB), F32), LAST_OUT((NR, 8, LANES), F32)),
-        compiler_params=params(4),
-        name="fold",
+def direct_kernel(r_ref, d_ref):
+    d_ref[...] = sum_rows(r_ref, slice(0, NJ))
+
+
+def from_received(kernel, r, out):
+    return pl.pallas_call(
+        kernel, in_specs=[VMEM], out_specs=VMEM, out_shape=out, compiler_params=params(4)
     )(on_chip(r))
 
 
@@ -336,7 +341,8 @@
     received = lax.all_to_all(
         partial, AXES, 0, 0, axis_index_groups=SAME_CORE, tiled=True
     )
-    direct, messages = fold(received)
+    messages = from_received(fold_kernel, received, LAST_OUT((NR, 8, LANES), F32))
+    direct = from_received(direct_kernel, received, pltpu.VMEM((NJ, NAB), F32))
     mirror = lax.all_to_all(messages, AXES, 0, 0, axis_index_groups=SAME_COLUMN, tiled=True)
 
     vir_local = lax.dynamic_slice_in_dim(vir_energy, row * 4, 4, 0)

time: 149 us -> 149 us (level)
  no operation moved by 1% of the time
where the time goes in v6:
time: 149 us; the launch traced here: 148 us
  starting transfers between devices  69.5 us (47%)
  waiting for transfers between devices  53.7 us (36%)
  Pallas kernels  21.9 us (15%)
  other arithmetic  1.53 us (1%)
    ppermute x31, starting transfers between devices, send(): return lax.ppermute(x, AXES, where)  52.8 us
    ppermute x31, waiting for transfers between devices, send(): return lax.ppermute(x, AXES, where)  48.8 us
    all_to_all x1, starting transfers between devices, on_device(): lax.all_to_all(messages, AXES, 0, 0, axis_index_groups=SAME_COLUMN, tiled...  9.63 us
    all_to_all x1, starting transfers between devices, on_device(): lax.all_to_all(partial, AXES, 0, 0, axis_index_groups=SAME_CORE, tiled=True)  7.08 us
    pallas_call x1, Pallas kernels, pack_va(): pl.pallas_call(pack_va_kernel, grid=(2, 4), in_specs=[pl.BlockSpec((None,...  6.18 us
    pallas_call x2, Pallas kernels, dot(): pl.pallas_call(kernel, in_specs=[VMEM] * len(args), out_specs=VMEM, out_s...  4.88 us
    pallas_call x1, Pallas kernels, last(): pl.pallas_call(lambda *refs: last_kernel(where, *refs), in_specs=[pl.Bloc...  4.53 us
    pallas_call x1, Pallas kernels, pack_vb(): pl.pallas_call(pack_vb_kernel, grid=(4,), in_specs=[pl.BlockSpec((None, 8...  3.23 us
  transfers between devices with their start and end apart: 33, of which 16 were waited for; matrix products, arithmetic and copies ran while one was open for 1% of the time, Pallas kernels for 10%

profile of v6, /device:TPU:1, one launch (start us, length us, event | category | flops | bytes accessed | tf_op | source)
XLA Modules:
  0.0 147.9 jit_solution(10669439803026519461)
XLA Ops:
  0.0 0.1 pad_add_fusion.at_ref.refs_0_
  0.1 1.3 pack_t.1
  1.3 6.5 %collective-permute-start.5 = (f32[52,16,128]{2,1,0:T(8,128)S(1)}, f32[52,16,128]{2,1,0:T(8,128)S(1)}, u32[]{:S(2)}, u32[]{:S(2)}) collective-permute-start(f32[52,16,128]{2,1,0:T(8,128)S(1)} %get-tuple-element.13.refs_0_), channel_id=1, source_target_pairs={{0,224},{1,225},{2,226},{3,227},{4,228},{5,229},{6,230},{7,231},{8... | collective-permute-start | bytes 1277960 | tf_op jit(solution)/shard_map/ppermute | solution.py:297
  7.8 2.9 %collective-permute-start.16 = (f32[27,16,128]{2,1,0:T(8,128)S(1)}, f32[27,16,128]{2,1,0:T(8,128)S(1)}, u32[]{:S(2)}, u32[]{:S(2)}) collective-permute-start(f32[27,16,128]{2,1,0:T(8,128)S(1)} %get-tuple-element.14.refs_0_), channel_id=1, source_target_pairs={{0,16},{1,17},{2,18},{3,19},{4,20},{5,21},{6,22},{7,23},{8,24},{9,... | collective-permute-start | bytes 663560 | tf_op jit(solution)/shard_map/ppermute | solution.py:297
  10.7 0.0 collective-permute-start
  10.7 0.1 collective-permute-start.25
  10.8 0.0 collective-permute-start.10
  10.8 4.6 %collective-permute-done.16.refs_1_ = f32[27,16,128]{2,1,0:T(8,128)S(1)} collective-permute-done((f32[27,16,128]{2,1,0:T(8,128)S(1)}, f32[27,16,128]{2,1,0:T(8,128)S(1)}, u32[]{:S(2)}, u32[]{:S(2)}) %collective-permute-start.16) | collective-permute-done | bytes 221216 | tf_op jit(solution)/shard_map/ppermute | solution.py:297
  15.4 0.7 collective-permute-start.13
  16.1 0.2 collective-permute-done.5.refs_4_
  16.3 3.4 %collective-permute-start.6 = (f32[52,16,128]{2,1,0:T(8,128)S(1)}, f32[52,16,128]{2,1,0:T(8,128)S(1)}, u32[]{:S(2)}, u32[]{:S(2)}) collective-permute-start(f32[52,16,128]{2,1,0:T(8,128)S(1)} %collective-permute-done.5.refs_4_), channel_id=1, source_target_pairs={{0,224},{1,225},{2,226},{3,227},{4,228},{5,229},{6,230},{7,231},{8... | collective-permute-start | bytes 1277960 | tf_op jit(solution)/shard_map/ppermute | solution.py:297
  19.7 7.1 %collective-permute-done.10.refs_2_ = f32[27,16,128]{2,1,0:T(8,128)S(1)} collective-permute-done((f32[27,16,128]{2,1,0:T(8,128)S(1)}, f32[27,16,128]{2,1,0:T(8,128)S(1)}, u32[]{:S(2)}, u32[]{:S(2)}) %collective-permute-start.10) | collective-permute-done | bytes 221216 | tf_op jit(solution)/shard_map/ppermute | solution.py:297
  26.8 0.0 collective-permute-start.17
  26.8 0.0 collective-permute-done.13.refs_4_
  26.8 1.5 collective-permute-start.20
  28.3 0.1 collective-permute-start.11
  28.4 2.6 %collective-permute-start.14 = (f32[27,16,128]{2,1,0:T(8,128)S(1)}, f32[27,16,128]{2,1,0:T(8,128)S(1)}, u32[]{:S(2)}, u32[]{:S(2)}) collective-permute-start(f32[27,16,128]{2,1,0:T(8,128)S(1)} %collective-permute-done.13.refs_4_), channel_id=1, source_target_pairs={{0,224},{1,225},{2,226},{3,227},{4,228},{5,229},{6,230},{7,231},{8... | collective-permute-start | bytes 663560 | tf_op jit(solution)/shard_map/ppermute | solution.py:297
  31.0 3.3 %collective-permute-done.17.refs_5_ = f32[27,16,128]{2,1,0:T(8,128)S(1)} collective-permute-done((f32[27,16,128]{2,1,0:T(8,128)S(1)}, f32[27,16,128]{2,1,0:T(8,128)S(1)}, u32[]{:S(2)}, u32[]{:S(2)}) %collective-permute-start.17) | collective-permute-done | bytes 221216 | tf_op jit(solution)/shard_map/ppermute | solution.py:297
  34.3 3.3 %collective-permute-start.18 = (f32[27,16,128]{2,1,0:T(8,128)S(1)}, f32[27,16,128]{2,1,0:T(8,128)S(1)}, u32[]{:S(2)}, u32[]{:S(2)}) collective-permute-start(f32[27,16,128]{2,1,0:T(8,128)S(1)} %collective-permute-done.17.refs_5_), channel_id=1, source_target_pairs={{0,224},{1,225},{2,226},{3,227},{4,228},{5,229},{6,230},{7,231},{8... | collective-permute-start | bytes 663560 | tf_op jit(solution)/shard_map/ppermute | solution.py:297
  37.5 0.1 collective-permute-done.11.refs_6_
  37.7 1.3 collective-permute-done.14.refs_8_
  39.0 3.3 %collective-permute-start.7 = (f32[52,16,128]{2,1,0:T(8,128)S(1)}, f32[52,16,128]{2,1,0:T(8,128)S(1)}, u32[]{:S(2)}, u32[]{:S(2)}) collective-permute-start(f32[52,16,128]{2,1,0:T(8,128)S(1)} %collective-permute-done.6.refs_8_), channel_id=1, source_target_pairs={{0,224},{1,225},{2,226},{3,227},{4,228},{5,229},{6,230},{7,231},{8... | collective-permute-start | bytes 1277960 | tf_op jit(solution)/shard_map/ppermute | solution.py:297
  42.3 1.5 %collective-permute-done.18.refs_9_ = f32[27,16,128]{2,1,0:T(8,128)S(1)} collective-permute-done((f32[27,16,128]{2,1,0:T(8,128)S(1)}, f32[27,16,128]{2,1,0:T(8,128)S(1)}, u32[]{:S(2)}, u32[]{:S(2)}) %collective-permute-start.18) | collective-permute-done | bytes 221216 | tf_op jit(solution)/shard_map/ppermute | solution.py:297
  43.7 3.2 %collective-permute-start.15 = (f32[27,16,128]{2,1,0:T(8,128)S(1)}, f32[27,16,128]{2,1,0:T(8,128)S(1)}, u32[]{:S(2)}, u32[]{:S(2)}) collective-permute-start(f32[27,16,128]{2,1,0:T(8,128)S(1)} %collective-permute-done.14.refs_8_), channel_id=1, source_target_pairs={{0,224},{1,225},{2,226},{3,227},{4,228},{5,229},{6,230},{7,231},{8... | collective-permute-start | bytes 663560 | tf_op jit(solution)/shard_map/ppermute | solution.py:297
  47.0 2.9 %collective-permute-start.26 = (f32[52,16,128]{2,1,0:T(8,128)S(1)}, f32[52,16,128]{2,1,0:T(8,128)S(1)}, u32[]{:S(2)}, u32[]{:S(2)}) collective-permute-start(f32[52,16,128]{2,1,0:T(8,128)S(1)} %collective-permute-done.refs_2_), channel_id=1, source_target_pairs={{0,16},{1,17},{2,18},{3,19},{4,20},{5,21},{6,22},{7,23},{8,24},{9,... | collective-permute-start | bytes 1277960 | tf_op jit(solution)/shard_map/ppermute | solution.py:297
  49.9 0.1 collective-permute-start.27
  50.0 7.6 %collective-permute-done.15.refs_5_ = f32[27,16,128]{2,1,0:T(8,128)S(1)} collective-permute-done((f32[27,16,128]{2,1,0:T(8,128)S(1)}, f32[27,16,128]{2,1,0:T(8,128)S(1)}, u32[]{:S(2)}, u32[]{:S(2)}) %collective-permute-start.15) | collective-permute-done | bytes 221216 | tf_op jit(solution)/shard_map/ppermute | solution.py:297
  57.6 2.6 %collective-permute-start.19 = (f32[27,16,128]{2,1,0:T(8,128)S(1)}, f32[27,16,128]{2,1,0:T(8,128)S(1)}, u32[]{:S(2)}, u32[]{:S(2)}) collective-permute-start(f32[27,16,128]{2,1,0:T(8,128)S(1)} %collective-permute-done.18.refs_9_), channel_id=1, source_target_pairs={{0,224},{1,225},{2,226},{3,227},{4,228},{5,229},{6,230},{7,231},{8... | collective-permute-start | bytes 663560 | tf_op jit(solution)/shard_map/ppermute | solution.py:297
  60.2 2.6 %collective-permute-start.8 = (f32[52,16,128]{2,1,0:T(8,128)S(1)}, f32[52,16,128]{2,1,0:T(8,128)S(1)}, u32[]{:S(2)}, u32[]{:S(2)}) collective-permute-start(f32[52,16,128]{2,1,0:T(8,128)S(1)} %collective-permute-done.7.refs_11_), channel_id=1, source_target_pairs={{0,16},{1,17},{2,18},{3,19},{4,20},{5,21},{6,22},{7,23},{8,24},{9,... | collective-permute-start | bytes 1277960 | tf_op jit(solution)/shard_map/ppermute | solution.py:297
  62.8 0.5 collective-permute-start.28
  63.3 0.5 collective-permute-done.27.refs_5_
  63.8 2.6 %collective-permute-start.29 = (f32[52,16,128]{2,1,0:T(8,128)S(1)}, f32[52,16,128]{2,1,0:T(8,128)S(1)}, u32[]{:S(2)}, u32[]{:S(2)}) collective-permute-start(f32[52,16,128]{2,1,0:T(8,128)S(1)} %collective-permute-done.6.refs_8_), channel_id=1, source_target_pairs={{0,16},{1,17},{2,18},{3,19},{4,20},{5,21},{6,22},{7,23},{8,24},{9,... | collective-permute-start | bytes 1277960 | tf_op jit(solution)/shard_map/ppermute | solution.py:297
  66.4 3.2 %collective-permute-done.2.refs_10_ = f32[52,16,128]{2,1,0:T(8,128)S(1)} collective-permute-done((f32[52,16,128]{2,1,0:T(8,128)S(1)}, f32[52,16,128]{2,1,0:T(8,128)S(1)}, u32[]{:S(2)}, u32[]{:S(2)}) %collective-permute-start.2) | collective-permute-done | bytes 426016 | tf_op jit(solution)/shard_map/ppermute | solution.py:297
  69.5 1.5 %collective-permute-start.3 = (f32[52,16,128]{2,1,0:T(8,128)S(1)}, f32[52,16,128]{2,1,0:T(8,128)S(1)}, u32[]{:S(2)}, u32[]{:S(2)}) collective-permute-start(f32[52,16,128]{2,1,0:T(8,128)S(1)} %collective-permute-done.2.refs_10_), channel_id=1, source_target_pairs={{0,16},{1,17},{2,18},{3,19},{4,20},{5,21},{6,22},{7,23},{8,24},{9,... | collective-permute-start | bytes 1277960 | tf_op jit(solution)/shard_map/ppermute | solution.py:297
  71.0 4.0 %collective-permute-done.22.refs_7_ = f32[27,16,128]{2,1,0:T(8,128)S(1)} collective-permute-done((f32[27,16,128]{2,1,0:T(8,128)S(1)}, f32[27,16,128]{2,1,0:T(8,128)S(1)}, u32[]{:S(2)}, u32[]{:S(2)}) %collective-permute-start.22) | collective-permute-done | bytes 221216 | tf_op jit(solution)/shard_map/ppermute | solution.py:297
  75.0 2.7 %collective-permute-start.9 = (f32[52,16,128]{2,1,0:T(8,128)S(1)}, f32[52,16,128]{2,1,0:T(8,128)S(1)}, u32[]{:S(2)}, u32[]{:S(2)}) collective-permute-start(f32[52,16,128]{2,1,0:T(8,128)S(1)} %collective-permute-done.8.refs_12_), channel_id=1, source_target_pairs={{0,224},{1,225},{2,226},{3,227},{4,228},{5,229},{6,230},{7,231},{8... | collective-permute-start | bytes 1277960 | tf_op jit(solution)/shard_map/ppermute | solution.py:297
  77.7 5.1 %collective-permute-done.28.refs_7_ = f32[52,16,128]{2,1,0:T(8,128)S(1)} collective-permute-done((f32[52,16,128]{2,1,0:T(8,128)S(1)}, f32[52,16,128]{2,1,0:T(8,128)S(1)}, u32[]{:S(2)}, u32[]{:S(2)}) %collective-permute-start.28) | collective-permute-done | bytes 426016 | tf_op jit(solution)/shard_map/ppermute | solution.py:297
  82.8 9.1 %collective-permute-done.29.refs_9_ = f32[52,16,128]{2,1,0:T(8,128)S(1)} collective-permute-done((f32[52,16,128]{2,1,0:T(8,128)S(1)}, f32[52,16,128]{2,1,0:T(8,128)S(1)}, u32[]{:S(2)}, u32[]{:S(2)}) %collective-permute-start.29) | collective-permute-done | bytes 426016 | tf_op jit(solution)/shard_map/ppermute | solution.py:297
  91.9 2.6 %collective-permute-start.24 = (f32[27,16,128]{2,1,0:T(8,128)S(1)}, f32[27,16,128]{2,1,0:T(8,128)S(1)}, u32[]{:S(2)}, u32[]{:S(2)}) collective-permute-start(f32[27,16,128]{2,1,0:T(8,128)S(1)} %collective-permute-done.19.refs_6_), channel_id=1, source_target_pairs={{0,224},{1,225},{2,226},{3,227},{4,228},{5,229},{6,230},{7,231},{8... | collective-permute-start | bytes 663560 | tf_op jit(solution)/shard_map/ppermute | solution.py:297
  94.5 6.2 %pack_va.1 = (bf16[52,256,128]{2,1,0:T(8,128)(2,1)S(1)}, bf16[52,256,128]{2,1,0:T(8,128)(2,1)S(1)}) custom-call(f32[4,25,64,400]{3,2,1,0:T(8,128)} %bitcast.8, f32[4,25,64,400]{3,2,1,0:T(8,128)} %bitcast.9), custom_call_target="tpu_custom_call" | custom-call | tf_op jit(solution)/shard_map/pack_va/pallas_call | solution.py:97
  100.7 3.2 %pack_vb.1 = (bf16[27,256,128]{2,1,0:T(8,128)(2,1)S(1)}, bf16[27,256,128]{2,1,0:T(8,128)(2,1)S(1)}) custom-call(f32[4,25,64,400]{3,2,1,0:T(8,128)} %bitcast.10, f32[4,25,64,400]{3,2,1,0:T(8,128)} %bitcast.11), custom_call_target="tpu_custom_call" | custom-call | tf_op jit(solution)/shard_map/pack_vb/pallas_call | solution.py:113
  103.9 1.3 shard_map.56.refs_15_
  105.2 3.6 %shard_map.55.refs_14_ = f32[208,256]{1,0:T(8,128)S(1)} custom-call(f32[52,16,128]{2,1,0:T(8,128)S(1)} %get-tuple-element.13.refs_0_, f32[52,16,128]{2,1,0:T(8,128)S(1)} %collective-permute-done.25.refs_1_, f32[52,16,128]{2,1,0:T(8,128)S(1)} %collective-permute-done.refs_2_, f32[52,16,128]{2,1,0:T(8,128)S(1)} %collective-permute-done.26.refs_3_, ...), custom_call_target="tpu_custom_call" | custom-call | tf_op jit(solution)/shard_map/pallas_call | solution.py:157
  108.8 0.0 copy-start.1
  108.8 0.0 copy-start
  108.8 0.0 copy-start.2
  108.9 4.5 %last.1 = (f32[8,32,256]{2,1,0:T(8,128)S(1)}, f32[8,32,256]{2,1,0:T(8,128)S(1)}) custom-call(s32[2]{0:T(128)S(1)} %pad_add_fusion.at_ref.refs_0_, f32[52,16,128]{2,1,0:T(8,128)S(1)} %collective-permute-done.3.refs_1_, f32[52,16,128]{2,1,0:T(8,128)S(1)} %collective-permute-done.4.refs_2_, f32[52,16,128]{2,1,0:T(8,128)S(1)} %collective-permute-done.9.refs_3_, ...), custom_call_target="tpu_custom_call" | custom-call | tf_op jit(solution)/shard_map/last/pallas_call | solution.py:200
  113.4 7.4 %collective-permute-start.30 = (f32[8,32,256]{2,1,0:T(8,128)S(1)}, f32[8,32,256]{2,1,0:T(8,128)S(1)}, u32[]{:S(2)}, u32[]{:S(2)}) collective-permute-start(f32[8,32,256]{2,1,0:T(8,128)S(1)} %get-tuple-element.20), channel_id=1, source_target_pairs={{0,1},{1,0},{2,3},{3,2},{4,5},{5,4},{6,7},{7,6},{8,9},{9,8},{10,11... | collective-permute-start | bytes 786440 | tf_op jit(solution)/shard_map/ppermute | solution.py:297
  120.8 0.1 dynamic_slice.6
  120.9 1.1 collective-permute-done.30
  122.0 0.7 add.31
  122.7 7.1 %all-to-all-start = ((f32[8,32,256]{2,1,0:T(8,128)}), f32[8,32,256]{2,1,0:T(8,128)S(1)}, u32[]{:S(2)}, u32[]{:S(2)}) async-start(f32[8,32,256]{2,1,0:T(8,128)} %add.31), calls=%async_computation | async-start | bytes 524288 | tf_op jit(solution)/shard_map/all_to_all | solution.py:341
  129.8 0.1 broadcast_reduce_fusion
  129.9 0.1 add.34
  130.0 0.1 add.36
  130.1 0.1 reshape.40.rest_ref
  130.1 0.6 dynamic_slice.7
  130.7 0.6 add_subtract_fusion
  131.4 2.6 %all-to-all-done.r_ref = f32[8,32,256]{2,1,0:T(8,128)S(1)} async-done(((f32[8,32,256]{2,1,0:T(8,128)}), f32[8,32,256]{2,1,0:T(8,128)S(1)}, u32[]{:S(2)}, u32[]{:S(2)}) %all-to-all-start) | async-done | bytes 262176 | tf_op jit(solution)/shard_map/all_to_all | solution.py:341
  134.0 0.9 shard_map.58
  134.9 9.6 %all-to-all-start.1 = ((f32[16,8,128]{2,1,0:T(8,128)}), f32[16,8,128]{2,1,0:T(8,128)S(1)}, u32[]{:S(2)}, u32[]{:S(2)}) async-start(f32[16,8,128]{2,1,0:T(8,128)} %shard_map.58), calls=%async_computation.1 | async-start | bytes 131072 | tf_op jit(solution)/shard_map/all_to_all | solution.py:346
  144.5 0.1 broadcast_subtract_fusion.den_ref
  144.6 2.3 %all-to-all-done.1.m_ref = f32[16,8,128]{2,1,0:T(8,128)S(1)} async-done(((f32[16,8,128]{2,1,0:T(8,128)}), f32[16,8,128]{2,1,0:T(8,128)S(1)}, u32[]{:S(2)}, u32[]{:S(2)}) %all-to-all-start.1) | async-done | bytes 65568 | tf_op jit(solution)/shard_map/all_to_all | solution.py:346
  147.0 0.9 finish.1
  (28 shorter events, 0.1 us)
Async XLA Ops:
  1.3 15.0 %collective-permute-start.5 = (f32[52,16,128]{2,1,0:T(8,128)S(1)}, f32[52,16,128]{2,1,0:T(8,128)S(1)}, u32[]{:S(2)}, u32[]{:S(2)}) collective-permute-start(f32[52,16,128]{2,1,0:T(8,128)S(1)} %get-tuple-element.13.refs_0_), channel_id=1, source_target_pairs={{0,224},{1,225},{2,226},{3,227},{4,228},{5,229},{6,230},{7,231},{8... | collective-permute-start | bytes 1277960 | tf_op jit(solution)/shard_map/ppermute | solution.py:297
  7.8 7.5 %collective-permute-start.16 = (f32[27,16,128]{2,1,0:T(8,128)S(1)}, f32[27,16,128]{2,1,0:T(8,128)S(1)}, u32[]{:S(2)}, u32[]{:S(2)}) collective-permute-start(f32[27,16,128]{2,1,0:T(8,128)S(1)} %get-tuple-element.14.refs_0_), channel_id=1, source_target_pairs={{0,16},{1,17},{2,18},{3,19},{4,20},{5,21},{6,22},{7,23},{8,24},{9,... | collective-permute-start | bytes 663560 | tf_op jit(solution)/shard_map/ppermute | solution.py:297
  10.7 17.6 %collective-permute-start = (f32[52,16,128]{2,1,0:T(8,128)S(1)}, f32[52,16,128]{2,1,0:T(8,128)S(1)}, u32[]{:S(2)}, u32[]{:S(2)}) collective-permute-start(f32[52,16,128]{2,1,0:T(8,128)S(1)} %get-tuple-element.13.refs_0_), channel_id=1, source_target_pairs={{0,32},{1,33},{2,34},{3,35},{4,36},{5,37},{6,38},{7,39},{8,40},{9,... | collective-permute-start | bytes 1277960 | tf_op jit(solution)/shard_map/ppermute | solution.py:297
  10.7 17.6 %collective-permute-start.25 = (f32[52,16,128]{2,1,0:T(8,128)S(1)}, f32[52,16,128]{2,1,0:T(8,128)S(1)}, u32[]{:S(2)}, u32[]{:S(2)}) collective-permute-start(f32[52,16,128]{2,1,0:T(8,128)S(1)} %get-tuple-element.13.refs_0_), channel_id=1, source_target_pairs={{0,16},{1,17},{2,18},{3,19},{4,20},{5,21},{6,22},{7,23},{8,24},{9,... | collective-permute-start | bytes 1277960 | tf_op jit(solution)/shard_map/ppermute | solution.py:297
  10.8 16.0 %collective-permute-start.10 = (f32[27,16,128]{2,1,0:T(8,128)S(1)}, f32[27,16,128]{2,1,0:T(8,128)S(1)}, u32[]{:S(2)}, u32[]{:S(2)}) collective-permute-start(f32[27,16,128]{2,1,0:T(8,128)S(1)} %get-tuple-element.14.refs_0_), channel_id=1, source_target_pairs={{0,32},{1,33},{2,34},{3,35},{4,36},{5,37},{6,38},{7,39},{8,40},{9,... | collective-permute-start | bytes 663560 | tf_op jit(solution)/shard_map/ppermute | solution.py:297
  15.4 11.5 %collective-permute-start.13 = (f32[27,16,128]{2,1,0:T(8,128)S(1)}, f32[27,16,128]{2,1,0:T(8,128)S(1)}, u32[]{:S(2)}, u32[]{:S(2)}) collective-permute-start(f32[27,16,128]{2,1,0:T(8,128)S(1)} %get-tuple-element.14.refs_0_), channel_id=1, source_target_pairs={{0,224},{1,225},{2,226},{3,227},{4,228},{5,229},{6,230},{7,231},{8... | collective-permute-start | bytes 663560 | tf_op jit(solution)/shard_map/ppermute | solution.py:297
  16.3 22.7 %collective-permute-start.6 = (f32[52,16,128]{2,1,0:T(8,128)S(1)}, f32[52,16,128]{2,1,0:T(8,128)S(1)}, u32[]{:S(2)}, u32[]{:S(2)}) collective-permute-start(f32[52,16,128]{2,1,0:T(8,128)S(1)} %collective-permute-done.5.refs_4_), channel_id=1, source_target_pairs={{0,224},{1,225},{2,226},{3,227},{4,228},{5,229},{6,230},{7,231},{8... | collective-permute-start | bytes 1277960 | tf_op jit(solution)/shard_map/ppermute | solution.py:297
  26.8 7.4 %collective-permute-start.17 = (f32[27,16,128]{2,1,0:T(8,128)S(1)}, f32[27,16,128]{2,1,0:T(8,128)S(1)}, u32[]{:S(2)}, u32[]{:S(2)}) collective-permute-start(f32[27,16,128]{2,1,0:T(8,128)S(1)} %collective-permute-done.16.refs_1_), channel_id=1, source_target_pairs={{0,224},{1,225},{2,226},{3,227},{4,228},{5,229},{6,230},{7,231},{8... | collective-permute-start | bytes 663560 | tf_op jit(solution)/shard_map/ppermute | solution.py:297
  26.8 10.7 %collective-permute-start.20 = (f32[27,16,128]{2,1,0:T(8,128)S(1)}, f32[27,16,128]{2,1,0:T(8,128)S(1)}, u32[]{:S(2)}, u32[]{:S(2)}) collective-permute-start(f32[27,16,128]{2,1,0:T(8,128)S(1)} %collective-permute-done.16.refs_1_), channel_id=1, source_target_pairs={{0,32},{1,33},{2,34},{3,35},{4,36},{5,37},{6,38},{7,39},{8,40},{9,... | collective-permute-start | bytes 663560 | tf_op jit(solution)/shard_map/ppermute | solution.py:297
  28.3 9.4 %collective-permute-start.11 = (f32[27,16,128]{2,1,0:T(8,128)S(1)}, f32[27,16,128]{2,1,0:T(8,128)S(1)}, u32[]{:S(2)}, u32[]{:S(2)}) collective-permute-start(f32[27,16,128]{2,1,0:T(8,128)S(1)} %collective-permute-done.10.refs_2_), channel_id=1, source_target_pairs={{0,32},{1,33},{2,34},{3,35},{4,36},{5,37},{6,38},{7,39},{8,40},{9,... | collective-permute-start | bytes 663560 | tf_op jit(solution)/shard_map/ppermute | solution.py:297
  28.4 10.6 %collective-permute-start.14 = (f32[27,16,128]{2,1,0:T(8,128)S(1)}, f32[27,16,128]{2,1,0:T(8,128)S(1)}, u32[]{:S(2)}, u32[]{:S(2)}) collective-permute-start(f32[27,16,128]{2,1,0:T(8,128)S(1)} %collective-permute-done.13.refs_4_), channel_id=1, source_target_pairs={{0,224},{1,225},{2,226},{3,227},{4,228},{5,229},{6,230},{7,231},{8... | collective-permute-start | bytes 663560 | tf_op jit(solution)/shard_map/ppermute | solution.py:297
  34.3 9.5 %collective-permute-start.18 = (f32[27,16,128]{2,1,0:T(8,128)S(1)}, f32[27,16,128]{2,1,0:T(8,128)S(1)}, u32[]{:S(2)}, u32[]{:S(2)}) collective-permute-start(f32[27,16,128]{2,1,0:T(8,128)S(1)} %collective-permute-done.17.refs_5_), channel_id=1, source_target_pairs={{0,224},{1,225},{2,226},{3,227},{4,228},{5,229},{6,230},{7,231},{8... | collective-permute-start | bytes 663560 | tf_op jit(solution)/shard_map/ppermute | solution.py:297
  37.5 9.4 %collective-permute-start.21 = (f32[27,16,128]{2,1,0:T(8,128)S(1)}, f32[27,16,128]{2,1,0:T(8,128)S(1)}, u32[]{:S(2)}, u32[]{:S(2)}) collective-permute-start(f32[27,16,128]{2,1,0:T(8,128)S(1)} %collective-permute-done.20.refs_3_), channel_id=1, source_target_pairs={{0,32},{1,33},{2,34},{3,35},{4,36},{5,37},{6,38},{7,39},{8,40},{9,... | collective-permute-start | bytes 663560 | tf_op jit(solution)/shard_map/ppermute | solution.py:297
  37.7 12.2 %collective-permute-start.12 = (f32[27,16,128]{2,1,0:T(8,128)S(1)}, f32[27,16,128]{2,1,0:T(8,128)S(1)}, u32[]{:S(2)}, u32[]{:S(2)}) collective-permute-start(f32[27,16,128]{2,1,0:T(8,128)S(1)} %collective-permute-done.11.refs_6_), channel_id=1, source_target_pairs={{0,32},{1,33},{2,34},{3,35},{4,36},{5,37},{6,38},{7,39},{8,40},{9,... | collective-permute-start | bytes 663560 | tf_op jit(solution)/shard_map/ppermute | solution.py:297
  39.0 21.2 %collective-permute-start.1 = (f32[52,16,128]{2,1,0:T(8,128)S(1)}, f32[52,16,128]{2,1,0:T(8,128)S(1)}, u32[]{:S(2)}, u32[]{:S(2)}) collective-permute-start(f32[52,16,128]{2,1,0:T(8,128)S(1)} %collective-permute-done.refs_2_), channel_id=1, source_target_pairs={{0,32},{1,33},{2,34},{3,35},{4,36},{5,37},{6,38},{7,39},{8,40},{9,... | collective-permute-start | bytes 1277960 | tf_op jit(solution)/shard_map/ppermute | solution.py:297
  39.0 21.2 %collective-permute-start.7 = (f32[52,16,128]{2,1,0:T(8,128)S(1)}, f32[52,16,128]{2,1,0:T(8,128)S(1)}, u32[]{:S(2)}, u32[]{:S(2)}) collective-permute-start(f32[52,16,128]{2,1,0:T(8,128)S(1)} %collective-permute-done.6.refs_8_), channel_id=1, source_target_pairs={{0,224},{1,225},{2,226},{3,227},{4,228},{5,229},{6,230},{7,231},{8... | collective-permute-start | bytes 1277960 | tf_op jit(solution)/shard_map/ppermute | solution.py:297
  43.7 13.9 %collective-permute-start.15 = (f32[27,16,128]{2,1,0:T(8,128)S(1)}, f32[27,16,128]{2,1,0:T(8,128)S(1)}, u32[]{:S(2)}, u32[]{:S(2)}) collective-permute-start(f32[27,16,128]{2,1,0:T(8,128)S(1)} %collective-permute-done.14.refs_8_), channel_id=1, source_target_pairs={{0,224},{1,225},{2,226},{3,227},{4,228},{5,229},{6,230},{7,231},{8... | collective-permute-start | bytes 663560 | tf_op jit(solution)/shard_map/ppermute | solution.py:297
  47.0 15.8 %collective-permute-start.26 = (f32[52,16,128]{2,1,0:T(8,128)S(1)}, f32[52,16,128]{2,1,0:T(8,128)S(1)}, u32[]{:S(2)}, u32[]{:S(2)}) collective-permute-start(f32[52,16,128]{2,1,0:T(8,128)S(1)} %collective-permute-done.refs_2_), channel_id=1, source_target_pairs={{0,16},{1,17},{2,18},{3,19},{4,20},{5,21},{6,22},{7,23},{8,24},{9,... | collective-permute-start | bytes 1277960 | tf_op jit(solution)/shard_map/ppermute | solution.py:297
  49.9 13.9 %collective-permute-start.27 = (f32[52,16,128]{2,1,0:T(8,128)S(1)}, f32[52,16,128]{2,1,0:T(8,128)S(1)}, u32[]{:S(2)}, u32[]{:S(2)}) collective-permute-start(f32[52,16,128]{2,1,0:T(8,128)S(1)} %collective-permute-done.5.refs_4_), channel_id=1, source_target_pairs={{0,16},{1,17},{2,18},{3,19},{4,20},{5,21},{6,22},{7,23},{8,24},{9,... | collective-permute-start | bytes 1277960 | tf_op jit(solution)/shard_map/ppermute | solution.py:297
  57.6 8.8 %collective-permute-start.19 = (f32[27,16,128]{2,1,0:T(8,128)S(1)}, f32[27,16,128]{2,1,0:T(8,128)S(1)}, u32[]{:S(2)}, u32[]{:S(2)}) collective-permute-start(f32[27,16,128]{2,1,0:T(8,128)S(1)} %collective-permute-done.18.refs_9_), channel_id=1, source_target_pairs={{0,224},{1,225},{2,226},{3,227},{4,228},{5,229},{6,230},{7,231},{8... | collective-permute-start | bytes 663560 | tf_op jit(solution)/shard_map/ppermute | solution.py:297
  60.2 9.3 %collective-permute-start.2 = (f32[52,16,128]{2,1,0:T(8,128)S(1)}, f32[52,16,128]{2,1,0:T(8,128)S(1)}, u32[]{:S(2)}, u32[]{:S(2)}) collective-permute-start(f32[52,16,128]{2,1,0:T(8,128)S(1)} %collective-permute-done.1.refs_6_), channel_id=1, source_target_pairs={{0,32},{1,33},{2,34},{3,35},{4,36},{5,37},{6,38},{7,39},{8,40},{9,... | collective-permute-start | bytes 1277960 | tf_op jit(solution)/shard_map/ppermute | solution.py:297
  60.2 14.8 %collective-permute-start.8 = (f32[52,16,128]{2,1,0:T(8,128)S(1)}, f32[52,16,128]{2,1,0:T(8,128)S(1)}, u32[]{:S(2)}, u32[]{:S(2)}) collective-permute-start(f32[52,16,128]{2,1,0:T(8,128)S(1)} %collective-permute-done.7.refs_11_), channel_id=1, source_target_pairs={{0,16},{1,17},{2,18},{3,19},{4,20},{5,21},{6,22},{7,23},{8,24},{9,... | collective-permute-start | bytes 1277960 | tf_op jit(solution)/shard_map/ppermute | solution.py:297
  62.8 20.0 %collective-permute-start.28 = (f32[52,16,128]{2,1,0:T(8,128)S(1)}, f32[52,16,128]{2,1,0:T(8,128)S(1)}, u32[]{:S(2)}, u32[]{:S(2)}) collective-permute-start(f32[52,16,128]{2,1,0:T(8,128)S(1)} %collective-permute-done.1.refs_6_), channel_id=1, source_target_pairs={{0,16},{1,17},{2,18},{3,19},{4,20},{5,21},{6,22},{7,23},{8,24},{9,... | collective-permute-start | bytes 1277960 | tf_op jit(solution)/shard_map/ppermute | solution.py:297
  63.8 28.1 %collective-permute-start.29 = (f32[52,16,128]{2,1,0:T(8,128)S(1)}, f32[52,16,128]{2,1,0:T(8,128)S(1)}, u32[]{:S(2)}, u32[]{:S(2)}) collective-permute-start(f32[52,16,128]{2,1,0:T(8,128)S(1)} %collective-permute-done.6.refs_8_), channel_id=1, source_target_pairs={{0,16},{1,17},{2,18},{3,19},{4,20},{5,21},{6,22},{7,23},{8,24},{9,... | collective-permute-start | bytes 1277960 | tf_op jit(solution)/shard_map/ppermute | solution.py:297
  66.4 8.7 %collective-permute-start.22 = (f32[27,16,128]{2,1,0:T(8,128)S(1)}, f32[27,16,128]{2,1,0:T(8,128)S(1)}, u32[]{:S(2)}, u32[]{:S(2)}) collective-permute-start(f32[27,16,128]{2,1,0:T(8,128)S(1)} %collective-permute-done.21.refs_7_), channel_id=1, source_target_pairs={{0,32},{1,33},{2,34},{3,35},{4,36},{5,37},{6,38},{7,39},{8,40},{9,... | collective-permute-start | bytes 663560 | tf_op jit(solution)/shard_map/ppermute | solution.py:297
  69.5 39.3 %collective-permute-start.3 = (f32[52,16,128]{2,1,0:T(8,128)S(1)}, f32[52,16,128]{2,1,0:T(8,128)S(1)}, u32[]{:S(2)}, u32[]{:S(2)}) collective-permute-start(f32[52,16,128]{2,1,0:T(8,128)S(1)} %collective-permute-done.2.refs_10_), channel_id=1, source_target_pairs={{0,16},{1,17},{2,18},{3,19},{4,20},{5,21},{6,22},{7,23},{8,24},{9,... | collective-permute-start | bytes 1277960 | tf_op jit(solution)/shard_map/ppermute | solution.py:297
  75.0 33.9 %collective-permute-start.4 = (f32[52,16,128]{2,1,0:T(8,128)S(1)}, f32[52,16,128]{2,1,0:T(8,128)S(1)}, u32[]{:S(2)}, u32[]{:S(2)}) collective-permute-start(f32[52,16,128]{2,1,0:T(8,128)S(1)} %collective-permute-done.2.refs_10_), channel_id=1, source_target_pairs={{0,32},{1,33},{2,34},{3,35},{4,36},{5,37},{6,38},{7,39},{8,40},{9,... | collective-permute-start | bytes 1277960 | tf_op jit(solution)/shard_map/ppermute | solution.py:297
  75.0 33.9 %collective-permute-start.9 = (f32[52,16,128]{2,1,0:T(8,128)S(1)}, f32[52,16,128]{2,1,0:T(8,128)S(1)}, u32[]{:S(2)}, u32[]{:S(2)}) collective-permute-start(f32[52,16,128]{2,1,0:T(8,128)S(1)} %collective-permute-done.8.refs_12_), channel_id=1, source_target_pairs={{0,224},{1,225},{2,226},{3,227},{4,228},{5,229},{6,230},{7,231},{8... | collective-permute-start | bytes 1277960 | tf_op jit(solution)/shard_map/ppermute | solution.py:297
  82.8 26.1 %collective-permute-start.23 = (f32[27,16,128]{2,1,0:T(8,128)S(1)}, f32[27,16,128]{2,1,0:T(8,128)S(1)}, u32[]{:S(2)}, u32[]{:S(2)}) collective-permute-start(f32[27,16,128]{2,1,0:T(8,128)S(1)} %collective-permute-done.12.refs_4_), channel_id=1, source_target_pairs={{0,32},{1,33},{2,34},{3,35},{4,36},{5,37},{6,38},{7,39},{8,40},{9,... | collective-permute-start | bytes 663560 | tf_op jit(solution)/shard_map/ppermute | solution.py:297
  91.9 16.9 %collective-permute-start.24 = (f32[27,16,128]{2,1,0:T(8,128)S(1)}, f32[27,16,128]{2,1,0:T(8,128)S(1)}, u32[]{:S(2)}, u32[]{:S(2)}) collective-permute-start(f32[27,16,128]{2,1,0:T(8,128)S(1)} %collective-permute-done.19.refs_6_), channel_id=1, source_target_pairs={{0,224},{1,225},{2,226},{3,227},{4,228},{5,229},{6,230},{7,231},{8... | collective-permute-start | bytes 663560 | tf_op jit(solution)/shard_map/ppermute | solution.py:297
  108.8 12.0 %copy-start.1 = (f32[64]{0:T(128)S(1)}, f32[64]{0:T(128)}, u32[]{:S(2)}) copy-start(f32[64]{0:T(128)} %param.9) | copy-start | bytes 772
  108.8 21.2 %copy-start = (f32[1,16,4,64]{3,2,1,0:T(4,128)S(1)}, f32[1,16,4,64]{3,2,1,0:T(4,128)}, u32[]{:S(2)}) copy-start(f32[1,16,4,64]{3,2,1,0:T(4,128)} %param.7) | copy-start | bytes 49156
  108.8 21.3 %copy-start.2 = (f32[16]{0:T(128)S(1)}, f32[16]{0:T(128)}, u32[]{:S(2)}) copy-start(f32[16]{0:T(128)} %param.8) | copy-start | bytes 196
  113.4 8.5 %collective-permute-start.30 = (f32[8,32,256]{2,1,0:T(8,128)S(1)}, f32[8,32,256]{2,1,0:T(8,128)S(1)}, u32[]{:S(2)}, u32[]{:S(2)}) collective-permute-start(f32[8,32,256]{2,1,0:T(8,128)S(1)} %get-tuple-element.20), channel_id=1, source_target_pairs={{0,1},{1,0},{2,3},{3,2},{4,5},{5,4},{6,7},{7,6},{8,9},{9,8},{10,11... | collective-permute-start | bytes 786440 | tf_op jit(solution)/shard_map/ppermute | solution.py:297
  122.7 11.3 %all-to-all-start = ((f32[8,32,256]{2,1,0:T(8,128)}), f32[8,32,256]{2,1,0:T(8,128)S(1)}, u32[]{:S(2)}, u32[]{:S(2)}) async-start(f32[8,32,256]{2,1,0:T(8,128)} %add.31), calls=%async_computation | async-start | bytes 524288 | tf_op jit(solution)/shard_map/all_to_all | solution.py:341
  134.9 12.1 %all-to-all-start.1 = ((f32[16,8,128]{2,1,0:T(8,128)}), f32[16,8,128]{2,1,0:T(8,128)S(1)}, u32[]{:S(2)}, u32[]{:S(2)}) async-start(f32[16,8,128]{2,1,0:T(8,128)} %shard_map.58), calls=%async_computation.1 | async-start | bytes 131072 | tf_op jit(solution)/shard_map/all_to_all | solution.py:346
